TPU v7x, 32 devices: a whole 2x2x4 slice. The times are simulated.
32 devices in a mesh: dp: 8 (over z, x), expert: 4 (over y, core).
Axes of the slice: x: 2, y: 2, z: 4, core: 2. Of those that a mesh axis runs over, the one named last changes fastest.
Arguments:
- tokens: bfloat16 [4096, 1024], P(('dp', 'expert')), may hold values from -6 to 6
- prefix_len: int32 [8], P('dp'), may hold values from 0 to 512
- routes: int32 [4096, 8], P(('dp', 'expert')), may hold values from 0 to 15, all different within a row; in each aligned block of 128 rows (0 to 127, 128 to 255, ...) at most 128 rows name the same one
- norm1_gain: float32 [1024], replicated, may hold values from 0.5 to 1.5
- w_query: bfloat16 [1024, 1024], replicated, may hold values from -0.1875 to 0.1875
- w_key: bfloat16 [1024, 512], replicated, may hold values from -0.1875 to 0.1875
- w_value: bfloat16 [1024, 512], replicated, may hold values from -0.1875 to 0.1875
- w_output: bfloat16 [1024, 1024], replicated, may hold values from -4 to 4
- norm2_gain: float32 [1024], replicated, may hold values from 0.5 to 1.5
- w_router: bfloat16 [1024, 16], replicated, may hold values from -0.09375 to 0.09375
- w_gate: bfloat16 [16, 1024, 512], P('expert'), may hold values from -0.1875 to 0.1875
- w_up: bfloat16 [16, 1024, 512], P('expert'), may hold values from -0.1875 to 0.1875
- w_down: bfloat16 [16, 512, 1024], P('expert'), may hold values from -1 to 1
- cotangent: bfloat16 [4096, 1024], P(('dp', 'expert')), may hold values from -6 to 6
Outputs:
- block_out: bfloat16 [4096, 1024], P(('dp', 'expert'))
- grad_tokens: bfloat16 [4096, 1024], P(('dp', 'expert'))
- grad_norm1: float32 [1024], P(('dp', 'expert'))
- grad_query_w: float32 [1024, 1024], P(('dp', 'expert'))
- grad_key_w: float32 [1024, 512], P(('dp', 'expert'))
- grad_value_w: float32 [1024, 512], P(('dp', 'expert'))
- grad_output_w: float32 [1024, 1024], P(('dp', 'expert'))
- grad_norm2: float32 [1024], P(('dp', 'expert'))
- grad_router: float32 [1024, 16], P(('dp', 'expert'))
- grad_gate_w: float32 [16, 1024, 512], P('expert', 'dp')
- grad_up_w: float32 [16, 1024, 512], P('expert', 'dp')
- grad_down_w: float32 [16, 512, 1024], P('expert', None, 'dp')
Inputs may be any that keep to these rules, and one draw needn't show every extreme that they name: `routes`: among the 128 rows of one device no expert is named more than 128 times, and in every draw some device names some expert exactly 128 times.
All inputs are finite; a program needn't handle non-finite values.
Results may differ from a plain program's by a relative error of at most 0.018.
Values may be sent and summed in bfloat16 or wider, within the bound.
No kernel may reach another device: no remote copies, remote signals or barrier semaphores. Data moves between devices by JAX's collectives and lax.ppermute only.
A program may use at most 192 MiB of HBM per device.

v0:
```python
import math

import jax
import jax.numpy as jnp
from jax import lax
from jax.experimental import pallas as pl
from jax.experimental.pallas import tpu as pltpu
from jax.sharding import PartitionSpec as P

H = 16
KV = 8
HD = 64


norm_eps = 1e-05
masked_score = -1e30


def rope_tables(me, tok_rows, groups):
    row = lax.broadcasted_iota(jnp.int32, (groups * tok_rows, LANES), 0)
    lane = lax.broadcasted_iota(jnp.int32, (groups * tok_rows, LANES), 1)
    position = ((row // tok_rows) ^ me) * tok_rows + row % tok_rows
    frequency = jnp.exp((lane % (HD // 2)).astype(jnp.float32) * (-2.0 * math.log(10000.0) / HD))
    angles = position.astype(jnp.float32) * frequency
    sine = jnp.sin(angles)
    return jnp.cos(angles), jnp.where(lane % HD < HD // 2, -sine, sine)


LANES = 128
LIMIT_MIB = 63


def norm_forward(source, gain_vec):
    inverse = lax.rsqrt(jnp.mean(source * source, axis=-1, keepdims=True) + norm_eps)
    return (source * inverse * gain_vec, inverse)


def norm_backward(source, inverse, gain_vec, upstream):
    weighted = upstream * gain_vec
    cubed = inverse * inverse * inverse
    back = inverse * weighted - source * cubed * jnp.mean(weighted * source, axis=-1, keepdims=True)
    return (back, jnp.sum(upstream * source * inverse, axis=0, keepdims=True))


def dot(left, right, left_dim=1, right_dim=0):
    return lax.dot_general(
        left, right, (((left_dim,), (right_dim,)), ((), ())), preferred_element_type=jnp.float32
    )


def lane_of(shape):
    return lax.broadcasted_iota(jnp.int32, shape, 1)


def swap_halves(source):
    lane = lane_of(source.shape)
    return jnp.where(
        lane % HD < HD // 2,
        pltpu.roll(source, LANES - HD // 2, 1),
        pltpu.roll(source, HD // 2, 1),
    )


def rope(source, cosine_table, sine_table):
    return source * cosine_table + swap_halves(source) * sine_table


def unrope(upstream, cosine_table, sine_table):
    return upstream * cosine_table - swap_halves(upstream) * sine_table


def twice(pair):
    lane = lane_of(pair.shape)
    other = pltpu.roll(pair, HD, 1)
    return (jnp.where(lane < HD, pair, other), jnp.where(lane < HD, other, pair))


def stack_heads(pair):
    lane = lane_of(pair.shape)
    zero = jnp.zeros_like(pair)
    return jnp.concatenate(
        [jnp.where(lane < HD, pair, zero), jnp.where(lane < HD, zero, pair)], axis=0
    )


def join_heads(stacked):
    rows = stacked.shape[0] // 2
    lane = lane_of((rows, LANES))
    return jnp.where(lane < HD, stacked[:rows], stacked[rows:])


def allowed_mask(info_ref, seq_len, rows):
    me, prefix = info_ref[0], info_ref[1]
    key = lax.broadcasted_iota(jnp.int32, (seq_len, 2 * rows), 0)
    query = lax.broadcasted_iota(jnp.int32, (seq_len, 2 * rows), 1) % rows + me * rows
    key_pos = ((key // rows) ^ me) * rows + key % rows
    return (key_pos <= query) | (key_pos < prefix)


def forward_kernel(
    info_ref, tokens_ref, query_ref, wk_ref, wv_ref, wo_ref, gain_ref, cos_ref, sin_ref, *rest
):
    blocks, outs = rest[:-9], rest[-9:]
    q_ref, k_ref, v_ref, lse_ref, att_ref, hid_ref, n2_ref, wo_held, sems = outs
    wo_copy = start_copies([(wo_ref, wo_held)], sems)
    rows = tokens_ref.shape[0]
    seq_len = rows * len(blocks)
    normed = jnp.concatenate([b[...] for b in blocks], axis=0)
    cosine, sine = cos_ref[...], sin_ref[...]
    keys = dot(normed, wk_ref[...])
    values = dot(normed, wv_ref[...])
    for c in range(KV // 2):
        cols = slice(c * LANES, (c + 1) * LANES)
        first, second = twice(rope(keys[:, cols], cosine, sine))
        k_ref[2 * c] = first.astype(jnp.bfloat16)
        k_ref[2 * c + 1] = second.astype(jnp.bfloat16)
        first, second = twice(values[:, cols])
        v_ref[2 * c] = first.astype(jnp.bfloat16)
        v_ref[2 * c + 1] = second.astype(jnp.bfloat16)
    allowed = allowed_mask(info_ref, seq_len, rows)
    for h in range(KV):
        cols = slice(h * LANES, (h + 1) * LANES)
        query = rope(query_ref[:, cols], cosine[:rows], sine[:rows]) * (1.0 / math.sqrt(HD))
        q_ref[:, cols] = query.astype(jnp.bfloat16)
        stacked = stack_heads(query).astype(jnp.bfloat16)
        scores = jnp.where(allowed, dot(k_ref[h], stacked, 1, 1), masked_score)
        row_max = jnp.max(scores, axis=0, keepdims=True)
        exps = jnp.exp(scores - row_max)
        total = jnp.sum(exps, axis=0, keepdims=True)
        lse_ref[h : h + 1, :] = row_max + jnp.log(total)
        prob = (exps * (1.0 / total)).astype(jnp.bfloat16)
        att_ref[:, cols] = join_heads(dot(prob, v_ref[h], 0, 0)).astype(jnp.bfloat16)
    wait_all(wo_copy)
    hidden = tokens_ref[...].astype(jnp.float32) + dot(att_ref[...], wo_held[...])
    hid_ref[...] = hidden
    n2_ref[...] = norm_forward(hidden, gain_ref[...])[0].astype(jnp.bfloat16)


def start_copies(pairs, sems):
    copies = describe(pairs, sems)
    for c in copies:
        c.start()
    return copies


def wait_all(copies):
    for c in copies:
        c.wait()


def own_half(info_ref, fh):
    return pl.ds(pl.multiple_of(info_ref[2] * fh, fh), fh)


def expert_parts(info_ref, wg_ref, wu_ref, w_ref, e):
    fh = wg_ref.shape[2] // 2
    mine = own_half(info_ref, fh)
    return [
        (wg_ref.at[e, :, mine], w_ref.at[e, :, pl.ds(0, fh)]),
        (wu_ref.at[e, :, mine], w_ref.at[e, :, pl.ds(fh, fh)]),
    ]


def down_part(info_ref, wd_ref, down_ref, e):
    mine = own_half(info_ref, wd_ref.shape[1] // 2)
    return [(wd_ref.at[e, mine, :], down_ref.at[e])]


def describe(pairs, sems):
    return [pltpu.make_async_copy(src, dst, sems.at[n]) for n, (src, dst) in enumerate(pairs)]


def row_parts(blocks, into, cols):
    rows = blocks[0].shape[0]
    return [(b.at[:, cols], into.at[pl.ds(n * rows, rows), :]) for n, b in enumerate(blocks)]


def widen(router_ref, wide_ref):
    wide_ref[...] = jnp.zeros_like(wide_ref)
    wide_ref[:, : router_ref.shape[1]] = router_ref[...]


def routing(routed_ref, n2_ref, router_wide, probs_ref):
    routed = routed_ref[...].astype(jnp.float32) > 0.5
    logits = jnp.where(routed, dot(n2_ref[...], router_wide[...]), masked_score)
    exps = jnp.where(routed, jnp.exp(logits - jnp.max(logits, axis=-1, keepdims=True)), 0.0)
    probs_ref[...] = exps / jnp.sum(exps, axis=-1, keepdims=True)


def experts_kernel(info_ref, router_ref, wg_ref, wu_ref, wd_ref, *rest, n_blocks, tiles):
    n2_blocks, cot_blocks = rest[:n_blocks], rest[n_blocks : 2 * n_blocks]
    sums_out, gu_out, scaled_out, extra_ref, gate_ref = rest[2 * n_blocks : 2 * n_blocks + 5]
    (
        n2_ref, g_ref, routed_ref, w_ref, down_ref, gu_ref, scaled_ref, sums_ref, probs_ref,
        router_wide,
    ) = rest[2 * n_blocks + 5 : 2 * n_blocks + 15]
    n2_sems, routed_sems, g_sems, w_sems, out_sems = rest[2 * n_blocks + 15 :]
    exp_dev, width, units = wg_ref.shape
    fh = units // 2
    n2_copies = start_copies(row_parts(n2_blocks, n2_ref, pl.ds(0, width)), n2_sems)
    routed_copies = start_copies(row_parts(cot_blocks, routed_ref, pl.ds(width, LANES)), routed_sems)

    def weights(e):
        pairs = expert_parts(info_ref, wg_ref, wu_ref, w_ref, e)
        return describe(pairs + down_part(info_ref, wd_ref, down_ref, e), w_sems.at[e])

    def results(e):
        cols = pl.ds(pl.multiple_of(e * 3 * fh, 3 * fh), 3 * fh)
        return describe(
            [
                (gu_ref.at[e], gu_out.at[e]),
                (scaled_ref.at[e], scaled_out.at[e]),
                (sums_ref.at[e], sums_out.at[:, cols]),
            ],
            out_sems.at[e],
        )

    for c in weights(0):
        c.start()
    widen(router_ref, router_wide)
    extra_ref[...] = jnp.zeros_like(extra_ref)
    wait_all(n2_copies)
    wait_all(routed_copies)
    g_copies = start_copies(row_parts(cot_blocks, g_ref, pl.ds(0, width)), g_sems)
    routing(routed_ref, n2_ref, router_wide, probs_ref)
    gate_ref[...] = probs_ref[: gate_ref.shape[0], :]
    wait_all(g_copies)
    step = n2_ref.shape[0] // tiles

    def one_expert(e, carry):
        wait_all(weights(e))

        @pl.when(e + 1 < exp_dev)
        def _():
            for c in weights(e + 1):
                c.start()

        spot = info_ref[0] * exp_dev + e
        for t in range(tiles):
            part = slice(t * step, (t + 1) * step)
            pre = dot(n2_ref[part, :], w_ref[e])
            gate_pre, up_pre = pre[:, :fh], pre[:, fh:]
            back = dot(g_ref[part, :], down_ref[e], 1, 1)
            sig = 0.5 * jnp.tanh(0.5 * gate_pre) + 0.5
            silu = gate_pre * sig
            act = silu * up_pre
            here = lane_of((step, LANES)) == spot
            weight = jnp.sum(jnp.where(here, probs_ref[part, :], 0.0), axis=1, keepdims=True)
            extra_ref[part, :] += jnp.where(here, jnp.sum(act * back, axis=1, keepdims=True), 0.0)
            grad_active = weight * back
            scaled_ref[e, part, :] = (weight * act).astype(jnp.bfloat16)
            gu_ref[e, part, :fh] = (
                grad_active * up_pre * (sig + silu * (1.0 - sig))
            ).astype(jnp.bfloat16)
            gu_ref[e, part, fh:] = (grad_active * silu).astype(jnp.bfloat16)
        sums_ref[e, :, : 2 * fh] = dot(n2_ref[...], gu_ref[e], 0, 0).astype(jnp.bfloat16)
        sums_ref[e, :, 2 * fh :] = dot(g_ref[...], scaled_ref[e], 0, 0).astype(jnp.bfloat16)
        for c in results(e):
            c.start()
        return carry

    lax.fori_loop(0, exp_dev, one_expert, 0)
    for e in range(exp_dev):
        wait_all(results(e))


def put_rows(values, t, odd_ref, even_ref, cols):
    rows = odd_ref.shape[1]
    count = values.shape[0] // rows
    for i in range(count):
        n = t * count + i
        out = odd_ref if n % 2 else even_ref
        out[n // 2, :, cols] = values[i * rows : (i + 1) * rows].astype(out.dtype)


def rows_kernel(
    info_ref, extra_ref, wg_ref, wu_ref, gu_in, odd_out, even_out, w_ref, gu_ref, total_ref,
    odd_ref, even_ref, w_sems, out_sems, *, experts
):
    exp_dev, width, _ = wg_ref.shape
    all_rows = gu_ref.shape[1]

    def operands(e):
        pairs = expert_parts(info_ref, wg_ref, wu_ref, w_ref, e)
        return describe(pairs + [(gu_in.at[e], gu_ref.at[e])], w_sems.at[e])

    for c in operands(0):
        c.start()
    found = extra_ref[...]
    high = found.astype(jnp.bfloat16).astype(jnp.float32)
    lower = (found - high).astype(jnp.bfloat16).astype(jnp.float32)
    put_rows(
        high + pltpu.roll(lower, experts, 1), 0, odd_ref, even_ref, slice(width, width + LANES)
    )
    total_ref[...] = jnp.zeros_like(total_ref)

    def one_expert(e, carry):
        wait_all(operands(e))
        for c in operands(e + 1):
            c.start()
        total_ref[...] += dot(gu_ref[e], w_ref[e], 1, 1)
        return carry

    lax.fori_loop(0, exp_dev - 1, one_expert, 0)
    wait_all(operands(exp_dev - 1))
    out_copies = []
    for t in range(2):
        part = slice(t * all_rows // 2, (t + 1) * all_rows // 2)
        new = total_ref[part, :] + dot(gu_ref[exp_dev - 1, part, :], w_ref[exp_dev - 1], 1, 1)
        put_rows(new, t, odd_ref, even_ref, slice(0, width))
        share = pl.ds(t * odd_ref.shape[0] // 2, odd_ref.shape[0] // 2)
        out_copies += start_copies(
            [(odd_ref.at[share], odd_out.at[share]), (even_ref.at[share], even_out.at[share])],
            out_sems.at[pl.ds(2 * t, 2)],
        )
    wait_all(out_copies)


def final_kernel(
    info_ref, sums_ref, arrived_ref, early_ref, late_ref, *rest, n_early, n_late
):
    dense = rest[:-10]
    gate_ref, up_ref, down_ref, wq_ref, wk_ref, wv_ref, wo_ref, router_ref, one_ref, two_ref = rest[-10:]
    exp_dev, rows, units = gate_ref.shape
    fh = units // 2
    half = info_ref[2]
    kept = sums_ref[pl.ds(pl.multiple_of(half * rows, rows), rows), :]
    got = arrived_ref[...]
    first = jnp.where(half == 0, kept, got).astype(jnp.float32)
    second = jnp.where(half == 0, got, kept).astype(jnp.float32)
    for e in range(exp_dev):
        at = 3 * e * fh
        gate_ref[e, :, :fh] = first[:, at : at + fh]
        gate_ref[e, :, fh:] = second[:, at : at + fh]
        up_ref[e, :, :fh] = first[:, at + fh : at + 2 * fh]
        up_ref[e, :, fh:] = second[:, at + fh : at + 2 * fh]
        at = (3 * e + 2) * fh
        down_ref[e, :fh, :] = first[:, at : at + fh].T
        down_ref[e, fh:, :] = second[:, at : at + fh].T
    early, late = early_ref[0], late_ref[0]
    for d in dense:
        early = early + d[:, :n_early].astype(jnp.float32)
        late = late + d[:, n_early:].astype(jnp.float32)
    width, k_cols = wo_ref.shape[1], wk_ref.shape[1]
    wo_ref[...] = early[:, :width]
    wq_ref[...] = early[:, width + LANES :]
    wk_ref[...] = late[:, :k_cols]
    wv_ref[...] = late[:, k_cols : 2 * k_cols]
    small = early[:, width : width + LANES]
    small = small.T
    router_ref[...] = small[1 : 1 + router_ref.shape[0], :]
    two_ref[...] = small[:1, :]
    one_ref[...] = late[:, 2 * k_cols :].T[:1, :]


def selection(info_ref, select_ref, own_rows):
    count, width = select_ref.shape
    groups = width // count
    row = lax.broadcasted_iota(jnp.int32, (count, width), 0)
    col = lax.broadcasted_iota(jnp.int32, (count, width), 1)
    want = ((row // own_rows) ^ info_ref[3]) * (own_rows * groups) + (
        info_ref[0] * own_rows + row % own_rows
    )
    select_ref[...] = jnp.where(col == want, 1.0, 0.0).astype(jnp.bfloat16)


def pick_small(blocks, rows, count, select):
    total = blocks[0][rows : rows + 2 * count].astype(jnp.float32)
    for b in blocks[1:]:
        total = total + b[rows : rows + 2 * count].astype(jnp.float32)
    total = jnp.concatenate(
        [total[:count] + total[count:], jnp.zeros((LANES - count, total.shape[1]), jnp.float32)],
        axis=0,
    )
    high = total.astype(jnp.bfloat16)
    lower = (total - high.astype(jnp.float32)).astype(jnp.bfloat16)
    return dot(select, high, 1, 1) + dot(select, lower, 1, 1)


def put_shares(values, odd_ref, even_ref, at):
    rows = odd_ref.shape[1]
    for n in range(2 * odd_ref.shape[0]):
        out = odd_ref if n % 2 else even_ref
        out[n // 2, :, at : at + values.shape[1]] = values[n * rows : (n + 1) * rows].astype(
            out.dtype
        )


def early_dense_kernel(info_ref, *rest, groups, count):
    normed, attended, branch, query = (rest[n * groups : (n + 1) * groups] for n in range(4))
    odd_ref, even_ref, normed_t_ref, select_ref = rest[4 * groups :]
    rows, width = normed[0].shape
    selection(info_ref, select_ref, odd_ref.shape[1])
    select = select_ref[...]

    def seq(blocks):
        return jnp.concatenate([b[:rows] for b in blocks], axis=0)

    normed_t = dot(select, seq(normed), 1, 1).astype(jnp.bfloat16)
    normed_t_ref[...] = normed_t
    attended_t = dot(select, seq(attended), 1, 1).astype(jnp.bfloat16)
    put_shares(dot(attended_t, seq(branch)), odd_ref, even_ref, 0)
    put_shares(pick_small(branch, rows, count, select), odd_ref, even_ref, width)
    put_shares(dot(normed_t, seq(query)), odd_ref, even_ref, width + LANES)


def late_dense_kernel(info_ref, normed_t_ref, *rest):
    blocks = rest[:-3]
    odd_ref, even_ref, select_ref = rest[-3:]
    rows = normed_t_ref.shape[1] // len(blocks)
    selection(info_ref, select_ref, odd_ref.shape[1])
    kv = jnp.concatenate([b[:rows] for b in blocks], axis=0)
    put_shares(dot(normed_t_ref[...], kv), odd_ref, even_ref, 0)
    put_shares(pick_small(blocks, rows, 1, select_ref[...]), odd_ref, even_ref, kv.shape[1])


def small_rows(count):
    return -(-2 * count // 16) * 16


def put_small(ref, start, values):
    count = values.shape[0]
    high = values.astype(jnp.bfloat16).astype(jnp.float32)
    fill = jnp.zeros((small_rows(count) - 2 * count, values.shape[1]), jnp.float32)
    ref[start:] = jnp.concatenate([high, values - high, fill], axis=0).astype(jnp.bfloat16)


def backward_kernel(
    info_ref, own_ref, gate_ref, cot_ref, n2_ref, hid_ref, router_ref, gain_ref, wo_ref, q_ref,
    lse_ref, cos_ref, sin_ref, k_hbm, v_hbm, wq_hbm, scaled_hbm, wd_hbm, *rest, experts
):
    arrived, outs = rest[:-18], rest[-18:]
    ghid_ref, branch_ref, dq_ref, odd_ref, even_ref, gn_ref, mix_odd_out, mix_even_out = outs[:8]
    (
        router_wide, k_ref, v_ref, wq_ref, scaled_ref, down_ref, mix_odd_ref, mix_even_ref, sems,
        mix_sems,
    ) = outs[8:]
    late = start_copies([(k_hbm, k_ref), (v_hbm, v_ref), (wq_hbm, wq_ref)], sems)
    exp_dev, units, _ = wd_hbm.shape
    fh = units // 2
    pairs = []
    for e in range(exp_dev):
        part = pl.ds(e * fh, fh)
        pairs += [(wd_hbm.at[e, own_half(info_ref, fh), :], down_ref.at[part, :])]
        pairs += [(scaled_hbm.at[e], scaled_ref.at[:, part])]
    mix_copies = start_copies(pairs, mix_sems)
    widen(router_ref, router_wide)
    rows, width = hid_ref.shape
    summed = own_ref[...]
    for a in arrived:
        summed = summed + a[...].astype(jnp.float32)
    extra = summed[:, width:]
    gate_grads = extra + pltpu.roll(extra, LANES - experts, 1)
    gate = gate_ref[...]
    grad_logits = (
        gate * (gate_grads - jnp.sum(gate * gate_grads, axis=-1, keepdims=True))
    ).astype(jnp.bfloat16)
    router_grad = dot(grad_logits, n2_ref[...], 0, 0)
    grad_normed = summed[:, :width] + dot(grad_logits, router_wide[...], 1, 1)
    hidden = hid_ref[...]
    inverse = lax.rsqrt(jnp.mean(hidden * hidden, axis=-1, keepdims=True) + norm_eps)
    back, norm_grad = norm_backward(hidden, inverse, gain_ref[...], grad_normed)
    grad_hidden = cot_ref[...].astype(jnp.float32) + back
    ghid_ref[...] = grad_hidden
    branch = grad_hidden.astype(jnp.bfloat16)
    branch_ref[:rows] = branch
    put_small(branch_ref, rows, jnp.concatenate([norm_grad, router_grad[:experts]], axis=0))
    grad_attended = dot(branch, wo_ref[...], 1, 1).astype(jnp.bfloat16)
    wait_all(late[:2])
    seq_len = k_ref.shape[1]
    allowed = allowed_mask(info_ref, seq_len, rows)
    cosine, sine = cos_ref[:rows, :], sin_ref[:rows, :]
    lane = lane_of((seq_len, LANES))
    kept = [None, None]
    for h in range(KV):
        cols = slice(h * LANES, (h + 1) * LANES)
        stacked = stack_heads(q_ref[:, cols])
        grad_stacked = stack_heads(grad_attended[:, cols])
        keys = k_ref[h]
        scores = jnp.where(allowed, dot(keys, stacked, 1, 1), masked_score)
        prob = jnp.exp(scores - lse_ref[h : h + 1, :])
        grad_prob = dot(v_ref[h], grad_stacked, 1, 1)
        delta = jnp.sum(prob * grad_prob, axis=0, keepdims=True)
        grad_scores = (prob * (grad_prob - delta)).astype(jnp.bfloat16)
        dq = join_heads(dot(grad_scores, keys, 0, 0)) * (1.0 / math.sqrt(HD))
        dq_ref[:, cols] = unrope(dq, cosine, sine).astype(jnp.bfloat16)
        parts = (dot(grad_scores, stacked), dot(prob.astype(jnp.bfloat16), grad_stacked))
        for n in range(2):
            both = parts[n] + pltpu.roll(parts[n], HD, 1)
            if h % 2 == 0:
                kept[n] = both
                continue
            pair = jnp.where(lane < HD, kept[n], both)
            start = (n * KV // 2 + h // 2) * LANES
            put_rows(pair, 0, odd_ref, even_ref, slice(start, start + LANES))
    wait_all(mix_copies)
    tokens = scaled_ref.shape[0] // 2
    out_copies = []
    for t in range(2):
        mix = dot(scaled_ref[t * tokens : (t + 1) * tokens, :], down_ref[...])
        put_rows(mix, t, mix_odd_ref, mix_even_ref, slice(0, width))
        share = pl.ds(t * mix_odd_ref.shape[0] // 2, mix_odd_ref.shape[0] // 2)
        out_copies += start_copies(
            [
                (mix_odd_ref.at[share], mix_odd_out.at[share]),
                (mix_even_ref.at[share], mix_even_out.at[share]),
            ],
            mix_sems.at[pl.ds(2 * t, 2)],
        )
    wait_all(late[2:])
    gn_ref[...] = dot(dq_ref[...], wq_ref[...], 1, 1)
    wait_all(out_copies)


def tokens_kernel(
    own_ref, gn_ref, wk_ref, wv_ref, tokens_ref, gain_ref, ghid_ref, cos_ref, sin_ref, *rest
):
    arrived, (kv_ref, out_ref) = rest[:-2], rest[-2:]
    rows = tokens_ref.shape[0]
    summed = own_ref[...]
    for a in arrived:
        summed = summed + a[...].astype(jnp.float32)
    k_cols = KV * HD
    for c in range(k_cols // LANES):
        cols = slice(c * LANES, (c + 1) * LANES)
        kv_ref[:rows, cols] = unrope(summed[:, cols], cos_ref[:rows, :], sin_ref[:rows, :]).astype(
            jnp.bfloat16
        )
    kv_ref[:rows, k_cols:] = summed[:, k_cols:].astype(jnp.bfloat16)
    grad_normed = (
        gn_ref[...]
        + dot(kv_ref[:rows, :k_cols], wk_ref[...], 1, 1)
        + dot(kv_ref[:rows, k_cols:], wv_ref[...], 1, 1)
    )
    source = tokens_ref[...].astype(jnp.float32)
    inverse = lax.rsqrt(jnp.mean(source * source, axis=-1, keepdims=True) + norm_eps)
    back, norm_grad = norm_backward(source, inverse, gain_ref[...], grad_normed)
    put_small(kv_ref, rows, norm_grad)
    out_ref[...] = (ghid_ref[...] + back).astype(jnp.bfloat16)


def call(kernel, out_shape, name, hbm=(), hbm_out=(), scratch=(), smem=True):
    def run(*args):
        specs = [
            pl.BlockSpec(memory_space=pl.ANY if n in hbm else pltpu.VMEM)
            for n in range(len(args))
        ]
        if smem:
            specs[0] = pl.BlockSpec(memory_space=pltpu.SMEM)
        return pl.pallas_call(
            kernel,
            out_shape=out_shape,
            in_specs=specs,
            out_specs=[
                pl.BlockSpec(memory_space=pl.ANY if n in hbm_out else pltpu.VMEM)
                for n in range(len(out_shape))
            ],
            scratch_shapes=list(scratch),
            compiler_params=pltpu.CompilerParams(vmem_limit_bytes=LIMIT_MIB * 1024 * 1024),
            name=name,
        )(*args)

    return run


def shape(*dims, dtype=jnp.bfloat16):
    return jax.ShapeDtypeStruct(dims, dtype)


def shards(
    tokens,
    prefix_len,
    routes,
    norm1_gain,
    w_query,
    w_key,
    w_value,
    w_output,
    norm2_gain,
    w_router,
    w_gate,
    w_up,
    w_down,
    cotangent,
):
    tok_rows, model_width = tokens.shape
    groups = lax.axis_size("expert")
    copies = lax.axis_size("dp")
    me = lax.axis_index("expert")
    half = lax.axis_index("dp") % 2
    exp_dev, _, hidden_units = w_gate.shape
    half_units = hidden_units // 2
    experts = exp_dev * groups
    f32 = jnp.float32
    seq_len = tok_rows * groups
    low = jnp.bfloat16

    def send(block, pair_flip, flip):
        return lax.ppermute(
            block,
            ("dp", "expert"),
            [
                (i * groups + j, (i ^ pair_flip) * groups + (j ^ flip))
                for i in range(copies)
                for j in range(groups)
            ],
        )

    def gather_even(block, pairs):
        return [
            block if (s, r) == (0, 0) else send(block, s, r)
            for s in range(pairs)
            for r in range(0, groups, 2)
        ]

    def gather_odd(even):
        out = []
        for b in even:
            out += [b, send(b, 0, 1)]
        return out

    def gather(block, pairs):
        return gather_odd(gather_even(block, pairs))

    def core_sum(odd, even):
        return even + send(odd, 0, 1).astype(jnp.float32)

    def swap(mine, pairs):
        mine = mine.astype(low)
        spots = [(s, r) for s in range(pairs) for r in range(0, groups, 2)]
        return [send(mine[n], *spots[n]) for n in range(1, len(spots))]

    tokens_f = tokens.astype(f32)
    normed1 = norm_forward(tokens_f, norm1_gain)[0].astype(low)
    normed1_even = gather_even(normed1, 1)
    cosine, sine = rope_tables(me, tok_rows, groups)
    cosine, sine, *normed1_even = lax.optimization_barrier((cosine, sine, *normed1_even))
    normed1_blocks = gather_odd(normed1_even)
    routed = jnp.any(
        routes[:, :, None] == jnp.arange(experts, dtype=jnp.int32)[None, None, :], axis=1
    )
    cot_mask = jnp.concatenate(
        [cotangent, jnp.pad(routed.astype(low), ((0, 0), (0, LANES - experts)))], axis=1
    )
    cot_mask, *normed1_even = lax.optimization_barrier((cot_mask, *normed1_even))
    cot_even = gather_even(cot_mask, 2)
    my_dp = lax.axis_index("dp")
    info = jnp.stack([me, prefix_len[0], half, my_dp]).astype(jnp.int32)
    gain_one, gain_two = norm1_gain[None], norm2_gain[None]

    query_pre = dot(normed1, w_query)
    q_low, k_two, v_two, lse, attended, hidden_state, normed2 = call(
        forward_kernel,
        (
            shape(tok_rows, H * HD),
            shape(KV, seq_len, LANES),
            shape(KV, seq_len, LANES),
            shape(KV, 2 * tok_rows, dtype=f32),
            shape(tok_rows, H * HD),
            shape(tok_rows, model_width, dtype=f32),
            shape(tok_rows, model_width),
        ),
        "attention_forward",
        hbm=(5,),
        scratch=(pltpu.VMEM((H * HD, model_width), low), pltpu.SemaphoreType.DMA((1,))),
    )(
        info, tokens, query_pre, w_key, w_value, w_output, gain_two, cosine, sine,
        *normed1_blocks,
    )

    normed2, *cot_even = lax.optimization_barrier((normed2, *cot_even))
    cot_blocks = gather_odd(cot_even)
    n2_blocks = gather(normed2, 2)
    attended_even = gather_even(attended, 1)
    n_blocks = 2 * groups
    all_rows = n_blocks * tok_rows
    wide = model_width + LANES

    dma = pltpu.SemaphoreType.DMA
    units = half_units * exp_dev
    sums, grad_gu, scaled, extra, gate_probs = call(
        lambda *refs: experts_kernel(*refs, n_blocks=n_blocks, tiles=2),
        (
            shape(model_width, 3 * units),
            shape(exp_dev, all_rows, 2 * half_units),
            shape(exp_dev, all_rows, half_units),
            shape(all_rows, LANES, dtype=f32),
            shape(tok_rows, LANES, dtype=f32),
        ),
        "experts",
        hbm=tuple(range(2, 5 + 2 * n_blocks)),
        hbm_out=(0, 1, 2),
        scratch=(
            pltpu.VMEM((all_rows, model_width), low),
            pltpu.VMEM((all_rows, model_width), low),
            pltpu.VMEM((all_rows, LANES), low),
            pltpu.VMEM((exp_dev, model_width, 2 * half_units), low),
            pltpu.VMEM((exp_dev, half_units, model_width), low),
            pltpu.VMEM((exp_dev, all_rows, 2 * half_units), low),
            pltpu.VMEM((exp_dev, all_rows, half_units), low),
            pltpu.VMEM((exp_dev, model_width, 3 * half_units), low),
            pltpu.VMEM((all_rows, LANES), f32),
            pltpu.VMEM((model_width, LANES), low),
            dma((n_blocks,)),
            dma((n_blocks,)),
            dma((n_blocks,)),
            dma((exp_dev, 3)),
            dma((exp_dev, 3)),
        ),
    )(info, w_router, w_gate, w_up, w_down, *n2_blocks, *cot_blocks)
    outer = copies // 2
    shard_rows = model_width // copies
    reduced = lax.psum_scatter(
        sums,
        "dp",
        scatter_dimension=0,
        axis_index_groups=[[2 * o + p for o in range(outer)] for p in range(2)],
        tiled=True,
    )

    odd, even = call(
        lambda *refs: rows_kernel(*refs, experts=experts),
        (shape(groups, tok_rows, wide), shape(groups, tok_rows, wide, dtype=f32)),
        "experts_rows",
        hbm=(2, 3, 4),
        hbm_out=(0, 1),
        scratch=(
            pltpu.VMEM((exp_dev, model_width, 2 * half_units), low),
            pltpu.VMEM((exp_dev, all_rows, 2 * half_units), low),
            pltpu.VMEM((all_rows, model_width), f32),
            pltpu.VMEM((groups, tok_rows, wide), low),
            pltpu.VMEM((groups, tok_rows, wide), f32),
            dma((exp_dev, 3)),
            dma((4,)),
        ),
    )(info, extra, w_gate, w_up, grad_gu)
    odd, *attended_even = lax.optimization_barrier((odd, *attended_even))
    mine = core_sum(odd, even)
    arrived = swap(mine, 2)
    attended_blocks = gather_odd(attended_even)

    (
        grad_hidden, grad_branch, grad_query, kv_odd, kv_even, grad_normed_q, mix_odd, mix_even
    ) = call(
        lambda *refs: backward_kernel(*refs, experts=experts),
        (
            shape(tok_rows, model_width, dtype=f32),
            shape(tok_rows + small_rows(experts + 1), model_width),
            shape(tok_rows, H * HD),
            shape(groups // 2, tok_rows, 2 * KV * HD),
            shape(groups // 2, tok_rows, 2 * KV * HD, dtype=f32),
            shape(tok_rows, model_width, dtype=f32),
            shape(groups, tok_rows, model_width),
            shape(groups, tok_rows, model_width, dtype=f32),
        ),
        "attention_backward",
        hbm=(13, 14, 15, 16, 17),
        hbm_out=(6, 7),
        scratch=(
            pltpu.VMEM((model_width, LANES), low),
            pltpu.VMEM((KV, seq_len, LANES), low),
            pltpu.VMEM((KV, seq_len, LANES), low),
            pltpu.VMEM((model_width, H * HD), low),
            pltpu.VMEM((all_rows, units), low),
            pltpu.VMEM((units, model_width), low),
            pltpu.VMEM((groups, tok_rows, model_width), low),
            pltpu.VMEM((groups, tok_rows, model_width), f32),
            dma((3,)),
            dma((2 * exp_dev,)),
        ),
    )(
        info, mine[0], gate_probs, cotangent, normed2, hidden_state, w_router, gain_two, w_output,
        q_low, lse, cosine, sine, k_two, v_two, w_query, scaled, w_down, *arrived,
    )
    kv_mine = core_sum(kv_odd, kv_even)
    kv_arrived = swap(kv_mine, 1)
    mix_odd, kv_mine = lax.optimization_barrier((mix_odd, kv_mine))
    mix_mine = core_sum(mix_odd, mix_even).reshape(2, groups // 2, tok_rows, model_width)
    mix_pair = mix_mine[0] + send(mix_mine[1].astype(low), 1, 0).astype(f32)
    query_later, grad_branch, *kv_arrived = lax.optimization_barrier(
        (grad_query, grad_branch, *kv_arrived)
    )
    branch_even = gather_even(grad_branch, 1)
    query_even = gather_even(query_later, 1)
    grad_kv, grad_tokens = call(
        tokens_kernel,
        (
            shape(tok_rows + small_rows(1), 2 * KV * HD),
            shape(tok_rows, model_width),
        ),
        "tokens_backward",
        smem=False,
    )(
        kv_mine[0], grad_normed_q, w_key, w_value, tokens, gain_one, grad_hidden, cosine, sine,
        *kv_arrived,
    )
    grad_kv, *later = lax.optimization_barrier((grad_kv, *branch_even, *query_even))
    kv_even_blocks = gather_even(grad_kv, 1)
    branch_blocks = gather_odd(later[: len(branch_even)])
    query_blocks = gather_odd(later[len(branch_even) :])
    mix_pair, *kv_even_blocks = lax.optimization_barrier((mix_pair, *kv_even_blocks))
    kv_blocks = gather_odd(kv_even_blocks)
    mixture = mix_pair[0]
    for a in swap(mix_pair, 1):
        mixture = mixture + a.astype(f32)
    block_out = (hidden_state + mixture).astype(low)

    own_rows = model_width // (copies * groups)
    n_early, n_late = model_width + LANES + H * HD, 2 * KV * HD + LANES
    select = pltpu.VMEM((copies * own_rows, model_width), low)
    early_odd, early_even, normed1_t = call(
        lambda *refs: early_dense_kernel(*refs, groups=groups, count=experts + 1),
        (
            shape(outer, own_rows, n_early),
            shape(outer, own_rows, n_early, dtype=f32),
            shape(copies * own_rows, seq_len),
        ),
        "dense_early",
        scratch=(select,),
    )(info, *normed1_blocks, *attended_blocks, *branch_blocks, *query_blocks)
    early = early_even + send(early_odd, 1, 0).astype(f32)
    late_odd, late_even = call(
        late_dense_kernel,
        (shape(outer, own_rows, n_late), shape(outer, own_rows, n_late, dtype=f32)),
        "dense_late",
        scratch=(select,),
    )(info, normed1_t, *kv_blocks)
    late = late_even + send(late_odd, 1, 0).astype(f32)
    dense_send = jnp.concatenate([early[1:].astype(low), late[1:].astype(low)], axis=2)

    swapped = send(
        lax.dynamic_slice_in_dim(reduced, (1 - half) * shard_rows, shard_rows, 0), 1, 0
    )
    _, dense_send = lax.optimization_barrier((reduced, dense_send))
    dense_arrived = [send(dense_send[o - 1], 2 * o, 0) for o in range(1, outer)]
    k_cols = KV * HD
    (
        grad_gate_w, grad_up_w, grad_down_w, grad_query_w, grad_key_w, grad_value_w,
        grad_output_w, grad_router, grad_norm1, grad_norm2,
    ) = call(
        lambda *refs: final_kernel(*refs, n_early=n_early, n_late=n_late),
        (
            shape(exp_dev, shard_rows, hidden_units, dtype=f32),
            shape(exp_dev, shard_rows, hidden_units, dtype=f32),
            shape(exp_dev, hidden_units, shard_rows, dtype=f32),
            shape(own_rows, H * HD, dtype=f32),
            shape(own_rows, k_cols, dtype=f32),
            shape(own_rows, k_cols, dtype=f32),
            shape(own_rows, model_width, dtype=f32),
            shape(experts, own_rows, dtype=f32),
            shape(1, own_rows, dtype=f32),
            shape(1, own_rows, dtype=f32),
        ),
        "place",
    )(info, reduced, swapped, early, late, *dense_arrived)
    return (
        block_out,
        grad_tokens,
        grad_norm1[0],
        grad_query_w,
        grad_key_w,
        grad_value_w,
        grad_output_w,
        grad_norm2[0],
        grad_router.T,
        grad_gate_w,
        grad_up_w,
        grad_down_w,
    )


def solution(mesh):
    return jax.shard_map(
        shards,
        mesh=mesh,
        in_specs=(
            P(("dp", "expert"), None),
            P("dp"),
            P(("dp", "expert"), None),
            P(),
            P(),
            P(),
            P(),
            P(),
            P(),
            P(),
            P("expert", None, None),
            P("expert", None, None),
            P("expert", None, None),
            P(("dp", "expert"), None),
        ),
        out_specs=(
            P(("dp", "expert"), None),
            P(("dp", "expert"), None),
            P(("dp", "expert")),
            P(("dp", "expert"), None),
            P(("dp", "expert"), None),
            P(("dp", "expert"), None),
            P(("dp", "expert"), None),
            P(("dp", "expert")),
            P(("dp", "expert"), None),
            P("expert", "dp", None),
            P("expert", "dp", None),
            P("expert", None, "dp"),
        ),
        check_vma=False,
    )
```

profile of v0, /device:TPU:0, one launch (start us, length us, event | category | flops | bytes accessed | tf_op | source)
XLA Modules:
  0.0 222.6 jit_solution(10815926686543695055)
XLA Ops:
  9.4 3.0 %collective-permute-start = (bf16[128,1024]{1,0:T(8,128)(2,1)S(1)}, bf16[128,1024]{1,0:T(8,128)(2,1)S(1)}, u32[]{:S(2)}, u32[]{:S(2)}) collective-permute-start(bf16[128,1024]{1,0:T(8,128)(2,1)S(1)} %fusion.2.rest_0_.refs_1_), channel_id=1, source_target_pairs={{0,2},{1,3},{2,0},{3,1},{4,6},{5,7},{6,4},{7,5},{8,10},{9,11},{10,... | collective-permute-start | bytes 786440 | tf_op jit(solution)/shard_map/ppermute | solution.py:599
  15.6 2.6 %negate_select_fusion = (f32[512,128]{1,0:T(8,128)}, f32[512,128]{1,0:T(8,128)}) fusion(s32[128]{0:T(128)S(1)} %get-tuple-element.162, s32[128]{0:T(128)S(1)} %get-tuple-element.164, s32[128]{0:T(128)S(1)} %get-tuple-element.163, s32[128]{0:T(128)S(1)} %get-tuple-element.165, s32[512]{0:T(512)S(1)} %get-tuple-element.155, s32[512]{0:T(512)S(1)} %get-tuple-element.156, ...), kind=kLoop, calls=%fused_computation.22 | loop fusion | flops 917504 | bytes 535812 | tf_op jit(solution)/shard_map/jit(_where)/select_n | solution.py:26
  19.3 1.7 collective-permute-start.3
  22.8 2.8 %fusion.16.query_ref = f32[128,1024]{1,0:T(8,128)} fusion(bf16[128,1024]{1,0:T(8,128)(2,1)S(1)} %fusion.2.rest_0_.refs_1_, bf16[1024,1024]{1,0:T(8,128)(2,1)} %refs_15_.1), kind=kOutput, calls=%fused_computation.58 | convolution fusion | flops 268435456 | bytes 2883584 | tf_op jit(solution)/shard_map/dot_general | solution.py:46
  27.0 7.6 %attention_forward.1 = (bf16[128,1024]{1,0:T(8,128)(2,1)}, bf16[8,512,128]{2,1,0:T(8,128)(2,1)}, bf16[8,512,128]{2,1,0:T(8,128)(2,1)}, f32[8,256]{1,0:T(8,128)},...) custom-call(s32[4]{0:T(128)} %pad_add_fusion.info_ref.refs_0_, ...), custom_call_target="tpu_custom_call" | custom-call | tf_op jit(solution)/shard_map/attention_forward/pallas_call | solution.py:550
  35.8 1.7 collective-permute-start.9
  39.8 5.5 %collective-permute-done.9.refs_9_ = bf16[128,1024]{1,0:T(8,128)(2,1)S(1)} collective-permute-done((bf16[128,1024]{1,0:T(8,128)(2,1)}, bf16[128,1024]{1,0:T(8,128)(2,1)S(1)}, u32[]{:S(2)}, u32[]{:S(2)}) %collective-permute-start.9) | collective-permute-done | bytes 262176 | tf_op jit(solution)/shard_map/ppermute | solution.py:599
  45.3 4.7 %collective-permute-done.11.refs_11_ = bf16[128,1024]{1,0:T(8,128)(2,1)S(1)} collective-permute-done((bf16[128,1024]{1,0:T(8,128)(2,1)}, bf16[128,1024]{1,0:T(8,128)(2,1)S(1)}, u32[]{:S(2)}, u32[]{:S(2)}) %collective-permute-start.11) | collective-permute-done | bytes 262176 | tf_op jit(solution)/shard_map/ppermute | solution.py:599
  54.7 22.1 %experts.1 = (bf16[1024,3072]{1,0:T(8,128)(2,1)}, bf16[4,1024,512]{2,1,0:T(8,128)(2,1)}, bf16[4,1024,256]{2,1,0:T(8,128)(2,1)}, f32[1024,128]{1,0:T(8,128)}, f32[128,128]{1,0:T(8,128)}) custom-call(s32[4]{0:T(128)} %pad_add_fusion.info_ref.refs_0_, bf16[1024,16]{1,0:T(8,128)(2,1)} %copy.30.refs_1_.refs_6_, bf16[4,1024,512]{2,1,0:T(8,128)(2,1)} %refs_2_.3, ...), custom_call_target="tpu_custom_call" | custom-call | tf_op jit(solution)/shard_map/experts/pallas_call | solution.py:550
  78.2 10.7 %experts_rows.1 = (bf16[4,128,1152]{2,1,0:T(8,128)(2,1)}, f32[4,128,1152]{2,1,0:T(8,128)}) custom-call(s32[4]{0:T(128)} %pad_add_fusion.info_ref.refs_0_, f32[1024,128]{1,0:T(8,128)} %get-tuple-element.90.refs_1_, bf16[4,1024,512]{2,1,0:T(8,128)(2,1)} %refs_2_.3, bf16[4,1024,512]{2,1,0:T(8,128)(2,1)} %refs_3_.4, bf16[4,1024,512]{2,1,0:T(8,128)(2,1)} %get-tuple-element.91.refs_4_), custom_call_target="tpu_custom_call" | custom-call | tf_op jit(solution)/shard_map/experts_rows/pallas_call | solution.py:550
  88.9 3.0 %collective-permute-done.18 = bf16[4,128,1152]{2,1,0:T(8,128)(2,1)S(1)} collective-permute-done((bf16[4,128,1152]{2,1,0:T(8,128)(2,1)}, bf16[4,128,1152]{2,1,0:T(8,128)(2,1)S(1)}, u32[]{:S(2)}, u32[]{:S(2)}) %collective-permute-start.18) | collective-permute-done | bytes 1179680 | tf_op jit(solution)/shard_map/ppermute | solution.py:599
  92.0 2.0 fusion.15
  94.1 1.8 collective-permute-start.19
  98.5 4.7 %collective-permute-done.19.refs_18_ = bf16[128,1152]{1,0:T(8,128)(2,1)S(1)} collective-permute-done((bf16[128,1152]{1,0:T(8,128)(2,1)S(1)}, bf16[128,1152]{1,0:T(8,128)(2,1)S(1)}, u32[]{:S(2)}, u32[]{:S(2)}) %collective-permute-start.19) | collective-permute-done | bytes 294944 | tf_op jit(solution)/shard_map/ppermute | solution.py:599
  103.2 2.5 %collective-permute-done.20.refs_19_ = bf16[128,1152]{1,0:T(8,128)(2,1)S(1)} collective-permute-done((bf16[128,1152]{1,0:T(8,128)(2,1)S(1)}, bf16[128,1152]{1,0:T(8,128)(2,1)S(1)}, u32[]{:S(2)}, u32[]{:S(2)}) %collective-permute-start.20) | collective-permute-done | bytes 294944 | tf_op jit(solution)/shard_map/ppermute | solution.py:599
  105.7 5.0 %collective-permute-done.21.refs_20_ = bf16[128,1152]{1,0:T(8,128)(2,1)S(1)} collective-permute-done((bf16[128,1152]{1,0:T(8,128)(2,1)S(1)}, bf16[128,1152]{1,0:T(8,128)(2,1)S(1)}, u32[]{:S(2)}, u32[]{:S(2)}) %collective-permute-start.21) | collective-permute-done | bytes 294944 | tf_op jit(solution)/shard_map/ppermute | solution.py:599
  111.5 15.2 %attention_backward.1 = (f32[128,1024]{1,0:T(8,128)}, bf16[176,1024]{1,0:T(8,128)(2,1)}, bf16[128,1024]{1,0:T(8,128)(2,1)}, bf16[2,128,1024]{2,1,0:T(8,128)(2,1)...) custom-call(s32[4]{0:T(128)} %pad_add_fusion.info_ref.refs_0_, ...), custom_call_target="tpu_custom_call" | custom-call | tf_op jit(solution)/shard_map/attention_backward/pallas_call | solution.py:550
  126.8 2.1 collective-permute-done.22
  130.5 1.7 collective-permute-start.25
  132.8 6.4 %collective-permute-done.25.rest_0_ = bf16[128,1024]{1,0:T(8,128)(2,1)S(1)} collective-permute-done((bf16[128,1024]{1,0:T(8,128)(2,1)S(1)}, bf16[128,1024]{1,0:T(8,128)(2,1)S(1)}, u32[]{:S(2)}, u32[]{:S(2)}) %collective-permute-start.25) | collective-permute-done | bytes 262176 | tf_op jit(solution)/shard_map/ppermute | solution.py:599
  146.4 4.0 %tokens_backward.1 = (bf16[144,1024]{1,0:T(8,128)(2,1)}, bf16[128,1024]{1,0:T(8,128)(2,1)}) custom-call(f32[128,1024]{1,0:T(8,128)} %slice_bitcast_fusion.1.own_ref, f32[128,1024]{1,0:T(8,128)} %get-tuple-element.108.gn_ref, bf16[1024,512]{1,0:T(8,128)(2,1)} %wk_ref.3, bf16[1024,512]{1,0:T(8,128)(2,1)} %wv_ref.3, bf16[128,1024]{1,0:T(8,128)(2,1)} %tokens_ref.3, ...), custom_call_target="tpu_custom_call" | custom-call | tf_op jit(solution)/shard_map/tokens_backward/pallas_call | solution.py:550
  150.4 4.5 %collective-permute-done.27.refs_15_ = bf16[128,1024]{1,0:T(8,128)(2,1)} collective-permute-done((bf16[128,1024]{1,0:T(8,128)(2,1)}, bf16[128,1024]{1,0:T(8,128)(2,1)}, u32[]{:S(2)}, u32[]{:S(2)}) %collective-permute-start.27) | collective-permute-done | bytes 262176 | tf_op jit(solution)/shard_map/ppermute | solution.py:599
  157.5 1.7 collective-permute-start.28
  160.6 5.4 %dense_early.1 = (bf16[4,32,2176]{2,1,0:T(8,128)(2,1)}, f32[4,32,2176]{2,1,0:T(8,128)}, bf16[256,512]{1,0:T(8,128)(2,1)}) custom-call(s32[4]{0:T(128)} %pad_add_fusion.info_ref.refs_0_, bf16[128,1024]{1,0:T(8,128)(2,1)} %copy-done.2, bf16[128,1024]{1,0:T(8,128)(2,1)} %copy-done.9, bf16[128,1024]{1,0:T(8,128)(2,1)} %copy-done.8, ...), custom_call_target="tpu_custom_call" | custom-call | tf_op jit(solution)/shard_map/dense_early/pallas_call | solution.py:550
  167.6 2.5 %slice_add_fusion = f32[2,128,1024]{2,1,0:T(8,128)} fusion(f32[4,128,1024]{2,1,0:T(8,128)} %copy-done, bf16[2,128,1024]{2,1,0:T(8,128)(2,1)} %collective-permute-done.24), kind=kLoop, calls=%fused_computation.4 | loop fusion | flops 524288 | bytes 2621440 | tf_op jit(solution)/shard_map/add | solution.py:779
  173.1 3.0 %dense_late.1 = (bf16[4,32,1152]{2,1,0:T(8,128)(2,1)}, f32[4,32,1152]{2,1,0:T(8,128)}) custom-call(s32[4]{0:T(128)} %pad_add_fusion.info_ref.refs_0_, bf16[256,512]{1,0:T(8,128)(2,1)} %get-tuple-element.128.normed_t_ref, bf16[144,1024]{1,0:T(8,128)(2,1)} %get-tuple-element.129.rest_0_, bf16[144,1024]{1,0:T(8,128)(2,1)} %copy-done.16, ...), custom_call_target="tpu_custom_call" | custom-call | tf_op jit(solution)/shard_map/dense_late/pallas_call | solution.py:550
  176.7 5.1 %collective-permute-done.37 = bf16[4,32,2176]{2,1,0:T(8,128)(2,1)S(1)} collective-permute-done((bf16[4,32,2176]{2,1,0:T(8,128)(2,1)}, bf16[4,32,2176]{2,1,0:T(8,128)(2,1)S(1)}, u32[]{:S(2)}, u32[]{:S(2)}) %collective-permute-start.37) | collective-permute-done | bytes 557088 | tf_op jit(solution)/shard_map/ppermute | solution.py:599
  184.9 2.2 collective-permute-done.40
  192.4 2.1 collective-permute-start.42
  196.2 5.4 %collective-permute-done.41.refs_5_ = bf16[32,3328]{1,0:T(8,128)(2,1)S(1)} collective-permute-done((bf16[32,3328]{1,0:T(8,128)(2,1)S(1)}, bf16[32,3328]{1,0:T(8,128)(2,1)S(1)}, u32[]{:S(2)}, u32[]{:S(2)}) %collective-permute-start.41) | collective-permute-done | bytes 213024 | tf_op jit(solution)/shard_map/ppermute | solution.py:599
  201.6 9.1 %collective-permute-done.42.refs_6_ = bf16[32,3328]{1,0:T(8,128)(2,1)S(1)} collective-permute-done((bf16[32,3328]{1,0:T(8,128)(2,1)S(1)}, bf16[32,3328]{1,0:T(8,128)(2,1)S(1)}, u32[]{:S(2)}, u32[]{:S(2)}) %collective-permute-start.42) | collective-permute-done | bytes 213024 | tf_op jit(solution)/shard_map/ppermute | solution.py:599
  211.4 4.4 %place.1 = (f32[4,128,512]{2,1,0:T(8,128)}, f32[4,128,512]{2,1,0:T(8,128)}, f32[4,512,128]{2,1,0:T(8,128)}, f32[32,1024]{1,0:T(8,128)}, f32[32,512]{1,0:T(8,128)...) custom-call(s32[4]{0:T(128)} %pad_add_fusion.info_ref.refs_0_, ...), custom_call_target="tpu_custom_call" | custom-call | tf_op jit(solution)/shard_map/place/pallas_call | solution.py:550
  (176 shorter events, 51.4 us)
Async XLA Ops:
  7.2 181.0 %reduce-scatter.2.cloned.1.call-start = ((), (), s32[]{:S(2)}) async-start(), calls=%async_computation.1 | async-start | bytes 7864320 | tf_op jit(solution)/shard_map/reduce_scatter | solution.py:713
  9.4 9.3 %collective-permute-start = (bf16[128,1024]{1,0:T(8,128)(2,1)S(1)}, bf16[128,1024]{1,0:T(8,128)(2,1)S(1)}, u32[]{:S(2)}, u32[]{:S(2)}) collective-permute-start(bf16[128,1024]{1,0:T(8,128)(2,1)S(1)} %fusion.2.rest_0_.refs_1_), channel_id=1, source_target_pairs={{0,2},{1,3},{2,0},{3,1},{4,6},{5,7},{6,4},{7,5},{8,10},{9,11},{10,... | collective-permute-start | bytes 786440 | tf_op jit(solution)/shard_map/ppermute | solution.py:599
  18.8 6.8 %collective-permute-start.1 = (bf16[128,1024]{1,0:T(8,128)(2,1)S(1)}, bf16[128,1024]{1,0:T(8,128)(2,1)S(1)}, u32[]{:S(2)}, u32[]{:S(2)}) collective-permute-start(bf16[128,1024]{1,0:T(8,128)(2,1)S(1)} %fusion.2.rest_0_.refs_1_), channel_id=1, source_target_pairs={{0,1},{1,0},{2,3},{3,2},{4,5},{5,4},{6,7},{7,6},{8,9},{9,8},{10,11... | collective-permute-start | bytes 786440 | tf_op jit(solution)/shard_map/ppermute | solution.py:599
  18.8 6.8 %collective-permute-start.2 = (bf16[128,1024]{1,0:T(8,128)(2,1)S(1)}, bf16[128,1024]{1,0:T(8,128)(2,1)S(1)}, u32[]{:S(2)}, u32[]{:S(2)}) collective-permute-start(bf16[128,1024]{1,0:T(8,128)(2,1)S(1)} %collective-permute-done.rest_2_.refs_3_), channel_id=1, source_target_pairs={{0,1},{1,0},{2,3},{3,2},{4,5},{5,4},{6,7},{7,6},{8,9},{9,8},{10,11... | collective-permute-start | bytes 786440 | tf_op jit(solution)/shard_map/ppermute | solution.py:599
  19.3 15.3 %collective-permute-start.3 = (bf16[128,1152]{1,0:T(8,128)(2,1)S(1)}, bf16[128,1152]{1,0:T(8,128)(2,1)}, u32[]{:S(2)}, u32[]{:S(2)}) collective-permute-start(bf16[128,1152]{1,0:T(8,128)(2,1)S(1)} %pad_maximum_fusion.1.refs_13_), channel_id=1, source_target_pairs={{0,2},{1,3},{2,0},{3,1},{4,6},{5,7},{6,4},{7,5},{8,10},{9,11},{10,... | collective-permute-start | bytes 884744 | tf_op jit(solution)/shard_map/ppermute | solution.py:599
  21.0 13.5 %collective-permute-start.4 = (bf16[128,1152]{1,0:T(8,128)(2,1)S(1)}, bf16[128,1152]{1,0:T(8,128)(2,1)}, u32[]{:S(2)}, u32[]{:S(2)}) collective-permute-start(bf16[128,1152]{1,0:T(8,128)(2,1)S(1)} %pad_maximum_fusion.1.refs_13_), channel_id=1, source_target_pairs={{0,4},{1,5},{2,6},{3,7},{4,0},{5,1},{6,2},{7,3},{8,12},{9,13},{10,... | collective-permute-start | bytes 884744 | tf_op jit(solution)/shard_map/ppermute | solution.py:599
  22.5 13.3 %collective-permute-start.5 = (bf16[128,1152]{1,0:T(8,128)(2,1)S(1)}, bf16[128,1152]{1,0:T(8,128)(2,1)}, u32[]{:S(2)}, u32[]{:S(2)}) collective-permute-start(bf16[128,1152]{1,0:T(8,128)(2,1)S(1)} %pad_maximum_fusion.1.refs_13_), channel_id=1, source_target_pairs={{0,6},{1,7},{2,4},{3,5},{4,2},{5,3},{6,0},{7,1},{8,14},{9,15},{10,... | collective-permute-start | bytes 884744 | tf_op jit(solution)/shard_map/ppermute | solution.py:599
  35.8 9.5 %collective-permute-start.9 = (bf16[128,1024]{1,0:T(8,128)(2,1)}, bf16[128,1024]{1,0:T(8,128)(2,1)S(1)}, u32[]{:S(2)}, u32[]{:S(2)}) collective-permute-start(bf16[128,1024]{1,0:T(8,128)(2,1)} %get-tuple-element.85.refs_5_.refs_4_), channel_id=1, source_target_pairs={{0,4},{1,5},{2,6},{3,7},{4,0},{5,1},{6,2},{7,3},{8,12},{9,13},{10,... | collective-permute-start | bytes 786440 | tf_op jit(solution)/shard_map/ppermute | solution.py:599
  37.5 12.4 %collective-permute-start.11 = (bf16[128,1024]{1,0:T(8,128)(2,1)}, bf16[128,1024]{1,0:T(8,128)(2,1)S(1)}, u32[]{:S(2)}, u32[]{:S(2)}) collective-permute-start(bf16[128,1024]{1,0:T(8,128)(2,1)} %get-tuple-element.85.refs_5_.refs_4_), channel_id=1, source_target_pairs={{0,6},{1,7},{2,4},{3,5},{4,2},{5,3},{6,0},{7,1},{8,14},{9,15},{10,... | collective-permute-start | bytes 786440 | tf_op jit(solution)/shard_map/ppermute | solution.py:599
  39.0 12.3 %collective-permute-start.7 = (bf16[128,1024]{1,0:T(8,128)(2,1)}, bf16[128,1024]{1,0:T(8,128)(2,1)S(1)}, u32[]{:S(2)}, u32[]{:S(2)}) collective-permute-start(bf16[128,1024]{1,0:T(8,128)(2,1)} %get-tuple-element.85.refs_5_.refs_4_), channel_id=1, source_target_pairs={{0,2},{1,3},{2,0},{3,1},{4,6},{5,7},{6,4},{7,5},{8,10},{9,11},{10,... | collective-permute-start | bytes 786440 | tf_op jit(solution)/shard_map/ppermute | solution.py:599
  39.3 12.5 %collective-permute-start.13 = (bf16[128,1152]{1,0:T(8,128)(2,1)S(1)}, bf16[128,1152]{1,0:T(8,128)(2,1)S(1)}, u32[]{:S(2)}, u32[]{:S(2)}) collective-permute-start(bf16[128,1152]{1,0:T(8,128)(2,1)S(1)} %pad_maximum_fusion.1.refs_13_), channel_id=1, source_target_pairs={{0,1},{1,0},{2,3},{3,2},{4,5},{5,4},{6,7},{7,6},{8,9},{9,8},{10,11... | collective-permute-start | bytes 884744 | tf_op jit(solution)/shard_map/ppermute | solution.py:599
  39.3 12.6 %collective-permute-start.14 = (bf16[128,1152]{1,0:T(8,128)(2,1)}, bf16[128,1152]{1,0:T(8,128)(2,1)}, u32[]{:S(2)}, u32[]{:S(2)}) collective-permute-start(bf16[128,1152]{1,0:T(8,128)(2,1)} %collective-permute-done.3.refs_15_), channel_id=1, source_target_pairs={{0,1},{1,0},{2,3},{3,2},{4,5},{5,4},{6,7},{7,6},{8,9},{9,8},{10,11... | collective-permute-start | bytes 884744 | tf_op jit(solution)/shard_map/ppermute | solution.py:599
  45.3 6.1 %collective-permute-start.6 = (bf16[128,1024]{1,0:T(8,128)(2,1)}, bf16[128,1024]{1,0:T(8,128)(2,1)S(1)}, u32[]{:S(2)}, u32[]{:S(2)}) collective-permute-start(bf16[128,1024]{1,0:T(8,128)(2,1)} %get-tuple-element.85.refs_5_.refs_4_), channel_id=1, source_target_pairs={{0,1},{1,0},{2,3},{3,2},{4,5},{5,4},{6,7},{7,6},{8,9},{9,8},{10,11... | collective-permute-start | bytes 786440 | tf_op jit(solution)/shard_map/ppermute | solution.py:599
  77.8 11.0 %collective-permute-start.17 = (bf16[128,1024]{1,0:T(8,128)(2,1)S(1)}, bf16[128,1024]{1,0:T(8,128)(2,1)}, u32[]{:S(2)}, u32[]{:S(2)}) collective-permute-start(bf16[128,1024]{1,0:T(8,128)(2,1)S(1)} %copy-done.28), channel_id=1, source_target_pairs={{0,2},{1,3},{2,0},{3,1},{4,6},{5,7},{6,4},{7,5},{8,10},{9,11},{10,... | collective-permute-start | bytes 786440 | tf_op jit(solution)/shard_map/ppermute | solution.py:599
  94.1 9.1 %collective-permute-start.19 = (bf16[128,1152]{1,0:T(8,128)(2,1)S(1)}, bf16[128,1152]{1,0:T(8,128)(2,1)S(1)}, u32[]{:S(2)}, u32[]{:S(2)}) collective-permute-start(bf16[128,1152]{1,0:T(8,128)(2,1)S(1)} %get-tuple-element.148), channel_id=1, source_target_pairs={{0,2},{1,3},{2,0},{3,1},{4,6},{5,7},{6,4},{7,5},{8,10},{9,11},{10,... | collective-permute-start | bytes 884744 | tf_op jit(solution)/shard_map/ppermute | solution.py:599
  95.8 9.9 %collective-permute-start.20 = (bf16[128,1152]{1,0:T(8,128)(2,1)S(1)}, bf16[128,1152]{1,0:T(8,128)(2,1)S(1)}, u32[]{:S(2)}, u32[]{:S(2)}) collective-permute-start(bf16[128,1152]{1,0:T(8,128)(2,1)S(1)} %get-tuple-element.147), channel_id=1, source_target_pairs={{0,4},{1,5},{2,6},{3,7},{4,0},{5,1},{6,2},{7,3},{8,12},{9,13},{10,... | collective-permute-start | bytes 884744 | tf_op jit(solution)/shard_map/ppermute | solution.py:599
  97.3 13.4 %collective-permute-start.21 = (bf16[128,1152]{1,0:T(8,128)(2,1)S(1)}, bf16[128,1152]{1,0:T(8,128)(2,1)S(1)}, u32[]{:S(2)}, u32[]{:S(2)}) collective-permute-start(bf16[128,1152]{1,0:T(8,128)(2,1)S(1)} %get-tuple-element.146), channel_id=1, source_target_pairs={{0,6},{1,7},{2,4},{3,5},{4,2},{5,3},{6,0},{7,1},{8,14},{9,15},{10,... | collective-permute-start | bytes 884744 | tf_op jit(solution)/shard_map/ppermute | solution.py:599
  130.3 10.9 %collective-permute-start.23 = (bf16[4,128,1024]{2,1,0:T(8,128)(2,1)}, bf16[4,128,1024]{2,1,0:T(8,128)(2,1)S(1)}, u32[]{:S(2)}, u32[]{:S(2)}) collective-permute-start(bf16[4,128,1024]{2,1,0:T(8,128)(2,1)} %get-tuple-element.106), channel_id=1, source_target_pairs={{0,1},{1,0},{2,3},{3,2},{4,5},{5,4},{6,7},{7,6},{8,9},{9,8},{10,11... | collective-permute-start | bytes 3145736 | tf_op jit(solution)/shard_map/ppermute | solution.py:599
  130.5 8.7 %collective-permute-start.25 = (bf16[128,1024]{1,0:T(8,128)(2,1)S(1)}, bf16[128,1024]{1,0:T(8,128)(2,1)S(1)}, u32[]{:S(2)}, u32[]{:S(2)}) collective-permute-start(bf16[128,1024]{1,0:T(8,128)(2,1)S(1)} %fusion.5), channel_id=1, source_target_pairs={{0,2},{1,3},{2,0},{3,1},{4,6},{5,7},{6,4},{7,5},{8,10},{9,11},{10,... | collective-permute-start | bytes 786440 | tf_op jit(solution)/shard_map/ppermute | solution.py:599
  132.2 23.1 %collective-permute-start.31 = (bf16[128,1024]{1,0:T(8,128)(2,1)S(1)}, bf16[128,1024]{1,0:T(8,128)(2,1)}, u32[]{:S(2)}, u32[]{:S(2)}) collective-permute-start(bf16[128,1024]{1,0:T(8,128)(2,1)S(1)} %copy-done.29), channel_id=1, source_target_pairs={{0,1},{1,0},{2,3},{3,2},{4,5},{5,4},{6,7},{7,6},{8,9},{9,8},{10,11... | collective-permute-start | bytes 786440 | tf_op jit(solution)/shard_map/ppermute | solution.py:599
  132.3 23.1 %collective-permute-start.32 = (bf16[128,1024]{1,0:T(8,128)(2,1)}, bf16[128,1024]{1,0:T(8,128)(2,1)}, u32[]{:S(2)}, u32[]{:S(2)}) collective-permute-start(bf16[128,1024]{1,0:T(8,128)(2,1)} %collective-permute-done.17.refs_7_), channel_id=1, source_target_pairs={{0,1},{1,0},{2,3},{3,2},{4,5},{5,4},{6,7},{7,6},{8,9},{9,8},{10,11... | collective-permute-start | bytes 786440 | tf_op jit(solution)/shard_map/ppermute | solution.py:599
  139.2 15.7 %collective-permute-start.26 = (bf16[176,1024]{1,0:T(8,128)(2,1)S(1)}, bf16[176,1024]{1,0:T(8,128)(2,1)S(1)}, u32[]{:S(2)}, u32[]{:S(2)}) collective-permute-start(bf16[176,1024]{1,0:T(8,128)(2,1)S(1)} %copy-done.12), channel_id=1, source_target_pairs={{0,2},{1,3},{2,0},{3,1},{4,6},{5,7},{6,4},{7,5},{8,10},{9,11},{10,... | collective-permute-start | bytes 1081352 | tf_op jit(solution)/shard_map/ppermute | solution.py:599
  140.8 14.0 %collective-permute-start.27 = (bf16[128,1024]{1,0:T(8,128)(2,1)}, bf16[128,1024]{1,0:T(8,128)(2,1)}, u32[]{:S(2)}, u32[]{:S(2)}) collective-permute-start(bf16[128,1024]{1,0:T(8,128)(2,1)} %get-tuple-element.124.refs_13_), channel_id=1, source_target_pairs={{0,2},{1,3},{2,0},{3,1},{4,6},{5,7},{6,4},{7,5},{8,10},{9,11},{10,... | collective-permute-start | bytes 786440 | tf_op jit(solution)/shard_map/ppermute | solution.py:599
  143.9 23.6 %collective-permute-start.24 = (bf16[2,128,1024]{2,1,0:T(8,128)(2,1)}, bf16[2,128,1024]{2,1,0:T(8,128)(2,1)}, u32[]{:S(2)}, u32[]{:S(2)}) collective-permute-start(bf16[2,128,1024]{2,1,0:T(8,128)(2,1)} %slice.94), channel_id=1, source_target_pairs={{0,4},{1,5},{2,6},{3,7},{4,0},{5,1},{6,2},{7,3},{8,12},{9,13},{10,... | collective-permute-start | bytes 1572872 | tf_op jit(solution)/shard_map/ppermute | solution.py:599
  157.5 12.6 %collective-permute-start.28 = (bf16[144,1024]{1,0:T(8,128)(2,1)}, bf16[144,1024]{1,0:T(8,128)(2,1)}, u32[]{:S(2)}, u32[]{:S(2)}) collective-permute-start(bf16[144,1024]{1,0:T(8,128)(2,1)} %get-tuple-element.129.rest_0_), channel_id=1, source_target_pairs={{0,2},{1,3},{2,0},{3,1},{4,6},{5,7},{6,4},{7,5},{8,10},{9,11},{10,... | collective-permute-start | bytes 884744 | tf_op jit(solution)/shard_map/ppermute | solution.py:599
  166.0 15.8 %collective-permute-start.37 = (bf16[4,32,2176]{2,1,0:T(8,128)(2,1)}, bf16[4,32,2176]{2,1,0:T(8,128)(2,1)S(1)}, u32[]{:S(2)}, u32[]{:S(2)}) collective-permute-start(bf16[4,32,2176]{2,1,0:T(8,128)(2,1)} %get-tuple-element.127), channel_id=1, source_target_pairs={{0,4},{1,5},{2,6},{3,7},{4,0},{5,1},{6,2},{7,3},{8,12},{9,13},{10,... | collective-permute-start | bytes 1671176 | tf_op jit(solution)/shard_map/ppermute | solution.py:599
  176.1 11.0 %collective-permute-start.40 = (bf16[4,32,1152]{2,1,0:T(8,128)(2,1)}, bf16[4,32,1152]{2,1,0:T(8,128)(2,1)S(1)}, u32[]{:S(2)}, u32[]{:S(2)}) collective-permute-start(bf16[4,32,1152]{2,1,0:T(8,128)(2,1)} %get-tuple-element.132), channel_id=1, source_target_pairs={{0,4},{1,5},{2,6},{3,7},{4,0},{5,1},{6,2},{7,3},{8,12},{9,13},{10,... | collective-permute-start | bytes 884744 | tf_op jit(solution)/shard_map/ppermute | solution.py:599
  184.4 11.0 %collective-permute-start.29 = (bf16[128,1024]{1,0:T(8,128)(2,1)S(1)}, bf16[128,1024]{1,0:T(8,128)(2,1)S(1)}, u32[]{:S(2)}, u32[]{:S(2)}) collective-permute-start(bf16[128,1024]{1,0:T(8,128)(2,1)S(1)} %fusion.6), channel_id=1, source_target_pairs={{0,2},{1,3},{2,0},{3,1},{4,6},{5,7},{6,4},{7,5},{8,10},{9,11},{10,... | collective-permute-start | bytes 786440 | tf_op jit(solution)/shard_map/ppermute | solution.py:599
  189.3 22.1 %collective-permute-start.30 = (bf16[128,3072]{1,0:T(8,128)(2,1)S(1)}, bf16[128,3072]{1,0:T(8,128)(2,1)}, u32[]{:S(2)}, u32[]{:S(2)}) collective-permute-start(bf16[128,3072]{1,0:T(8,128)(2,1)S(1)} %constant_dynamic-slice_fusion), channel_id=1, source_target_pairs={{0,4},{1,5},{2,6},{3,7},{4,0},{5,1},{6,2},{7,3},{8,12},{9,13},{10,... | collective-permute-start | bytes 2359304 | tf_op jit(solution)/shard_map/ppermute | solution.py:599
  190.9 10.7 %collective-permute-start.41 = (bf16[32,3328]{1,0:T(8,128)(2,1)S(1)}, bf16[32,3328]{1,0:T(8,128)(2,1)S(1)}, u32[]{:S(2)}, u32[]{:S(2)}) collective-permute-start(bf16[32,3328]{1,0:T(8,128)(2,1)S(1)} %get-tuple-element.151), channel_id=1, source_target_pairs={{0,8},{1,9},{2,10},{3,11},{4,12},{5,13},{6,14},{7,15},{8,0},{9,1},... | collective-permute-start | bytes 638984 | tf_op jit(solution)/shard_map/ppermute | solution.py:599
  192.4 18.2 %collective-permute-start.42 = (bf16[32,3328]{1,0:T(8,128)(2,1)S(1)}, bf16[32,3328]{1,0:T(8,128)(2,1)S(1)}, u32[]{:S(2)}, u32[]{:S(2)}) collective-permute-start(bf16[32,3328]{1,0:T(8,128)(2,1)S(1)} %get-tuple-element.150), channel_id=1, source_target_pairs={{0,16},{1,17},{2,18},{3,19},{4,20},{5,21},{6,22},{7,23},{8,24},{9,... | collective-permute-start | bytes 638984 | tf_op jit(solution)/shard_map/ppermute | solution.py:599
  194.5 16.2 %collective-permute-start.43 = (bf16[32,3328]{1,0:T(8,128)(2,1)S(1)}, bf16[32,3328]{1,0:T(8,128)(2,1)S(1)}, u32[]{:S(2)}, u32[]{:S(2)}) collective-permute-start(bf16[32,3328]{1,0:T(8,128)(2,1)S(1)} %get-tuple-element.149), channel_id=1, source_target_pairs={{0,24},{1,25},{2,26},{3,27},{4,28},{5,29},{6,30},{7,31},{8,16},{9,... | collective-permute-start | bytes 638984 | tf_op jit(solution)/shard_map/ppermute | solution.py:599
  (50 other events, 244.5 us)
Sparse Core Ops, SparseCore 0:
  77.0 111.0 reduce-scatter.1
where the time goes:
time: 224 us; the launch traced here: 223 us
  Pallas kernels  72.3 us (32%)
  waiting for transfers between devices  67.9 us (30%)
  starting transfers between devices  34 us (15%)
  other arithmetic  15.7 us (7%)
  between operations  15.1 us (7%)
  local copies, waits for them, and re-layouts  14.8 us (7%)
  matrix products  2.83 us (1%)
    pallas_call x8, Pallas kernels, run(): pl.pallas_call(kernel, out_shape=out_shape, in_specs=specs, out_specs=[pl...  72.3 us
    ppermute x44, waiting for transfers between devices, send(): lax.ppermute(block, ('dp', 'expert'), [(i * groups + j, (i ^ pair_flip) *...  67 us
    ppermute x44, starting transfers between devices, send(): lax.ppermute(block, ('dp', 'expert'), [(i * groups + j, (i ^ pair_flip) *...  34 us
    unnamed x75, local copies, waits for them, and re-layouts  10.6 us
  transfers between devices with their start and end apart: 45, of which 21 were waited for; matrix products, arithmetic and copies ran while one was open for 10% of the time, Pallas kernels for 21%

commit v1 on v0

--- a/solution.py
+++ b/solution.py
@@ -98,14 +98,19 @@
 
 
 def forward_kernel(
-    info_ref, tokens_ref, query_ref, wk_ref, wv_ref, wo_ref, gain_ref, cos_ref, sin_ref, *rest
+    info_ref, wq_ref, wk_ref, wv_ref, wo_ref, gain_one_ref, gain_two_ref, cos_ref, sin_ref, *rest
 ):
-    blocks, outs = rest[:-9], rest[-9:]
-    q_ref, k_ref, v_ref, lse_ref, att_ref, hid_ref, n2_ref, wo_held, sems = outs
-    wo_copy = start_copies([(wo_ref, wo_held)], sems)
+    blocks, outs = rest[:-11], rest[-11:]
+    q_ref, k_ref, v_ref, lse_ref, att_ref, hid_ref, n2_ref, n1_ref, wq_held, wo_held, sems = outs
+    copies = start_copies([(wq_ref, wq_held), (wo_ref, wo_held)], sems)
+    tokens_ref = blocks[0]
     rows = tokens_ref.shape[0]
     seq_len = rows * len(blocks)
-    normed = jnp.concatenate([b[...] for b in blocks], axis=0)
+    for n, b in enumerate(blocks):
+        n1_ref[n * rows : (n + 1) * rows, :] = norm_forward(
+            b[...].astype(jnp.float32), gain_one_ref[...]
+        )[0].astype(jnp.bfloat16)
+    normed = n1_ref[...]
     cosine, sine = cos_ref[...], sin_ref[...]
     keys = dot(normed, wk_ref[...])
     values = dot(normed, wv_ref[...])
@@ -118,9 +123,11 @@
         v_ref[2 * c] = first.astype(jnp.bfloat16)
         v_ref[2 * c + 1] = second.astype(jnp.bfloat16)
     allowed = allowed_mask(info_ref, seq_len, rows)
+    wait_all(copies[:1])
+    query_pre = dot(n1_ref[:rows, :], wq_held[...])
     for h in range(KV):
         cols = slice(h * LANES, (h + 1) * LANES)
-        query = rope(query_ref[:, cols], cosine[:rows], sine[:rows]) * (1.0 / math.sqrt(HD))
+        query = rope(query_pre[:, cols], cosine[:rows], sine[:rows]) * (1.0 / math.sqrt(HD))
         q_ref[:, cols] = query.astype(jnp.bfloat16)
         stacked = stack_heads(query).astype(jnp.bfloat16)
         scores = jnp.where(allowed, dot(k_ref[h], stacked, 1, 1), masked_score)
@@ -130,10 +137,10 @@
         lse_ref[h : h + 1, :] = row_max + jnp.log(total)
         prob = (exps * (1.0 / total)).astype(jnp.bfloat16)
         att_ref[:, cols] = join_heads(dot(prob, v_ref[h], 0, 0)).astype(jnp.bfloat16)
-    wait_all(wo_copy)
+    wait_all(copies[1:])
     hidden = tokens_ref[...].astype(jnp.float32) + dot(att_ref[...], wo_held[...])
     hid_ref[...] = hidden
-    n2_ref[...] = norm_forward(hidden, gain_ref[...])[0].astype(jnp.bfloat16)
+    n2_ref[...] = norm_forward(hidden, gain_two_ref[...])[0].astype(jnp.bfloat16)
 
 
 def start_copies(pairs, sems):
@@ -180,22 +187,24 @@
     wide_ref[:, : router_ref.shape[1]] = router_ref[...]
 
 
-def routing(routed_ref, n2_ref, router_wide, probs_ref):
-    routed = routed_ref[...].astype(jnp.float32) > 0.5
-    logits = jnp.where(routed, dot(n2_ref[...], router_wide[...]), masked_score)
+def routing(routed, logits):
+    logits = jnp.where(routed, logits, masked_score)
     exps = jnp.where(routed, jnp.exp(logits - jnp.max(logits, axis=-1, keepdims=True)), 0.0)
-    probs_ref[...] = exps / jnp.sum(exps, axis=-1, keepdims=True)
-
-
-def experts_kernel(info_ref, router_ref, wg_ref, wu_ref, wd_ref, *rest, n_blocks, tiles):
-    n2_blocks, cot_blocks = rest[:n_blocks], rest[n_blocks : 2 * n_blocks]
-    sums_out, gu_out, scaled_out, extra_ref, gate_ref = rest[2 * n_blocks : 2 * n_blocks + 5]
+    return exps / jnp.sum(exps, axis=-1, keepdims=True)
+
+
+def experts_kernel(
+    info_ref, router_ref, wg_ref, wu_ref, wd_ref, *rest, n_blocks, experts, tiles
+):
+    cot_blocks, n2_blocks = rest[:n_blocks], rest[n_blocks : 2 * n_blocks]
+    sums_out, acts_out = rest[2 * n_blocks : 2 * n_blocks + 2]
     (
-        n2_ref, g_ref, routed_ref, w_ref, down_ref, gu_ref, scaled_ref, sums_ref, probs_ref,
-        router_wide,
-    ) = rest[2 * n_blocks + 5 : 2 * n_blocks + 15]
-    n2_sems, routed_sems, g_sems, w_sems, out_sems = rest[2 * n_blocks + 15 :]
+        n2_ref, g_ref, routed_ref, w_ref, down_ref, acts_ref, sums_ref, probs_ref, router_wide,
+        extra_ref,
+    ) = rest[2 * n_blocks + 2 : 2 * n_blocks + 12]
+    n2_sems, routed_sems, g_sems, w_sems, out_sems = rest[2 * n_blocks + 12 :]
     exp_dev, width, units = wg_ref.shape
+    rows = n2_blocks[0].shape[0]
     fh = units // 2
     n2_copies = start_copies(row_parts(n2_blocks, n2_ref, pl.ds(0, width)), n2_sems)
     routed_copies = start_copies(row_parts(cot_blocks, routed_ref, pl.ds(width, LANES)), routed_sems)
@@ -205,12 +214,13 @@
         return describe(pairs + down_part(info_ref, wd_ref, down_ref, e), w_sems.at[e])
 
     def results(e):
-        cols = pl.ds(pl.multiple_of(e * 3 * fh, 3 * fh), 3 * fh)
+        two = pl.ds(pl.multiple_of(e * 3 * fh, fh), 2 * fh)
+        one = pl.ds(pl.multiple_of((3 * e + 2) * fh, fh), fh)
         return describe(
             [
-                (gu_ref.at[e], gu_out.at[e]),
-                (scaled_ref.at[e], scaled_out.at[e]),
-                (sums_ref.at[e], sums_out.at[:, cols]),
+                (acts_ref.at[e], acts_out.at[e]),
+                (sums_ref.at[e, :, pl.ds(0, 2 * fh)], sums_out.at[:, two]),
+                (sums_ref.at[e, :, pl.ds(2 * fh, fh)], sums_out.at[:, one]),
             ],
             out_sems.at[e],
         )
@@ -222,8 +232,9 @@
     wait_all(n2_copies)
     wait_all(routed_copies)
     g_copies = start_copies(row_parts(cot_blocks, g_ref, pl.ds(0, width)), g_sems)
-    routing(routed_ref, n2_ref, router_wide, probs_ref)
-    gate_ref[...] = probs_ref[: gate_ref.shape[0], :]
+    probs_ref[...] = routing(
+        routed_ref[...].astype(jnp.float32) > 0.5, dot(n2_ref[...], router_wide[...])
+    )
     wait_all(g_copies)
     step = n2_ref.shape[0] // tiles
 
@@ -248,15 +259,27 @@
             weight = jnp.sum(jnp.where(here, probs_ref[part, :], 0.0), axis=1, keepdims=True)
             extra_ref[part, :] += jnp.where(here, jnp.sum(act * back, axis=1, keepdims=True), 0.0)
             grad_active = weight * back
-            scaled_ref[e, part, :] = (weight * act).astype(jnp.bfloat16)
-            gu_ref[e, part, :fh] = (
+            acts_ref[e, part, :fh] = (
                 grad_active * up_pre * (sig + silu * (1.0 - sig))
             ).astype(jnp.bfloat16)
-            gu_ref[e, part, fh:] = (grad_active * silu).astype(jnp.bfloat16)
-        sums_ref[e, :, : 2 * fh] = dot(n2_ref[...], gu_ref[e], 0, 0).astype(jnp.bfloat16)
-        sums_ref[e, :, 2 * fh :] = dot(g_ref[...], scaled_ref[e], 0, 0).astype(jnp.bfloat16)
-        for c in results(e):
-            c.start()
+            acts_ref[e, part, fh : 2 * fh] = (grad_active * silu).astype(jnp.bfloat16)
+            acts_ref[e, part, 2 * fh : 3 * fh] = (weight * act).astype(jnp.bfloat16)
+            found = extra_ref[part, :]
+            high = found.astype(jnp.bfloat16).astype(jnp.float32)
+            lower = (found - high).astype(jnp.bfloat16).astype(jnp.float32)
+            acts_ref[e, part, 3 * fh :] = (high + pltpu.roll(lower, experts, 1)).astype(
+                jnp.bfloat16
+            )
+        leaving = results(e)
+        leaving[0].start()
+        sums_ref[e, :, : 2 * fh] = dot(n2_ref[...], acts_ref[e, :, : 2 * fh], 0, 0).astype(
+            jnp.bfloat16
+        )
+        leaving[1].start()
+        sums_ref[e, :, 2 * fh :] = dot(g_ref[...], acts_ref[e, :, 2 * fh : 3 * fh], 0, 0).astype(
+            jnp.bfloat16
+        )
+        leaving[2].start()
         return carry
 
     lax.fori_loop(0, exp_dev, one_expert, 0)
@@ -274,23 +297,24 @@
 
 
 def rows_kernel(
-    info_ref, extra_ref, wg_ref, wu_ref, gu_in, odd_out, even_out, w_ref, gu_ref, total_ref,
-    odd_ref, even_ref, w_sems, out_sems, *, experts
+    info_ref, wg_ref, wu_ref, acts_in, odd_out, even_out, w_ref, gu_ref, total_ref, extra_ref,
+    odd_ref, even_ref, w_sems, out_sems, extra_sems
 ):
     exp_dev, width, _ = wg_ref.shape
-    all_rows = gu_ref.shape[1]
+    all_rows, two = gu_ref.shape[1:]
+    extra_part = pl.ds(3 * two // 2, LANES)
+    extra_copy = start_copies([(acts_in.at[exp_dev - 1, :, extra_part], extra_ref)], extra_sems)
 
     def operands(e):
         pairs = expert_parts(info_ref, wg_ref, wu_ref, w_ref, e)
-        return describe(pairs + [(gu_in.at[e], gu_ref.at[e])], w_sems.at[e])
+        acts = acts_in.at[e, :, pl.ds(0, two)]
+        return describe(pairs + [(acts, gu_ref.at[e])], w_sems.at[e])
 
     for c in operands(0):
         c.start()
-    found = extra_ref[...]
-    high = found.astype(jnp.bfloat16).astype(jnp.float32)
-    lower = (found - high).astype(jnp.bfloat16).astype(jnp.float32)
+    wait_all(extra_copy)
     put_rows(
-        high + pltpu.roll(lower, experts, 1), 0, odd_ref, even_ref, slice(width, width + LANES)
+        extra_ref[...].astype(jnp.float32), 0, odd_ref, even_ref, slice(width, width + LANES)
     )
     total_ref[...] = jnp.zeros_like(total_ref)
 
@@ -387,16 +411,16 @@
 
 
 def early_dense_kernel(info_ref, *rest, groups, count):
-    normed, attended, branch, query = (rest[n * groups : (n + 1) * groups] for n in range(4))
-    odd_ref, even_ref, normed_t_ref, select_ref = rest[4 * groups :]
-    rows, width = normed[0].shape
+    attended, branch, query = (rest[1 + n * groups : 1 + (n + 1) * groups] for n in range(3))
+    odd_ref, even_ref, normed_t_ref, select_ref = rest[1 + 3 * groups :]
+    rows, width = attended[0].shape
     selection(info_ref, select_ref, odd_ref.shape[1])
     select = select_ref[...]
 
     def seq(blocks):
         return jnp.concatenate([b[:rows] for b in blocks], axis=0)
 
-    normed_t = dot(select, seq(normed), 1, 1).astype(jnp.bfloat16)
+    normed_t = dot(select, rest[0][...], 1, 1).astype(jnp.bfloat16)
     normed_t_ref[...] = normed_t
     attended_t = dot(select, seq(attended), 1, 1).astype(jnp.bfloat16)
     put_shares(dot(attended_t, seq(branch)), odd_ref, even_ref, 0)
@@ -426,8 +450,8 @@
 
 
 def backward_kernel(
-    info_ref, own_ref, gate_ref, cot_ref, n2_ref, hid_ref, router_ref, gain_ref, wo_ref, q_ref,
-    lse_ref, cos_ref, sin_ref, k_hbm, v_hbm, wq_hbm, scaled_hbm, wd_hbm, *rest, experts
+    info_ref, own_ref, cot_ref, n2_ref, hid_ref, router_ref, gain_ref, wo_ref, q_ref,
+    lse_ref, cos_ref, sin_ref, k_hbm, v_hbm, wq_hbm, acts_hbm, wd_hbm, *rest, experts
 ):
     arrived, outs = rest[:-18], rest[-18:]
     ghid_ref, branch_ref, dq_ref, odd_ref, even_ref, gn_ref, mix_odd_out, mix_even_out = outs[:8]
@@ -442,7 +466,7 @@
     for e in range(exp_dev):
         part = pl.ds(e * fh, fh)
         pairs += [(wd_hbm.at[e, own_half(info_ref, fh), :], down_ref.at[part, :])]
-        pairs += [(scaled_hbm.at[e], scaled_ref.at[:, part])]
+        pairs += [(acts_hbm.at[e, :, pl.ds(2 * fh, fh)], scaled_ref.at[:, part])]
     mix_copies = start_copies(pairs, mix_sems)
     widen(router_ref, router_wide)
     rows, width = hid_ref.shape
@@ -451,7 +475,8 @@
         summed = summed + a[...].astype(jnp.float32)
     extra = summed[:, width:]
     gate_grads = extra + pltpu.roll(extra, LANES - experts, 1)
-    gate = gate_ref[...]
+    routed = cot_ref[:, width:].astype(jnp.float32) > 0.5
+    gate = routing(routed, dot(n2_ref[...], router_wide[...]))
     grad_logits = (
         gate * (gate_grads - jnp.sum(gate * gate_grads, axis=-1, keepdims=True))
     ).astype(jnp.bfloat16)
@@ -460,7 +485,7 @@
     hidden = hid_ref[...]
     inverse = lax.rsqrt(jnp.mean(hidden * hidden, axis=-1, keepdims=True) + norm_eps)
     back, norm_grad = norm_backward(hidden, inverse, gain_ref[...], grad_normed)
-    grad_hidden = cot_ref[...].astype(jnp.float32) + back
+    grad_hidden = cot_ref[:, :width].astype(jnp.float32) + back
     ghid_ref[...] = grad_hidden
     branch = grad_hidden.astype(jnp.bfloat16)
     branch_ref[:rows] = branch
@@ -539,7 +564,7 @@
     out_ref[...] = (ghid_ref[...] + back).astype(jnp.bfloat16)
 
 
-def call(kernel, out_shape, name, hbm=(), hbm_out=(), scratch=(), smem=True):
+def call(kernel, out_shape, name, hbm=(), hbm_out=(), scratch=(), smem=True, limit=LIMIT_MIB):
     def run(*args):
         specs = [
             pl.BlockSpec(memory_space=pl.ANY if n in hbm else pltpu.VMEM)
@@ -556,7 +581,7 @@
                 for n in range(len(out_shape))
             ],
             scratch_shapes=list(scratch),
-            compiler_params=pltpu.CompilerParams(vmem_limit_bytes=LIMIT_MIB * 1024 * 1024),
+            compiler_params=pltpu.CompilerParams(vmem_limit_bytes=limit * 1024 * 1024),
             name=name,
         )(*args)
 
@@ -630,26 +655,23 @@
         spots = [(s, r) for s in range(pairs) for r in range(0, groups, 2)]
         return [send(mine[n], *spots[n]) for n in range(1, len(spots))]
 
-    tokens_f = tokens.astype(f32)
-    normed1 = norm_forward(tokens_f, norm1_gain)[0].astype(low)
-    normed1_even = gather_even(normed1, 1)
+    tokens_even = gather_even(tokens, 1)
     cosine, sine = rope_tables(me, tok_rows, groups)
-    cosine, sine, *normed1_even = lax.optimization_barrier((cosine, sine, *normed1_even))
-    normed1_blocks = gather_odd(normed1_even)
+    cosine, sine, *tokens_even = lax.optimization_barrier((cosine, sine, *tokens_even))
+    tokens_blocks = gather_odd(tokens_even)
     routed = jnp.any(
         routes[:, :, None] == jnp.arange(experts, dtype=jnp.int32)[None, None, :], axis=1
     )
     cot_mask = jnp.concatenate(
         [cotangent, jnp.pad(routed.astype(low), ((0, 0), (0, LANES - experts)))], axis=1
     )
-    cot_mask, *normed1_even = lax.optimization_barrier((cot_mask, *normed1_even))
+    cot_mask, *tokens_even = lax.optimization_barrier((cot_mask, *tokens_even))
     cot_even = gather_even(cot_mask, 2)
     my_dp = lax.axis_index("dp")
     info = jnp.stack([me, prefix_len[0], half, my_dp]).astype(jnp.int32)
     gain_one, gain_two = norm1_gain[None], norm2_gain[None]
 
-    query_pre = dot(normed1, w_query)
-    q_low, k_two, v_two, lse, attended, hidden_state, normed2 = call(
+    q_low, k_two, v_two, lse, attended, hidden_state, normed2, normed1_all = call(
         forward_kernel,
         (
             shape(tok_rows, H * HD),
@@ -659,13 +681,17 @@
             shape(tok_rows, H * HD),
             shape(tok_rows, model_width, dtype=f32),
             shape(tok_rows, model_width),
+            shape(seq_len, model_width),
         ),
         "attention_forward",
-        hbm=(5,),
-        scratch=(pltpu.VMEM((H * HD, model_width), low), pltpu.SemaphoreType.DMA((1,))),
+        hbm=(1, 4),
+        scratch=(
+            pltpu.VMEM((model_width, H * HD), low),
+            pltpu.VMEM((H * HD, model_width), low),
+            pltpu.SemaphoreType.DMA((2,)),
+        ),
     )(
-        info, tokens, query_pre, w_key, w_value, w_output, gain_two, cosine, sine,
-        *normed1_blocks,
+        info, w_query, w_key, w_value, w_output, gain_one, gain_two, cosine, sine, *tokens_blocks,
     )
 
     normed2, *cot_even = lax.optimization_barrier((normed2, *cot_even))
@@ -678,36 +704,35 @@
 
     dma = pltpu.SemaphoreType.DMA
     units = half_units * exp_dev
-    sums, grad_gu, scaled, extra, gate_probs = call(
-        lambda *refs: experts_kernel(*refs, n_blocks=n_blocks, tiles=2),
+    wide_acts = 3 * half_units + LANES
+    sums, acts = call(
+        lambda *refs: experts_kernel(*refs, n_blocks=n_blocks, experts=experts, tiles=2),
         (
             shape(model_width, 3 * units),
-            shape(exp_dev, all_rows, 2 * half_units),
-            shape(exp_dev, all_rows, half_units),
-            shape(all_rows, LANES, dtype=f32),
-            shape(tok_rows, LANES, dtype=f32),
+            shape(exp_dev, all_rows, wide_acts),
         ),
         "experts",
+        limit=48 if all_rows <= 1024 else LIMIT_MIB,
         hbm=tuple(range(2, 5 + 2 * n_blocks)),
-        hbm_out=(0, 1, 2),
+        hbm_out=(0, 1),
         scratch=(
             pltpu.VMEM((all_rows, model_width), low),
             pltpu.VMEM((all_rows, model_width), low),
             pltpu.VMEM((all_rows, LANES), low),
             pltpu.VMEM((exp_dev, model_width, 2 * half_units), low),
             pltpu.VMEM((exp_dev, half_units, model_width), low),
-            pltpu.VMEM((exp_dev, all_rows, 2 * half_units), low),
-            pltpu.VMEM((exp_dev, all_rows, half_units), low),
+            pltpu.VMEM((exp_dev, all_rows, wide_acts), low),
             pltpu.VMEM((exp_dev, model_width, 3 * half_units), low),
             pltpu.VMEM((all_rows, LANES), f32),
             pltpu.VMEM((model_width, LANES), low),
+            pltpu.VMEM((all_rows, LANES), f32),
             dma((n_blocks,)),
             dma((n_blocks,)),
             dma((n_blocks,)),
             dma((exp_dev, 3)),
             dma((exp_dev, 3)),
         ),
-    )(info, w_router, w_gate, w_up, w_down, *n2_blocks, *cot_blocks)
+    )(info, w_router, w_gate, w_up, w_down, *cot_blocks, *n2_blocks)
     outer = copies // 2
     shard_rows = model_width // copies
     reduced = lax.psum_scatter(
@@ -719,21 +744,23 @@
     )
 
     odd, even = call(
-        lambda *refs: rows_kernel(*refs, experts=experts),
+        rows_kernel,
         (shape(groups, tok_rows, wide), shape(groups, tok_rows, wide, dtype=f32)),
         "experts_rows",
-        hbm=(2, 3, 4),
+        hbm=(1, 2, 3),
         hbm_out=(0, 1),
         scratch=(
             pltpu.VMEM((exp_dev, model_width, 2 * half_units), low),
             pltpu.VMEM((exp_dev, all_rows, 2 * half_units), low),
             pltpu.VMEM((all_rows, model_width), f32),
+            pltpu.VMEM((all_rows, LANES), low),
             pltpu.VMEM((groups, tok_rows, wide), low),
             pltpu.VMEM((groups, tok_rows, wide), f32),
             dma((exp_dev, 3)),
             dma((4,)),
-        ),
-    )(info, extra, w_gate, w_up, grad_gu)
+            dma((1,)),
+        ),
+    )(info, w_gate, w_up, acts)
     odd, *attended_even = lax.optimization_barrier((odd, *attended_even))
     mine = core_sum(odd, even)
     arrived = swap(mine, 2)
@@ -754,7 +781,7 @@
             shape(groups, tok_rows, model_width, dtype=f32),
         ),
         "attention_backward",
-        hbm=(13, 14, 15, 16, 17),
+        hbm=(12, 13, 14, 15, 16),
         hbm_out=(6, 7),
         scratch=(
             pltpu.VMEM((model_width, LANES), low),
@@ -769,8 +796,8 @@
             dma((2 * exp_dev,)),
         ),
     )(
-        info, mine[0], gate_probs, cotangent, normed2, hidden_state, w_router, gain_two, w_output,
-        q_low, lse, cosine, sine, k_two, v_two, w_query, scaled, w_down, *arrived,
+        info, mine[0], cot_mask, normed2, hidden_state, w_router, gain_two, w_output,
+        q_low, lse, cosine, sine, k_two, v_two, w_query, acts, w_down, *arrived,
     )
     kv_mine = core_sum(kv_odd, kv_even)
     kv_arrived = swap(kv_mine, 1)
@@ -817,7 +844,7 @@
         ),
         "dense_early",
         scratch=(select,),
-    )(info, *normed1_blocks, *attended_blocks, *branch_blocks, *query_blocks)
+    )(info, normed1_all, *attended_blocks, *branch_blocks, *query_blocks)
     early = early_even + send(early_odd, 1, 0).astype(f32)
     late_odd, late_even = call(
         late_dense_kernel,

time: 224 us -> 220 us (0.982)
  waiting for transfers between devices: 67.9 us -> 72.2 us
  matrix products: 2.83 us -> 0 us
    ppermute x44, waiting for transfers between devices: 67 us -> 70.4 us  [send(): lax.ppermute(block, ('dp', 'expert'), [(i * groups + j, (i ^ pair_flip) *...]
    dot_general x1 -> x0, matrix products: 2.83 us -> none  [dot(): lax.dot_general(left, right, (((left_dim,), (right_dim,)), ((), ())), pre...]
    unnamed x75 -> x67, local copies, waits for them, and re-layouts: 10.6 us -> 9.8 us
  transfers between devices with their start and end apart: 45 -> 45, of which waited for: 21 -> 22; matrix products, arithmetic and copies ran while one was open for 10% -> 8% of each run, Pallas kernels for 21% -> 21%
where the time goes in v1:
time: 220 us; the launch traced here: 219 us
  waiting for transfers between devices  72.2 us (33%)
  Pallas kernels  70.6 us (32%)
  starting transfers between devices  33.8 us (15%)
  between operations  15.1 us (7%)
  local copies, waits for them, and re-layouts  14 us (6%)
  other arithmetic  13.5 us (6%)
    pallas_call x8, Pallas kernels, run(): pl.pallas_call(kernel, out_shape=out_shape, in_specs=specs, out_specs=[pl...  70.6 us
    ppermute x44, waiting for transfers between devices, send(): lax.ppermute(block, ('dp', 'expert'), [(i * groups + j, (i ^ pair_flip) *...  70.4 us
    ppermute x44, starting transfers between devices, send(): lax.ppermute(block, ('dp', 'expert'), [(i * groups + j, (i ^ pair_flip) *...  33.8 us
    unnamed x67, local copies, waits for them, and re-layouts  9.8 us
  transfers between devices with their start and end apart: 45, of which 22 were waited for; matrix products, arithmetic and copies ran while one was open for 8% of the time, Pallas kernels for 21%

profile of v1, /device:TPU:0, one launch (start us, length us, event | category | flops | bytes accessed | tf_op | source)
XLA Modules:
  0.0 219.2 jit_solution(12806706386453026667)
XLA Ops:
  7.2 3.0 %collective-permute-start = (bf16[128,1024]{1,0:T(8,128)(2,1)}, bf16[128,1024]{1,0:T(8,128)(2,1)S(1)}, u32[]{:S(2)}, u32[]{:S(2)}) collective-permute-start(bf16[128,1024]{1,0:T(8,128)(2,1)} %tokens_ref.1), channel_id=1, source_target_pairs={{0,2},{1,3},{2,0},{3,1},{4,6},{5,7},{6,4},{7,5},{8,10},{9,11},{10,... | collective-permute-start | bytes 786440 | tf_op jit(solution)/shard_map/ppermute | solution.py:624
  12.1 2.6 %negate_select_fusion = (f32[512,128]{1,0:T(8,128)}, f32[512,128]{1,0:T(8,128)}) fusion(s32[128]{0:T(128)S(1)} %get-tuple-element.158, s32[128]{0:T(128)S(1)} %get-tuple-element.160, s32[128]{0:T(128)S(1)} %get-tuple-element.159, s32[128]{0:T(128)S(1)} %get-tuple-element.161, s32[512]{0:T(512)S(1)} %get-tuple-element.151, s32[512]{0:T(512)S(1)} %get-tuple-element.152, ...), kind=kLoop, calls=%fused_computation.17 | loop fusion | flops 917504 | bytes 535812 | tf_op jit(solution)/shard_map/jit(_where)/select_n | solution.py:26
  14.8 2.0 collective-permute-done.rest_2_
  16.8 2.7 %collective-permute-start.5 = (bf16[128,1152]{1,0:T(8,128)(2,1)S(1)}, bf16[128,1152]{1,0:T(8,128)(2,1)S(1)}, u32[]{:S(2)}, u32[]{:S(2)}) collective-permute-start(bf16[128,1152]{1,0:T(8,128)(2,1)S(1)} %pad_maximum_fusion.1.refs_5_.refs_2_), channel_id=1, source_target_pairs={{0,6},{1,7},{2,4},{3,5},{4,2},{5,3},{6,0},{7,1},{8,14},{9,15},{10,... | collective-permute-start | bytes 884744 | tf_op jit(solution)/shard_map/ppermute | solution.py:624
  23.2 8.7 %attention_forward.1 = (bf16[128,1024]{1,0:T(8,128)(2,1)}, bf16[8,512,128]{2,1,0:T(8,128)(2,1)}, bf16[8,512,128]{2,1,0:T(8,128)(2,1)}, f32[8,256]{1,0:T(8,128)},...) custom-call(s32[4]{0:T(128)} %pad_add_fusion.info_ref.refs_0_, ...), custom_call_target="tpu_custom_call" | custom-call | tf_op jit(solution)/shard_map/attention_forward/pallas_call | solution.py:575
  32.3 2.3 %collective-permute-start.15 = (bf16[128,1024]{1,0:T(8,128)(2,1)}, bf16[128,1024]{1,0:T(8,128)(2,1)S(1)}, u32[]{:S(2)}, u32[]{:S(2)}) collective-permute-start(bf16[128,1024]{1,0:T(8,128)(2,1)} %get-tuple-element.87.refs_13_.refs_3_), channel_id=1, source_target_pairs={{0,6},{1,7},{2,4},{3,5},{4,2},{5,3},{6,0},{7,1},{8,14},{9,15},{10,... | collective-permute-start | bytes 786440 | tf_op jit(solution)/shard_map/ppermute | solution.py:624
  36.3 6.3 %collective-permute-done.15.refs_19_ = bf16[128,1024]{1,0:T(8,128)(2,1)S(1)} collective-permute-done((bf16[128,1024]{1,0:T(8,128)(2,1)}, bf16[128,1024]{1,0:T(8,128)(2,1)S(1)}, u32[]{:S(2)}, u32[]{:S(2)}) %collective-permute-start.15) | collective-permute-done | bytes 262176 | tf_op jit(solution)/shard_map/ppermute | solution.py:624
  42.6 4.7 %collective-permute-done.13.refs_17_ = bf16[128,1024]{1,0:T(8,128)(2,1)S(1)} collective-permute-done((bf16[128,1024]{1,0:T(8,128)(2,1)}, bf16[128,1024]{1,0:T(8,128)(2,1)S(1)}, u32[]{:S(2)}, u32[]{:S(2)}) %collective-permute-start.13) | collective-permute-done | bytes 262176 | tf_op jit(solution)/shard_map/ppermute | solution.py:624
  51.5 19.5 %experts.1 = (bf16[1024,3072]{1,0:T(8,128)(2,1)}, bf16[4,1024,896]{2,1,0:T(8,128)(2,1)}) custom-call(s32[4]{0:T(128)S(1)} %copy-done.3, bf16[1024,16]{1,0:T(8,128)(2,1)S(1)} %copy.30.refs_1_.refs_5_, bf16[4,1024,512]{2,1,0:T(8,128)(2,1)} %wg_ref.1, bf16[4,1024,512]{2,1,0:T(8,128)(2,1)} %wu_ref.1, bf16[4,512,1024]{2,1,0:T(8,128)(2,1)} %refs_16_.1, ...), custom_call_target="tpu_custom_call" | custom-call | tf_op jit(solution)/shard_map/experts/pallas_call | solution.py:575
  73.0 10.4 %experts_rows.1 = (bf16[4,128,1152]{2,1,0:T(8,128)(2,1)}, f32[4,128,1152]{2,1,0:T(8,128)}) custom-call(s32[4]{0:T(128)} %pad_add_fusion.info_ref.refs_0_, bf16[4,1024,512]{2,1,0:T(8,128)(2,1)} %wg_ref.1, bf16[4,1024,512]{2,1,0:T(8,128)(2,1)} %wu_ref.1, bf16[4,1024,896]{2,1,0:T(8,128)(2,1)} %get-tuple-element.88.acts_in.refs_15_), custom_call_target="tpu_custom_call" | custom-call | tf_op jit(solution)/shard_map/experts_rows/pallas_call | solution.py:575
  83.6 3.0 %collective-permute-done.18 = bf16[4,128,1152]{2,1,0:T(8,128)(2,1)S(1)} collective-permute-done((bf16[4,128,1152]{2,1,0:T(8,128)(2,1)}, bf16[4,128,1152]{2,1,0:T(8,128)(2,1)S(1)}, u32[]{:S(2)}, u32[]{:S(2)}) %collective-permute-start.18) | collective-permute-done | bytes 1179680 | tf_op jit(solution)/shard_map/ppermute | solution.py:624
  86.6 2.0 fusion.12
  88.7 1.9 collective-permute-start.21
  93.2 6.4 %collective-permute-done.21.refs_19_ = bf16[128,1152]{1,0:T(8,128)(2,1)S(1)} collective-permute-done((bf16[128,1152]{1,0:T(8,128)(2,1)S(1)}, bf16[128,1152]{1,0:T(8,128)(2,1)S(1)}, u32[]{:S(2)}, u32[]{:S(2)}) %collective-permute-start.21) | collective-permute-done | bytes 294944 | tf_op jit(solution)/shard_map/ppermute | solution.py:624
  99.6 5.0 %collective-permute-done.20.refs_18_ = bf16[128,1152]{1,0:T(8,128)(2,1)S(1)} collective-permute-done((bf16[128,1152]{1,0:T(8,128)(2,1)S(1)}, bf16[128,1152]{1,0:T(8,128)(2,1)S(1)}, u32[]{:S(2)}, u32[]{:S(2)}) %collective-permute-start.20) | collective-permute-done | bytes 294944 | tf_op jit(solution)/shard_map/ppermute | solution.py:624
  105.8 15.6 %attention_backward.1 = (f32[128,1024]{1,0:T(8,128)}, bf16[176,1024]{1,0:T(8,128)(2,1)}, bf16[128,1024]{1,0:T(8,128)(2,1)}, bf16[2,128,1024]{2,1,0:T(8,128)(2,1)...) custom-call(s32[4]{0:T(128)} %pad_add_fusion.info_ref.refs_0_, ...), custom_call_target="tpu_custom_call" | custom-call | tf_op jit(solution)/shard_map/attention_backward/pallas_call | solution.py:575
  121.5 2.0 collective-permute-done.22
  126.6 7.2 %collective-permute-done.25.rest_0_ = bf16[128,1024]{1,0:T(8,128)(2,1)S(1)} collective-permute-done((bf16[128,1024]{1,0:T(8,128)(2,1)S(1)}, bf16[128,1024]{1,0:T(8,128)(2,1)S(1)}, u32[]{:S(2)}, u32[]{:S(2)}) %collective-permute-start.25) | collective-permute-done | bytes 262176 | tf_op jit(solution)/shard_map/ppermute | solution.py:624
  140.8 4.0 %tokens_backward.1 = (bf16[144,1024]{1,0:T(8,128)(2,1)}, bf16[128,1024]{1,0:T(8,128)(2,1)}) custom-call(f32[128,1024]{1,0:T(8,128)} %slice_bitcast_fusion.1.own_ref, f32[128,1024]{1,0:T(8,128)} %get-tuple-element.103.gn_ref, bf16[1024,512]{1,0:T(8,128)(2,1)} %wk_ref.3, bf16[1024,512]{1,0:T(8,128)(2,1)} %wv_ref.3, bf16[128,1024]{1,0:T(8,128)(2,1)} %tokens_ref.1, ...), custom_call_target="tpu_custom_call" | custom-call | tf_op jit(solution)/shard_map/tokens_backward/pallas_call | solution.py:575
  144.9 4.8 %collective-permute-done.26.refs_8_ = bf16[176,1024]{1,0:T(8,128)(2,1)S(1)} collective-permute-done((bf16[176,1024]{1,0:T(8,128)(2,1)S(1)}, bf16[176,1024]{1,0:T(8,128)(2,1)S(1)}, u32[]{:S(2)}, u32[]{:S(2)}) %collective-permute-start.26) | collective-permute-done | bytes 360480 | tf_op jit(solution)/shard_map/ppermute | solution.py:624
  150.7 1.6 collective-permute-done.35.refs_11_
  154.7 5.1 %dense_early.1 = (bf16[4,32,2176]{2,1,0:T(8,128)(2,1)}, f32[4,32,2176]{2,1,0:T(8,128)}, bf16[256,512]{1,0:T(8,128)(2,1)}) custom-call(s32[4]{0:T(128)} %pad_add_fusion.info_ref.refs_0_, bf16[512,1024]{1,0:T(8,128)(2,1)} %get-tuple-element.115.refs_1_, bf16[128,1024]{1,0:T(8,128)(2,1)} %get-tuple-element.116.refs_2_, ...), custom_call_target="tpu_custom_call" | custom-call | tf_op jit(solution)/shard_map/dense_early/pallas_call | solution.py:575
  159.8 1.6 collective-permute-start.37
  161.4 2.5 %slice_add_fusion = f32[2,128,1024]{2,1,0:T(8,128)} fusion(f32[4,128,1024]{2,1,0:T(8,128)} %copy-done.4, bf16[2,128,1024]{2,1,0:T(8,128)(2,1)} %collective-permute-done.24), kind=kLoop, calls=%fused_computation.4 | loop fusion | flops 524288 | bytes 2621440 | tf_op jit(solution)/shard_map/add | solution.py:806
  166.9 2.9 %dense_late.1 = (bf16[4,32,1152]{2,1,0:T(8,128)(2,1)}, f32[4,32,1152]{2,1,0:T(8,128)}) custom-call(s32[4]{0:T(128)} %pad_add_fusion.info_ref.refs_0_, bf16[256,512]{1,0:T(8,128)(2,1)} %get-tuple-element.124.normed_t_ref, bf16[144,1024]{1,0:T(8,128)(2,1)} %get-tuple-element.125.rest_0_, bf16[144,1024]{1,0:T(8,128)(2,1)} %copy-done.16, ...), custom_call_target="tpu_custom_call" | custom-call | tf_op jit(solution)/shard_map/dense_late/pallas_call | solution.py:575
  170.5 5.2 %collective-permute-done.37 = bf16[4,32,2176]{2,1,0:T(8,128)(2,1)S(1)} collective-permute-done((bf16[4,32,2176]{2,1,0:T(8,128)(2,1)}, bf16[4,32,2176]{2,1,0:T(8,128)(2,1)S(1)}, u32[]{:S(2)}, u32[]{:S(2)}) %collective-permute-start.37) | collective-permute-done | bytes 557088 | tf_op jit(solution)/shard_map/ppermute | solution.py:624
  181.0 1.7 reduce-scatter.2.cloned.1.call-done.refs_1_
  183.9 1.6 collective-permute-start.30
  185.5 2.9 %collective-permute-start.43 = (bf16[32,3328]{1,0:T(8,128)(2,1)S(1)}, bf16[32,3328]{1,0:T(8,128)(2,1)S(1)}, u32[]{:S(2)}, u32[]{:S(2)}) collective-permute-start(bf16[32,3328]{1,0:T(8,128)(2,1)S(1)} %get-tuple-element.145), channel_id=1, source_target_pairs={{0,24},{1,25},{2,26},{3,27},{4,28},{5,29},{6,30},{7,31},{8,16},{9,... | collective-permute-start | bytes 638984 | tf_op jit(solution)/shard_map/ppermute | solution.py:624
  190.8 4.9 %collective-permute-done.43.refs_7_ = bf16[32,3328]{1,0:T(8,128)(2,1)S(1)} collective-permute-done((bf16[32,3328]{1,0:T(8,128)(2,1)S(1)}, bf16[32,3328]{1,0:T(8,128)(2,1)S(1)}, u32[]{:S(2)}, u32[]{:S(2)}) %collective-permute-start.43) | collective-permute-done | bytes 213024 | tf_op jit(solution)/shard_map/ppermute | solution.py:624
  195.7 11.6 %collective-permute-done.42.refs_6_ = bf16[32,3328]{1,0:T(8,128)(2,1)S(1)} collective-permute-done((bf16[32,3328]{1,0:T(8,128)(2,1)S(1)}, bf16[32,3328]{1,0:T(8,128)(2,1)S(1)}, u32[]{:S(2)}, u32[]{:S(2)}) %collective-permute-start.42) | collective-permute-done | bytes 213024 | tf_op jit(solution)/shard_map/ppermute | solution.py:624
  208.0 4.4 %place.1 = (f32[4,128,512]{2,1,0:T(8,128)}, f32[4,128,512]{2,1,0:T(8,128)}, f32[4,512,128]{2,1,0:T(8,128)}, f32[32,1024]{1,0:T(8,128)}, f32[32,512]{1,0:T(8,128)...) custom-call(s32[4]{0:T(128)} %pad_add_fusion.info_ref.refs_0_, ...), custom_call_target="tpu_custom_call" | custom-call | tf_op jit(solution)/shard_map/place/pallas_call | solution.py:575
  (164 shorter events, 44.0 us)
Async XLA Ops:
  7.2 175.6 %reduce-scatter.2.cloned.1.call-start = ((), (), s32[]{:S(2)}) async-start(), calls=%async_computation.1 | async-start | bytes 7864320 | tf_op jit(solution)/shard_map/reduce_scatter | solution.py:738
  7.2 9.6 %collective-permute-start = (bf16[128,1024]{1,0:T(8,128)(2,1)}, bf16[128,1024]{1,0:T(8,128)(2,1)S(1)}, u32[]{:S(2)}, u32[]{:S(2)}) collective-permute-start(bf16[128,1024]{1,0:T(8,128)(2,1)} %tokens_ref.1), channel_id=1, source_target_pairs={{0,2},{1,3},{2,0},{3,1},{4,6},{5,7},{6,4},{7,5},{8,10},{9,11},{10,... | collective-permute-start | bytes 786440 | tf_op jit(solution)/shard_map/ppermute | solution.py:624
  16.8 15.1 %collective-permute-start.5 = (bf16[128,1152]{1,0:T(8,128)(2,1)S(1)}, bf16[128,1152]{1,0:T(8,128)(2,1)S(1)}, u32[]{:S(2)}, u32[]{:S(2)}) collective-permute-start(bf16[128,1152]{1,0:T(8,128)(2,1)S(1)} %pad_maximum_fusion.1.refs_5_.refs_2_), channel_id=1, source_target_pairs={{0,6},{1,7},{2,4},{3,5},{4,2},{5,3},{6,0},{7,1},{8,14},{9,15},{10,... | collective-permute-start | bytes 884744 | tf_op jit(solution)/shard_map/ppermute | solution.py:624
  19.4 12.9 %collective-permute-start.4 = (bf16[128,1152]{1,0:T(8,128)(2,1)S(1)}, bf16[128,1152]{1,0:T(8,128)(2,1)}, u32[]{:S(2)}, u32[]{:S(2)}) collective-permute-start(bf16[128,1152]{1,0:T(8,128)(2,1)S(1)} %pad_maximum_fusion.1.refs_5_.refs_2_), channel_id=1, source_target_pairs={{0,4},{1,5},{2,6},{3,7},{4,0},{5,1},{6,2},{7,3},{8,12},{9,13},{10,... | collective-permute-start | bytes 884744 | tf_op jit(solution)/shard_map/ppermute | solution.py:624
  20.0 12.3 %collective-permute-start.3 = (bf16[128,1152]{1,0:T(8,128)(2,1)S(1)}, bf16[128,1152]{1,0:T(8,128)(2,1)}, u32[]{:S(2)}, u32[]{:S(2)}) collective-permute-start(bf16[128,1152]{1,0:T(8,128)(2,1)S(1)} %pad_maximum_fusion.1.refs_5_.refs_2_), channel_id=1, source_target_pairs={{0,2},{1,3},{2,0},{3,1},{4,6},{5,7},{6,4},{7,5},{8,10},{9,11},{10,... | collective-permute-start | bytes 884744 | tf_op jit(solution)/shard_map/ppermute | solution.py:624
  32.3 10.3 %collective-permute-start.15 = (bf16[128,1024]{1,0:T(8,128)(2,1)}, bf16[128,1024]{1,0:T(8,128)(2,1)S(1)}, u32[]{:S(2)}, u32[]{:S(2)}) collective-permute-start(bf16[128,1024]{1,0:T(8,128)(2,1)} %get-tuple-element.87.refs_13_.refs_3_), channel_id=1, source_target_pairs={{0,6},{1,7},{2,4},{3,5},{4,2},{5,3},{6,0},{7,1},{8,14},{9,15},{10,... | collective-permute-start | bytes 786440 | tf_op jit(solution)/shard_map/ppermute | solution.py:624
  34.6 12.7 %collective-permute-start.13 = (bf16[128,1024]{1,0:T(8,128)(2,1)}, bf16[128,1024]{1,0:T(8,128)(2,1)S(1)}, u32[]{:S(2)}, u32[]{:S(2)}) collective-permute-start(bf16[128,1024]{1,0:T(8,128)(2,1)} %get-tuple-element.87.refs_13_.refs_3_), channel_id=1, source_target_pairs={{0,4},{1,5},{2,6},{3,7},{4,0},{5,1},{6,2},{7,3},{8,12},{9,13},{10,... | collective-permute-start | bytes 786440 | tf_op jit(solution)/shard_map/ppermute | solution.py:624
  35.2 12.2 %collective-permute-start.11 = (bf16[128,1024]{1,0:T(8,128)(2,1)}, bf16[128,1024]{1,0:T(8,128)(2,1)S(1)}, u32[]{:S(2)}, u32[]{:S(2)}) collective-permute-start(bf16[128,1024]{1,0:T(8,128)(2,1)} %get-tuple-element.87.refs_13_.refs_3_), channel_id=1, source_target_pairs={{0,2},{1,3},{2,0},{3,1},{4,6},{5,7},{6,4},{7,5},{8,10},{9,11},{10,... | collective-permute-start | bytes 786440 | tf_op jit(solution)/shard_map/ppermute | solution.py:624
  35.8 12.1 %collective-permute-start.6 = (bf16[128,1152]{1,0:T(8,128)(2,1)S(1)}, bf16[128,1152]{1,0:T(8,128)(2,1)S(1)}, u32[]{:S(2)}, u32[]{:S(2)}) collective-permute-start(bf16[128,1152]{1,0:T(8,128)(2,1)S(1)} %pad_maximum_fusion.1.refs_5_.refs_2_), channel_id=1, source_target_pairs={{0,1},{1,0},{2,3},{3,2},{4,5},{5,4},{6,7},{7,6},{8,9},{9,8},{10,11... | collective-permute-start | bytes 884744 | tf_op jit(solution)/shard_map/ppermute | solution.py:624
  35.8 12.6 %collective-permute-start.7 = (bf16[128,1152]{1,0:T(8,128)(2,1)}, bf16[128,1152]{1,0:T(8,128)(2,1)S(1)}, u32[]{:S(2)}, u32[]{:S(2)}) collective-permute-start(bf16[128,1152]{1,0:T(8,128)(2,1)} %collective-permute-done.3.refs_7_), channel_id=1, source_target_pairs={{0,1},{1,0},{2,3},{3,2},{4,5},{5,4},{6,7},{7,6},{8,9},{9,8},{10,11... | collective-permute-start | bytes 884744 | tf_op jit(solution)/shard_map/ppermute | solution.py:624
  42.6 5.2 %collective-permute-start.10 = (bf16[128,1024]{1,0:T(8,128)(2,1)}, bf16[128,1024]{1,0:T(8,128)(2,1)S(1)}, u32[]{:S(2)}, u32[]{:S(2)}) collective-permute-start(bf16[128,1024]{1,0:T(8,128)(2,1)} %get-tuple-element.87.refs_13_.refs_3_), channel_id=1, source_target_pairs={{0,1},{1,0},{2,3},{3,2},{4,5},{5,4},{6,7},{7,6},{8,9},{9,8},{10,11... | collective-permute-start | bytes 786440 | tf_op jit(solution)/shard_map/ppermute | solution.py:624
  72.0 11.4 %collective-permute-start.17 = (bf16[128,1024]{1,0:T(8,128)(2,1)S(1)}, bf16[128,1024]{1,0:T(8,128)(2,1)}, u32[]{:S(2)}, u32[]{:S(2)}) collective-permute-start(bf16[128,1024]{1,0:T(8,128)(2,1)S(1)} %copy-done.21), channel_id=1, source_target_pairs={{0,2},{1,3},{2,0},{3,1},{4,6},{5,7},{6,4},{7,5},{8,10},{9,11},{10,... | collective-permute-start | bytes 786440 | tf_op jit(solution)/shard_map/ppermute | solution.py:624
  88.7 10.9 %collective-permute-start.21 = (bf16[128,1152]{1,0:T(8,128)(2,1)S(1)}, bf16[128,1152]{1,0:T(8,128)(2,1)S(1)}, u32[]{:S(2)}, u32[]{:S(2)}) collective-permute-start(bf16[128,1152]{1,0:T(8,128)(2,1)S(1)} %get-tuple-element.142), channel_id=1, source_target_pairs={{0,6},{1,7},{2,4},{3,5},{4,2},{5,3},{6,0},{7,1},{8,14},{9,15},{10,... | collective-permute-start | bytes 884744 | tf_op jit(solution)/shard_map/ppermute | solution.py:624
  90.6 13.9 %collective-permute-start.20 = (bf16[128,1152]{1,0:T(8,128)(2,1)S(1)}, bf16[128,1152]{1,0:T(8,128)(2,1)S(1)}, u32[]{:S(2)}, u32[]{:S(2)}) collective-permute-start(bf16[128,1152]{1,0:T(8,128)(2,1)S(1)} %get-tuple-element.143), channel_id=1, source_target_pairs={{0,4},{1,5},{2,6},{3,7},{4,0},{5,1},{6,2},{7,3},{8,12},{9,13},{10,... | collective-permute-start | bytes 884744 | tf_op jit(solution)/shard_map/ppermute | solution.py:624
  91.2 13.9 %collective-permute-start.19 = (bf16[128,1152]{1,0:T(8,128)(2,1)S(1)}, bf16[128,1152]{1,0:T(8,128)(2,1)S(1)}, u32[]{:S(2)}, u32[]{:S(2)}) collective-permute-start(bf16[128,1152]{1,0:T(8,128)(2,1)S(1)} %get-tuple-element.144), channel_id=1, source_target_pairs={{0,2},{1,3},{2,0},{3,1},{4,6},{5,7},{6,4},{7,5},{8,10},{9,11},{10,... | collective-permute-start | bytes 884744 | tf_op jit(solution)/shard_map/ppermute | solution.py:624
  124.9 10.9 %collective-permute-start.23 = (bf16[4,128,1024]{2,1,0:T(8,128)(2,1)}, bf16[4,128,1024]{2,1,0:T(8,128)(2,1)S(1)}, u32[]{:S(2)}, u32[]{:S(2)}) collective-permute-start(bf16[4,128,1024]{2,1,0:T(8,128)(2,1)} %get-tuple-element.101), channel_id=1, source_target_pairs={{0,1},{1,0},{2,3},{3,2},{4,5},{5,4},{6,7},{7,6},{8,9},{9,8},{10,11... | collective-permute-start | bytes 3145736 | tf_op jit(solution)/shard_map/ppermute | solution.py:624
  125.2 8.7 %collective-permute-start.25 = (bf16[128,1024]{1,0:T(8,128)(2,1)S(1)}, bf16[128,1024]{1,0:T(8,128)(2,1)S(1)}, u32[]{:S(2)}, u32[]{:S(2)}) collective-permute-start(bf16[128,1024]{1,0:T(8,128)(2,1)S(1)} %fusion.2), channel_id=1, source_target_pairs={{0,2},{1,3},{2,0},{3,1},{4,6},{5,7},{6,4},{7,5},{8,10},{9,11},{10,... | collective-permute-start | bytes 786440 | tf_op jit(solution)/shard_map/ppermute | solution.py:624
  126.1 24.0 %collective-permute-start.31 = (bf16[128,1024]{1,0:T(8,128)(2,1)S(1)}, bf16[128,1024]{1,0:T(8,128)(2,1)}, u32[]{:S(2)}, u32[]{:S(2)}) collective-permute-start(bf16[128,1024]{1,0:T(8,128)(2,1)S(1)} %copy-done.22), channel_id=1, source_target_pairs={{0,1},{1,0},{2,3},{3,2},{4,5},{5,4},{6,7},{7,6},{8,9},{9,8},{10,11... | collective-permute-start | bytes 786440 | tf_op jit(solution)/shard_map/ppermute | solution.py:624
  126.2 24.0 %collective-permute-start.32 = (bf16[128,1024]{1,0:T(8,128)(2,1)}, bf16[128,1024]{1,0:T(8,128)(2,1)}, u32[]{:S(2)}, u32[]{:S(2)}) collective-permute-start(bf16[128,1024]{1,0:T(8,128)(2,1)} %collective-permute-done.17.refs_4_), channel_id=1, source_target_pairs={{0,1},{1,0},{2,3},{3,2},{4,5},{5,4},{6,7},{7,6},{8,9},{9,8},{10,11... | collective-permute-start | bytes 786440 | tf_op jit(solution)/shard_map/ppermute | solution.py:624
  133.8 11.0 %collective-permute-start.27 = (bf16[128,1024]{1,0:T(8,128)(2,1)}, bf16[128,1024]{1,0:T(8,128)(2,1)}, u32[]{:S(2)}, u32[]{:S(2)}) collective-permute-start(bf16[128,1024]{1,0:T(8,128)(2,1)} %get-tuple-element.120.refs_10_), channel_id=1, source_target_pairs={{0,2},{1,3},{2,0},{3,1},{4,6},{5,7},{6,4},{7,5},{8,10},{9,11},{10,... | collective-permute-start | bytes 786440 | tf_op jit(solution)/shard_map/ppermute | solution.py:624
  134.7 14.9 %collective-permute-start.26 = (bf16[176,1024]{1,0:T(8,128)(2,1)S(1)}, bf16[176,1024]{1,0:T(8,128)(2,1)S(1)}, u32[]{:S(2)}, u32[]{:S(2)}) collective-permute-start(bf16[176,1024]{1,0:T(8,128)(2,1)S(1)} %copy-done.11), channel_id=1, source_target_pairs={{0,2},{1,3},{2,0},{3,1},{4,6},{5,7},{6,4},{7,5},{8,10},{9,11},{10,... | collective-permute-start | bytes 1081352 | tf_op jit(solution)/shard_map/ppermute | solution.py:624
  138.6 22.8 %collective-permute-start.24 = (bf16[2,128,1024]{2,1,0:T(8,128)(2,1)}, bf16[2,128,1024]{2,1,0:T(8,128)(2,1)}, u32[]{:S(2)}, u32[]{:S(2)}) collective-permute-start(bf16[2,128,1024]{2,1,0:T(8,128)(2,1)} %slice.94), channel_id=1, source_target_pairs={{0,4},{1,5},{2,6},{3,7},{4,0},{5,1},{6,2},{7,3},{8,12},{9,13},{10,... | collective-permute-start | bytes 1572872 | tf_op jit(solution)/shard_map/ppermute | solution.py:624
  149.6 3.5 %collective-permute-start.33 = (bf16[176,1024]{1,0:T(8,128)(2,1)S(1)}, bf16[176,1024]{1,0:T(8,128)(2,1)S(1)}, u32[]{:S(2)}, u32[]{:S(2)}) collective-permute-start(bf16[176,1024]{1,0:T(8,128)(2,1)S(1)} %copy-done.11), channel_id=1, source_target_pairs={{0,1},{1,0},{2,3},{3,2},{4,5},{5,4},{6,7},{7,6},{8,9},{9,8},{10,11... | collective-permute-start | bytes 1081352 | tf_op jit(solution)/shard_map/ppermute | solution.py:624
  149.6 3.5 %collective-permute-start.34 = (bf16[176,1024]{1,0:T(8,128)(2,1)S(1)}, bf16[176,1024]{1,0:T(8,128)(2,1)S(1)}, u32[]{:S(2)}, u32[]{:S(2)}) collective-permute-start(bf16[176,1024]{1,0:T(8,128)(2,1)S(1)} %collective-permute-done.26.refs_8_), channel_id=1, source_target_pairs={{0,1},{1,0},{2,3},{3,2},{4,5},{5,4},{6,7},{7,6},{8,9},{9,8},{10,11... | collective-permute-start | bytes 1081352 | tf_op jit(solution)/shard_map/ppermute | solution.py:624
  152.3 11.6 %collective-permute-start.28 = (bf16[144,1024]{1,0:T(8,128)(2,1)}, bf16[144,1024]{1,0:T(8,128)(2,1)}, u32[]{:S(2)}, u32[]{:S(2)}) collective-permute-start(bf16[144,1024]{1,0:T(8,128)(2,1)} %get-tuple-element.125.rest_0_), channel_id=1, source_target_pairs={{0,2},{1,3},{2,0},{3,1},{4,6},{5,7},{6,4},{7,5},{8,10},{9,11},{10,... | collective-permute-start | bytes 884744 | tf_op jit(solution)/shard_map/ppermute | solution.py:624
  159.8 15.8 %collective-permute-start.37 = (bf16[4,32,2176]{2,1,0:T(8,128)(2,1)}, bf16[4,32,2176]{2,1,0:T(8,128)(2,1)S(1)}, u32[]{:S(2)}, u32[]{:S(2)}) collective-permute-start(bf16[4,32,2176]{2,1,0:T(8,128)(2,1)} %get-tuple-element.123), channel_id=1, source_target_pairs={{0,4},{1,5},{2,6},{3,7},{4,0},{5,1},{6,2},{7,3},{8,12},{9,13},{10,... | collective-permute-start | bytes 1671176 | tf_op jit(solution)/shard_map/ppermute | solution.py:624
  169.9 11.0 %collective-permute-start.40 = (bf16[4,32,1152]{2,1,0:T(8,128)(2,1)}, bf16[4,32,1152]{2,1,0:T(8,128)(2,1)S(1)}, u32[]{:S(2)}, u32[]{:S(2)}) collective-permute-start(bf16[4,32,1152]{2,1,0:T(8,128)(2,1)} %get-tuple-element.128), channel_id=1, source_target_pairs={{0,4},{1,5},{2,6},{3,7},{4,0},{5,1},{6,2},{7,3},{8,12},{9,13},{10,... | collective-permute-start | bytes 884744 | tf_op jit(solution)/shard_map/ppermute | solution.py:624
  178.1 11.9 %collective-permute-start.29 = (bf16[128,1024]{1,0:T(8,128)(2,1)S(1)}, bf16[128,1024]{1,0:T(8,128)(2,1)S(1)}, u32[]{:S(2)}, u32[]{:S(2)}) collective-permute-start(bf16[128,1024]{1,0:T(8,128)(2,1)S(1)} %fusion.3), channel_id=1, source_target_pairs={{0,2},{1,3},{2,0},{3,1},{4,6},{5,7},{6,4},{7,5},{8,10},{9,11},{10,... | collective-permute-start | bytes 786440 | tf_op jit(solution)/shard_map/ppermute | solution.py:624
  183.9 24.0 %collective-permute-start.30 = (bf16[128,3072]{1,0:T(8,128)(2,1)S(1)}, bf16[128,3072]{1,0:T(8,128)(2,1)}, u32[]{:S(2)}, u32[]{:S(2)}) collective-permute-start(bf16[128,3072]{1,0:T(8,128)(2,1)S(1)} %constant_dynamic-slice_fusion), channel_id=1, source_target_pairs={{0,4},{1,5},{2,6},{3,7},{4,0},{5,1},{6,2},{7,3},{8,12},{9,13},{10,... | collective-permute-start | bytes 2359304 | tf_op jit(solution)/shard_map/ppermute | solution.py:624
  185.5 10.1 %collective-permute-start.43 = (bf16[32,3328]{1,0:T(8,128)(2,1)S(1)}, bf16[32,3328]{1,0:T(8,128)(2,1)S(1)}, u32[]{:S(2)}, u32[]{:S(2)}) collective-permute-start(bf16[32,3328]{1,0:T(8,128)(2,1)S(1)} %get-tuple-element.145), channel_id=1, source_target_pairs={{0,24},{1,25},{2,26},{3,27},{4,28},{5,29},{6,30},{7,31},{8,16},{9,... | collective-permute-start | bytes 638984 | tf_op jit(solution)/shard_map/ppermute | solution.py:624
  188.4 18.8 %collective-permute-start.42 = (bf16[32,3328]{1,0:T(8,128)(2,1)S(1)}, bf16[32,3328]{1,0:T(8,128)(2,1)S(1)}, u32[]{:S(2)}, u32[]{:S(2)}) collective-permute-start(bf16[32,3328]{1,0:T(8,128)(2,1)S(1)} %get-tuple-element.146), channel_id=1, source_target_pairs={{0,16},{1,17},{2,18},{3,19},{4,20},{5,21},{6,22},{7,23},{8,24},{9,... | collective-permute-start | bytes 638984 | tf_op jit(solution)/shard_map/ppermute | solution.py:624
  188.6 18.6 %collective-permute-start.41 = (bf16[32,3328]{1,0:T(8,128)(2,1)S(1)}, bf16[32,3328]{1,0:T(8,128)(2,1)S(1)}, u32[]{:S(2)}, u32[]{:S(2)}) collective-permute-start(bf16[32,3328]{1,0:T(8,128)(2,1)S(1)} %get-tuple-element.147), channel_id=1, source_target_pairs={{0,8},{1,9},{2,10},{3,11},{4,12},{5,13},{6,14},{7,15},{8,0},{9,1},... | collective-permute-start | bytes 638984 | tf_op jit(solution)/shard_map/ppermute | solution.py:624
  (46 other events, 258.7 us)
Sparse Core Ops, SparseCore 0:
  71.2 111.4 reduce-scatter.1

commit v2 on v1

--- a/solution.py
+++ b/solution.py
@@ -100,8 +100,9 @@
 def forward_kernel(
     info_ref, wq_ref, wk_ref, wv_ref, wo_ref, gain_one_ref, gain_two_ref, cos_ref, sin_ref, *rest
 ):
-    blocks, outs = rest[:-11], rest[-11:]
-    q_ref, k_ref, v_ref, lse_ref, att_ref, hid_ref, n2_ref, n1_ref, wq_held, wo_held, sems = outs
+    blocks, outs = rest[:-16], rest[-16:]
+    q_out, k_out, v_out, lse_ref, att_ref, hid_ref, n2_ref, n1_out = outs[:8]
+    wq_held, wo_held, q_ref, k_ref, v_ref, n1_ref, sems, out_sems = outs[8:]
     copies = start_copies([(wq_ref, wq_held), (wo_ref, wo_held)], sems)
     tokens_ref = blocks[0]
     rows = tokens_ref.shape[0]
@@ -111,6 +112,7 @@
             b[...].astype(jnp.float32), gain_one_ref[...]
         )[0].astype(jnp.bfloat16)
     normed = n1_ref[...]
+    out_copies = start_copies([(n1_ref, n1_out)], out_sems)
     cosine, sine = cos_ref[...], sin_ref[...]
     keys = dot(normed, wk_ref[...])
     values = dot(normed, wv_ref[...])
@@ -122,6 +124,7 @@
         first, second = twice(values[:, cols])
         v_ref[2 * c] = first.astype(jnp.bfloat16)
         v_ref[2 * c + 1] = second.astype(jnp.bfloat16)
+    out_copies += start_copies([(k_ref, k_out), (v_ref, v_out)], out_sems.at[pl.ds(1, 2)])
     allowed = allowed_mask(info_ref, seq_len, rows)
     wait_all(copies[:1])
     query_pre = dot(n1_ref[:rows, :], wq_held[...])
@@ -137,10 +140,12 @@
         lse_ref[h : h + 1, :] = row_max + jnp.log(total)
         prob = (exps * (1.0 / total)).astype(jnp.bfloat16)
         att_ref[:, cols] = join_heads(dot(prob, v_ref[h], 0, 0)).astype(jnp.bfloat16)
+    out_copies += start_copies([(q_ref, q_out)], out_sems.at[pl.ds(3, 1)])
     wait_all(copies[1:])
     hidden = tokens_ref[...].astype(jnp.float32) + dot(att_ref[...], wo_held[...])
     hid_ref[...] = hidden
     n2_ref[...] = norm_forward(hidden, gain_two_ref[...])[0].astype(jnp.bfloat16)
+    wait_all(out_copies)
 
 
 def start_copies(pairs, sems):
@@ -665,8 +670,12 @@
     cot_mask = jnp.concatenate(
         [cotangent, jnp.pad(routed.astype(low), ((0, 0), (0, LANES - experts)))], axis=1
     )
+    first_cot = cot_mask
     cot_mask, *tokens_even = lax.optimization_barrier((cot_mask, *tokens_even))
-    cot_even = gather_even(cot_mask, 2)
+    cot_even = [
+        cot_mask if q == (0, 0) else send(first_cot if q == (1, 0) else cot_mask, *q)
+        for q in [(s, r) for s in range(2) for r in range(0, groups, 2)]
+    ]
     my_dp = lax.axis_index("dp")
     info = jnp.stack([me, prefix_len[0], half, my_dp]).astype(jnp.int32)
     gain_one, gain_two = norm1_gain[None], norm2_gain[None]
@@ -685,10 +694,16 @@
         ),
         "attention_forward",
         hbm=(1, 4),
+        hbm_out=(0, 1, 2, 7),
         scratch=(
             pltpu.VMEM((model_width, H * HD), low),
             pltpu.VMEM((H * HD, model_width), low),
+            pltpu.VMEM((tok_rows, H * HD), low),
+            pltpu.VMEM((KV, seq_len, LANES), low),
+            pltpu.VMEM((KV, seq_len, LANES), low),
+            pltpu.VMEM((seq_len, model_width), low),
             pltpu.SemaphoreType.DMA((2,)),
+            pltpu.SemaphoreType.DMA((4,)),
         ),
     )(
         info, w_query, w_key, w_value, w_output, gain_one, gain_two, cosine, sine, *tokens_blocks,
@@ -802,8 +817,11 @@
     kv_mine = core_sum(kv_odd, kv_even)
     kv_arrived = swap(kv_mine, 1)
     mix_odd, kv_mine = lax.optimization_barrier((mix_odd, kv_mine))
-    mix_mine = core_sum(mix_odd, mix_even).reshape(2, groups // 2, tok_rows, model_width)
-    mix_pair = mix_mine[0] + send(mix_mine[1].astype(low), 1, 0).astype(f32)
+    mix_got = send(mix_odd, 0, 1)
+    n_own = groups // 2
+    mix_got_pair = send(
+        (mix_even[n_own:] + mix_got[n_own:].astype(f32)).astype(low), 1, 0
+    )
     query_later, grad_branch, *kv_arrived = lax.optimization_barrier(
         (grad_query, grad_branch, *kv_arrived)
     )
@@ -821,17 +839,12 @@
         kv_mine[0], grad_normed_q, w_key, w_value, tokens, gain_one, grad_hidden, cosine, sine,
         *kv_arrived,
     )
-    grad_kv, *later = lax.optimization_barrier((grad_kv, *branch_even, *query_even))
+    grad_kv, mix_got_pair, *later = lax.optimization_barrier(
+        (grad_kv, mix_got_pair, *branch_even, *query_even)
+    )
     kv_even_blocks = gather_even(grad_kv, 1)
     branch_blocks = gather_odd(later[: len(branch_even)])
     query_blocks = gather_odd(later[len(branch_even) :])
-    mix_pair, *kv_even_blocks = lax.optimization_barrier((mix_pair, *kv_even_blocks))
-    kv_blocks = gather_odd(kv_even_blocks)
-    mixture = mix_pair[0]
-    for a in swap(mix_pair, 1):
-        mixture = mixture + a.astype(f32)
-    block_out = (hidden_state + mixture).astype(low)
-
     own_rows = model_width // (copies * groups)
     n_early, n_late = model_width + LANES + H * HD, 2 * KV * HD + LANES
     select = pltpu.VMEM((copies * own_rows, model_width), low)
@@ -846,12 +859,20 @@
         scratch=(select,),
     )(info, normed1_all, *attended_blocks, *branch_blocks, *query_blocks)
     early = early_even + send(early_odd, 1, 0).astype(f32)
+    _, *kv_even_blocks = lax.optimization_barrier((early_odd, *kv_even_blocks))
+    kv_blocks = gather_odd(kv_even_blocks)
     late_odd, late_even = call(
         late_dense_kernel,
         (shape(outer, own_rows, n_late), shape(outer, own_rows, n_late, dtype=f32)),
         "dense_late",
         scratch=(select,),
     )(info, normed1_t, *kv_blocks)
+    mix_got_pair, late_odd = lax.optimization_barrier((mix_got_pair, late_odd))
+    mix_pair = mix_even[:n_own] + mix_got[:n_own].astype(f32) + mix_got_pair.astype(f32)
+    mixture = mix_pair[0]
+    for a in swap(mix_pair, 1):
+        mixture = mixture + a.astype(f32)
+    block_out = (hidden_state + mixture).astype(low)
     late = late_even + send(late_odd, 1, 0).astype(f32)
     dense_send = jnp.concatenate([early[1:].astype(low), late[1:].astype(low)], axis=2)
 
@@ -879,6 +900,7 @@
             shape(1, own_rows, dtype=f32),
         ),
         "place",
+        limit=48,
     )(info, reduced, swapped, early, late, *dense_arrived)
     return (
         block_out,

time: 220 us -> 216 us (0.982)
  local copies, waits for them, and re-layouts: 14 us -> 9.84 us
  waiting for transfers between devices: 72.2 us -> 75.9 us
    ppermute x44, waiting for transfers between devices: 70.4 us -> 75.9 us  [send(): lax.ppermute(block, ('dp', 'expert'), [(i * groups + j, (i ^ pair_flip) *...]
    unnamed x67 -> x59, local copies, waits for them, and re-layouts: 9.8 us -> 5.73 us
  transfers between devices with their start and end apart: 45 -> 45, of which waited for: 22 -> 26; matrix products, arithmetic and copies ran while one was open for 8% -> 8% of each run, Pallas kernels for 21% -> 22%
where the time goes in v2:
time: 216 us; the launch traced here: 215 us
  waiting for transfers between devices  75.9 us (35%)
  Pallas kernels  68.7 us (32%)
  starting transfers between devices  32.7 us (15%)
  between operations  15.1 us (7%)
  other arithmetic  13.2 us (6%)
  local copies, waits for them, and re-layouts  9.84 us (5%)
    ppermute x44, waiting for transfers between devices, send(): lax.ppermute(block, ('dp', 'expert'), [(i * groups + j, (i ^ pair_flip) *...  75.9 us
    pallas_call x8, Pallas kernels, run(): pl.pallas_call(kernel, out_shape=out_shape, in_specs=specs, out_specs=[pl...  68.7 us
    ppermute x44, starting transfers between devices, send(): lax.ppermute(block, ('dp', 'expert'), [(i * groups + j, (i ^ pair_flip) *...  32.7 us
    unnamed x59, local copies, waits for them, and re-layouts  5.73 us
  transfers between devices with their start and end apart: 45, of which 26 were waited for; matrix products, arithmetic and copies ran while one was open for 8% of the time, Pallas kernels for 22%

profile of v2, /device:TPU:0, one launch (start us, length us, event | category | flops | bytes accessed | tf_op | source)
XLA Modules:
  0.0 215.5 jit_solution(11792844071762950692)
XLA Ops:
  7.2 3.0 %collective-permute-start = (bf16[128,1024]{1,0:T(8,128)(2,1)}, bf16[128,1024]{1,0:T(8,128)(2,1)S(1)}, u32[]{:S(2)}, u32[]{:S(2)}) collective-permute-start(bf16[128,1024]{1,0:T(8,128)(2,1)} %tokens_ref.1), channel_id=1, source_target_pairs={{0,2},{1,3},{2,0},{3,1},{4,6},{5,7},{6,4},{7,5},{8,10},{9,11},{10,... | collective-permute-start | bytes 786440 | tf_op jit(solution)/shard_map/ppermute | solution.py:629
  12.1 1.6 collective-permute-start.4
  13.7 2.6 %negate_select_fusion = (f32[512,128]{1,0:T(8,128)}, f32[512,128]{1,0:T(8,128)}) fusion(s32[128]{0:T(128)S(1)} %get-tuple-element.162, s32[128]{0:T(128)S(1)} %get-tuple-element.164, s32[128]{0:T(128)S(1)} %get-tuple-element.163, s32[128]{0:T(128)S(1)} %get-tuple-element.165, s32[512]{0:T(512)S(1)} %get-tuple-element.155, s32[512]{0:T(512)S(1)} %get-tuple-element.156, ...), kind=kLoop, calls=%fused_computation.17 | loop fusion | flops 917504 | bytes 535812 | tf_op jit(solution)/shard_map/jit(_where)/select_n | solution.py:26
  16.8 2.7 %collective-permute-start.5 = (bf16[128,1152]{1,0:T(8,128)(2,1)S(1)}, bf16[128,1152]{1,0:T(8,128)(2,1)}, u32[]{:S(2)}, u32[]{:S(2)}) collective-permute-start(bf16[128,1152]{1,0:T(8,128)(2,1)S(1)} %pad_maximum_fusion.1.refs_5_.refs_2_), channel_id=1, source_target_pairs={{0,6},{1,7},{2,4},{3,5},{4,2},{5,3},{6,0},{7,1},{8,14},{9,15},{10,... | collective-permute-start | bytes 884744 | tf_op jit(solution)/shard_map/ppermute | solution.py:629
  22.8 8.2 %attention_forward.1 = (bf16[128,1024]{1,0:T(8,128)(2,1)}, bf16[8,512,128]{2,1,0:T(8,128)(2,1)}, bf16[8,512,128]{2,1,0:T(8,128)(2,1)}, f32[8,256]{1,0:T(8,128)},...) custom-call(s32[4]{0:T(128)} %pad_add_fusion.info_ref.refs_0_, ...), custom_call_target="tpu_custom_call" | custom-call | tf_op jit(solution)/shard_map/attention_forward/pallas_call | solution.py:580
  31.1 1.8 collective-permute-done.3.refs_7_
  36.9 6.3 %collective-permute-done.15.refs_19_ = bf16[128,1024]{1,0:T(8,128)(2,1)S(1)} collective-permute-done((bf16[128,1024]{1,0:T(8,128)(2,1)}, bf16[128,1024]{1,0:T(8,128)(2,1)S(1)}, u32[]{:S(2)}, u32[]{:S(2)}) %collective-permute-start.15) | collective-permute-done | bytes 262176 | tf_op jit(solution)/shard_map/ppermute | solution.py:629
  43.3 3.1 %collective-permute-done.13.refs_17_ = bf16[128,1024]{1,0:T(8,128)(2,1)S(1)} collective-permute-done((bf16[128,1024]{1,0:T(8,128)(2,1)}, bf16[128,1024]{1,0:T(8,128)(2,1)S(1)}, u32[]{:S(2)}, u32[]{:S(2)}) %collective-permute-start.13) | collective-permute-done | bytes 262176 | tf_op jit(solution)/shard_map/ppermute | solution.py:629
  51.5 19.5 %experts.1 = (bf16[1024,3072]{1,0:T(8,128)(2,1)}, bf16[4,1024,896]{2,1,0:T(8,128)(2,1)}) custom-call(s32[4]{0:T(128)S(1)} %copy-done.4, bf16[1024,16]{1,0:T(8,128)(2,1)S(1)} %copy.30.refs_1_.refs_5_, bf16[4,1024,512]{2,1,0:T(8,128)(2,1)} %wg_ref.1, bf16[4,1024,512]{2,1,0:T(8,128)(2,1)} %wu_ref.1, bf16[4,512,1024]{2,1,0:T(8,128)(2,1)} %refs_16_.1, ...), custom_call_target="tpu_custom_call" | custom-call | tf_op jit(solution)/shard_map/experts/pallas_call | solution.py:580
  72.1 10.3 %experts_rows.1 = (bf16[4,128,1152]{2,1,0:T(8,128)(2,1)}, f32[4,128,1152]{2,1,0:T(8,128)}) custom-call(s32[4]{0:T(128)} %pad_add_fusion.info_ref.refs_0_, bf16[4,1024,512]{2,1,0:T(8,128)(2,1)} %wg_ref.1, bf16[4,1024,512]{2,1,0:T(8,128)(2,1)} %wu_ref.1, bf16[4,1024,896]{2,1,0:T(8,128)(2,1)} %get-tuple-element.90.acts_in.refs_15_), custom_call_target="tpu_custom_call" | custom-call | tf_op jit(solution)/shard_map/experts_rows/pallas_call | solution.py:580
  82.5 3.0 %collective-permute-done.18 = bf16[4,128,1152]{2,1,0:T(8,128)(2,1)S(1)} collective-permute-done((bf16[4,128,1152]{2,1,0:T(8,128)(2,1)}, bf16[4,128,1152]{2,1,0:T(8,128)(2,1)S(1)}, u32[]{:S(2)}, u32[]{:S(2)}) %collective-permute-start.18) | collective-permute-done | bytes 1179680 | tf_op jit(solution)/shard_map/ppermute | solution.py:629
  85.5 2.0 fusion.13
  88.2 2.0 collective-permute-start.20
  92.0 6.5 %collective-permute-done.21.refs_19_ = bf16[128,1152]{1,0:T(8,128)(2,1)S(1)} collective-permute-done((bf16[128,1152]{1,0:T(8,128)(2,1)S(1)}, bf16[128,1152]{1,0:T(8,128)(2,1)S(1)}, u32[]{:S(2)}, u32[]{:S(2)}) %collective-permute-start.21) | collective-permute-done | bytes 294944 | tf_op jit(solution)/shard_map/ppermute | solution.py:629
  98.5 5.0 %collective-permute-done.20.refs_18_ = bf16[128,1152]{1,0:T(8,128)(2,1)S(1)} collective-permute-done((bf16[128,1152]{1,0:T(8,128)(2,1)S(1)}, bf16[128,1152]{1,0:T(8,128)(2,1)S(1)}, u32[]{:S(2)}, u32[]{:S(2)}) %collective-permute-start.20) | collective-permute-done | bytes 294944 | tf_op jit(solution)/shard_map/ppermute | solution.py:629
  104.7 15.5 %attention_backward.1 = (f32[128,1024]{1,0:T(8,128)}, bf16[176,1024]{1,0:T(8,128)(2,1)}, bf16[128,1024]{1,0:T(8,128)(2,1)}, bf16[2,128,1024]{2,1,0:T(8,128)(2,1)...) custom-call(s32[4]{0:T(128)} %pad_add_fusion.info_ref.refs_0_, ...), custom_call_target="tpu_custom_call" | custom-call | tf_op jit(solution)/shard_map/attention_backward/pallas_call | solution.py:580
  120.4 2.1 collective-permute-done.22
  125.2 1.6 collective-permute-done.23
  127.9 4.8 %collective-permute-done.24.rest_0_ = bf16[128,1024]{1,0:T(8,128)(2,1)S(1)} collective-permute-done((bf16[128,1024]{1,0:T(8,128)(2,1)S(1)}, bf16[128,1024]{1,0:T(8,128)(2,1)S(1)}, u32[]{:S(2)}, u32[]{:S(2)}) %collective-permute-start.24) | collective-permute-done | bytes 262176 | tf_op jit(solution)/shard_map/ppermute | solution.py:629
  136.2 4.1 %tokens_backward.1 = (bf16[144,1024]{1,0:T(8,128)(2,1)}, bf16[128,1024]{1,0:T(8,128)(2,1)}) custom-call(f32[128,1024]{1,0:T(8,128)} %slice_bitcast_fusion.2.own_ref, f32[128,1024]{1,0:T(8,128)} %get-tuple-element.105.gn_ref, bf16[1024,512]{1,0:T(8,128)(2,1)} %wk_ref.3, bf16[1024,512]{1,0:T(8,128)(2,1)} %wv_ref.3, bf16[128,1024]{1,0:T(8,128)(2,1)} %tokens_ref.1, ...), custom_call_target="tpu_custom_call" | custom-call | tf_op jit(solution)/shard_map/tokens_backward/pallas_call | solution.py:580
  140.3 8.2 %collective-permute-done.27.refs_12_ = bf16[128,1024]{1,0:T(8,128)(2,1)} collective-permute-done((bf16[128,1024]{1,0:T(8,128)(2,1)}, bf16[128,1024]{1,0:T(8,128)(2,1)}, u32[]{:S(2)}, u32[]{:S(2)}) %collective-permute-start.27) | collective-permute-done | bytes 262176 | tf_op jit(solution)/shard_map/ppermute | solution.py:629
  153.8 5.5 %dense_early.1 = (bf16[4,32,2176]{2,1,0:T(8,128)(2,1)}, f32[4,32,2176]{2,1,0:T(8,128)}, bf16[256,512]{1,0:T(8,128)(2,1)}) custom-call(s32[4]{0:T(128)} %pad_add_fusion.info_ref.refs_0_, bf16[512,1024]{1,0:T(8,128)(2,1)} %get-tuple-element.114.refs_1_, bf16[128,1024]{1,0:T(8,128)(2,1)} %get-tuple-element.115.refs_2_, ...), custom_call_target="tpu_custom_call" | custom-call | tf_op jit(solution)/shard_map/dense_early/pallas_call | solution.py:580
  162.4 3.0 %dense_late.1 = (bf16[4,32,1152]{2,1,0:T(8,128)(2,1)}, f32[4,32,1152]{2,1,0:T(8,128)}) custom-call(s32[4]{0:T(128)} %pad_add_fusion.info_ref.refs_0_, bf16[256,512]{1,0:T(8,128)(2,1)} %get-tuple-element.121.normed_t_ref, bf16[144,1024]{1,0:T(8,128)(2,1)} %get-tuple-element.124.rest_0_, bf16[144,1024]{1,0:T(8,128)(2,1)} %copy-done.16, ...), custom_call_target="tpu_custom_call" | custom-call | tf_op jit(solution)/shard_map/dense_late/pallas_call | solution.py:580
  165.3 1.8 convert_add_fusion.2
  169.9 5.6 %collective-permute-done.39 = bf16[4,32,2176]{2,1,0:T(8,128)(2,1)S(1)} collective-permute-done((bf16[4,32,2176]{2,1,0:T(8,128)(2,1)}, bf16[4,32,2176]{2,1,0:T(8,128)(2,1)S(1)}, u32[]{:S(2)}, u32[]{:S(2)}) %collective-permute-start.39) | collective-permute-done | bytes 557088 | tf_op jit(solution)/shard_map/ppermute | solution.py:629
  175.7 5.5 %collective-permute-done.40 = bf16[4,32,1152]{2,1,0:T(8,128)(2,1)S(1)} collective-permute-done((bf16[4,32,1152]{2,1,0:T(8,128)(2,1)S(1)}, bf16[4,32,1152]{2,1,0:T(8,128)(2,1)S(1)}, u32[]{:S(2)}, u32[]{:S(2)}) %collective-permute-start.40) | collective-permute-done | bytes 294944 | tf_op jit(solution)/shard_map/ppermute | solution.py:629
  182.7 1.5 collective-permute-start.38
  184.3 2.9 %collective-permute-start.43 = (bf16[32,3328]{1,0:T(8,128)(2,1)S(1)}, bf16[32,3328]{1,0:T(8,128)(2,1)S(1)}, u32[]{:S(2)}, u32[]{:S(2)}) collective-permute-start(bf16[32,3328]{1,0:T(8,128)(2,1)S(1)} %get-tuple-element.149), channel_id=1, source_target_pairs={{0,24},{1,25},{2,26},{3,27},{4,28},{5,29},{6,30},{7,31},{8,16},{9,... | collective-permute-start | bytes 638984 | tf_op jit(solution)/shard_map/ppermute | solution.py:629
  188.7 1.8 fusion.2
  190.5 3.9 %collective-permute-done.43.refs_7_ = bf16[32,3328]{1,0:T(8,128)(2,1)S(1)} collective-permute-done((bf16[32,3328]{1,0:T(8,128)(2,1)S(1)}, bf16[32,3328]{1,0:T(8,128)(2,1)S(1)}, u32[]{:S(2)}, u32[]{:S(2)}) %collective-permute-start.43) | collective-permute-done | bytes 213024 | tf_op jit(solution)/shard_map/ppermute | solution.py:629
  194.4 11.6 %collective-permute-done.42.refs_6_ = bf16[32,3328]{1,0:T(8,128)(2,1)S(1)} collective-permute-done((bf16[32,3328]{1,0:T(8,128)(2,1)S(1)}, bf16[32,3328]{1,0:T(8,128)(2,1)S(1)}, u32[]{:S(2)}, u32[]{:S(2)}) %collective-permute-start.42) | collective-permute-done | bytes 213024 | tf_op jit(solution)/shard_map/ppermute | solution.py:629
  206.0 2.6 %place.1 = (f32[4,128,512]{2,1,0:T(8,128)}, f32[4,128,512]{2,1,0:T(8,128)}, f32[4,512,128]{2,1,0:T(8,128)}, f32[32,1024]{1,0:T(8,128)}, f32[32,512]{1,0:T(8,128)...) custom-call(s32[4]{0:T(128)S(1)} %copy-done.5, ...), custom_call_target="tpu_custom_call" | custom-call | tf_op jit(solution)/shard_map/place/pallas_call | solution.py:580
  (155 shorter events, 40.8 us)
Async XLA Ops:
  7.2 174.2 %reduce-scatter.2.cloned.1.call-start = ((), (), s32[]{:S(2)}) async-start(), calls=%async_computation.1 | async-start | bytes 7864320 | tf_op jit(solution)/shard_map/reduce_scatter | solution.py:753
  7.2 9.6 %collective-permute-start = (bf16[128,1024]{1,0:T(8,128)(2,1)}, bf16[128,1024]{1,0:T(8,128)(2,1)S(1)}, u32[]{:S(2)}, u32[]{:S(2)}) collective-permute-start(bf16[128,1024]{1,0:T(8,128)(2,1)} %tokens_ref.1), channel_id=1, source_target_pairs={{0,2},{1,3},{2,0},{3,1},{4,6},{5,7},{6,4},{7,5},{8,10},{9,11},{10,... | collective-permute-start | bytes 786440 | tf_op jit(solution)/shard_map/ppermute | solution.py:629
  12.1 19.0 %collective-permute-start.4 = (bf16[128,1152]{1,0:T(8,128)(2,1)S(1)}, bf16[128,1152]{1,0:T(8,128)(2,1)S(1)}, u32[]{:S(2)}, u32[]{:S(2)}) collective-permute-start(bf16[128,1152]{1,0:T(8,128)(2,1)S(1)} %pad_maximum_fusion.1.refs_5_.refs_2_), channel_id=1, source_target_pairs={{0,4},{1,5},{2,6},{3,7},{4,0},{5,1},{6,2},{7,3},{8,12},{9,13},{10,... | collective-permute-start | bytes 884744 | tf_op jit(solution)/shard_map/ppermute | solution.py:629
  16.8 14.3 %collective-permute-start.5 = (bf16[128,1152]{1,0:T(8,128)(2,1)S(1)}, bf16[128,1152]{1,0:T(8,128)(2,1)}, u32[]{:S(2)}, u32[]{:S(2)}) collective-permute-start(bf16[128,1152]{1,0:T(8,128)(2,1)S(1)} %pad_maximum_fusion.1.refs_5_.refs_2_), channel_id=1, source_target_pairs={{0,6},{1,7},{2,4},{3,5},{4,2},{5,3},{6,0},{7,1},{8,14},{9,15},{10,... | collective-permute-start | bytes 884744 | tf_op jit(solution)/shard_map/ppermute | solution.py:629
  19.4 13.5 %collective-permute-start.3 = (bf16[128,1152]{1,0:T(8,128)(2,1)S(1)}, bf16[128,1152]{1,0:T(8,128)(2,1)}, u32[]{:S(2)}, u32[]{:S(2)}) collective-permute-start(bf16[128,1152]{1,0:T(8,128)(2,1)S(1)} %pad_maximum_fusion.1.refs_5_.refs_2_), channel_id=1, source_target_pairs={{0,2},{1,3},{2,0},{3,1},{4,6},{5,7},{6,4},{7,5},{8,10},{9,11},{10,... | collective-permute-start | bytes 884744 | tf_op jit(solution)/shard_map/ppermute | solution.py:629
  32.9 10.3 %collective-permute-start.15 = (bf16[128,1024]{1,0:T(8,128)(2,1)}, bf16[128,1024]{1,0:T(8,128)(2,1)S(1)}, u32[]{:S(2)}, u32[]{:S(2)}) collective-permute-start(bf16[128,1024]{1,0:T(8,128)(2,1)} %get-tuple-element.89.refs_13_.refs_3_), channel_id=1, source_target_pairs={{0,6},{1,7},{2,4},{3,5},{4,2},{5,3},{6,0},{7,1},{8,14},{9,15},{10,... | collective-permute-start | bytes 786440 | tf_op jit(solution)/shard_map/ppermute | solution.py:629
  34.0 12.3 %collective-permute-start.13 = (bf16[128,1024]{1,0:T(8,128)(2,1)}, bf16[128,1024]{1,0:T(8,128)(2,1)S(1)}, u32[]{:S(2)}, u32[]{:S(2)}) collective-permute-start(bf16[128,1024]{1,0:T(8,128)(2,1)} %get-tuple-element.89.refs_13_.refs_3_), channel_id=1, source_target_pairs={{0,4},{1,5},{2,6},{3,7},{4,0},{5,1},{6,2},{7,3},{8,12},{9,13},{10,... | collective-permute-start | bytes 786440 | tf_op jit(solution)/shard_map/ppermute | solution.py:629
  35.3 12.3 %collective-permute-start.11 = (bf16[128,1024]{1,0:T(8,128)(2,1)}, bf16[128,1024]{1,0:T(8,128)(2,1)S(1)}, u32[]{:S(2)}, u32[]{:S(2)}) collective-permute-start(bf16[128,1024]{1,0:T(8,128)(2,1)} %get-tuple-element.89.refs_13_.refs_3_), channel_id=1, source_target_pairs={{0,2},{1,3},{2,0},{3,1},{4,6},{5,7},{6,4},{7,5},{8,10},{9,11},{10,... | collective-permute-start | bytes 786440 | tf_op jit(solution)/shard_map/ppermute | solution.py:629
  36.4 11.8 %collective-permute-start.6 = (bf16[128,1152]{1,0:T(8,128)(2,1)S(1)}, bf16[128,1152]{1,0:T(8,128)(2,1)S(1)}, u32[]{:S(2)}, u32[]{:S(2)}) collective-permute-start(bf16[128,1152]{1,0:T(8,128)(2,1)S(1)} %pad_maximum_fusion.1.refs_5_.refs_2_), channel_id=1, source_target_pairs={{0,1},{1,0},{2,3},{3,2},{4,5},{5,4},{6,7},{7,6},{8,9},{9,8},{10,11... | collective-permute-start | bytes 884744 | tf_op jit(solution)/shard_map/ppermute | solution.py:629
  36.4 11.9 %collective-permute-start.7 = (bf16[128,1152]{1,0:T(8,128)(2,1)}, bf16[128,1152]{1,0:T(8,128)(2,1)S(1)}, u32[]{:S(2)}, u32[]{:S(2)}) collective-permute-start(bf16[128,1152]{1,0:T(8,128)(2,1)} %collective-permute-done.3.refs_7_), channel_id=1, source_target_pairs={{0,1},{1,0},{2,3},{3,2},{4,5},{5,4},{6,7},{7,6},{8,9},{9,8},{10,11... | collective-permute-start | bytes 884744 | tf_op jit(solution)/shard_map/ppermute | solution.py:629
  43.3 4.4 %collective-permute-start.10 = (bf16[128,1024]{1,0:T(8,128)(2,1)}, bf16[128,1024]{1,0:T(8,128)(2,1)S(1)}, u32[]{:S(2)}, u32[]{:S(2)}) collective-permute-start(bf16[128,1024]{1,0:T(8,128)(2,1)} %get-tuple-element.89.refs_13_.refs_3_), channel_id=1, source_target_pairs={{0,1},{1,0},{2,3},{3,2},{4,5},{5,4},{6,7},{7,6},{8,9},{9,8},{10,11... | collective-permute-start | bytes 786440 | tf_op jit(solution)/shard_map/ppermute | solution.py:629
  71.0 11.4 %collective-permute-start.17 = (bf16[128,1024]{1,0:T(8,128)(2,1)}, bf16[128,1024]{1,0:T(8,128)(2,1)}, u32[]{:S(2)}, u32[]{:S(2)}) collective-permute-start(bf16[128,1024]{1,0:T(8,128)(2,1)} %get-tuple-element.115.refs_2_), channel_id=1, source_target_pairs={{0,2},{1,3},{2,0},{3,1},{4,6},{5,7},{6,4},{7,5},{8,10},{9,11},{10,... | collective-permute-start | bytes 786440 | tf_op jit(solution)/shard_map/ppermute | solution.py:629
  82.4 3.1 %collective-permute-start.18 = (bf16[4,128,1152]{2,1,0:T(8,128)(2,1)}, bf16[4,128,1152]{2,1,0:T(8,128)(2,1)S(1)}, u32[]{:S(2)}, u32[]{:S(2)}) collective-permute-start(bf16[4,128,1152]{2,1,0:T(8,128)(2,1)} %get-tuple-element.94), channel_id=1, source_target_pairs={{0,1},{1,0},{2,3},{3,2},{4,5},{5,4},{6,7},{7,6},{8,9},{9,8},{10,11... | collective-permute-start | bytes 3538952 | tf_op jit(solution)/shard_map/ppermute | solution.py:629
  87.6 10.9 %collective-permute-start.21 = (bf16[128,1152]{1,0:T(8,128)(2,1)S(1)}, bf16[128,1152]{1,0:T(8,128)(2,1)S(1)}, u32[]{:S(2)}, u32[]{:S(2)}) collective-permute-start(bf16[128,1152]{1,0:T(8,128)(2,1)S(1)} %get-tuple-element.146), channel_id=1, source_target_pairs={{0,6},{1,7},{2,4},{3,5},{4,2},{5,3},{6,0},{7,1},{8,14},{9,15},{10,... | collective-permute-start | bytes 884744 | tf_op jit(solution)/shard_map/ppermute | solution.py:629
  88.2 15.4 %collective-permute-start.20 = (bf16[128,1152]{1,0:T(8,128)(2,1)S(1)}, bf16[128,1152]{1,0:T(8,128)(2,1)S(1)}, u32[]{:S(2)}, u32[]{:S(2)}) collective-permute-start(bf16[128,1152]{1,0:T(8,128)(2,1)S(1)} %get-tuple-element.147), channel_id=1, source_target_pairs={{0,4},{1,5},{2,6},{3,7},{4,0},{5,1},{6,2},{7,3},{8,12},{9,13},{10,... | collective-permute-start | bytes 884744 | tf_op jit(solution)/shard_map/ppermute | solution.py:629
  90.2 13.8 %collective-permute-start.19 = (bf16[128,1152]{1,0:T(8,128)(2,1)S(1)}, bf16[128,1152]{1,0:T(8,128)(2,1)S(1)}, u32[]{:S(2)}, u32[]{:S(2)}) collective-permute-start(bf16[128,1152]{1,0:T(8,128)(2,1)S(1)} %get-tuple-element.148), channel_id=1, source_target_pairs={{0,2},{1,3},{2,0},{3,1},{4,6},{5,7},{6,4},{7,5},{8,10},{9,11},{10,... | collective-permute-start | bytes 884744 | tf_op jit(solution)/shard_map/ppermute | solution.py:629
  124.1 8.7 %collective-permute-start.24 = (bf16[128,1024]{1,0:T(8,128)(2,1)S(1)}, bf16[128,1024]{1,0:T(8,128)(2,1)S(1)}, u32[]{:S(2)}, u32[]{:S(2)}) collective-permute-start(bf16[128,1024]{1,0:T(8,128)(2,1)S(1)} %fusion.3), channel_id=1, source_target_pairs={{0,2},{1,3},{2,0},{3,1},{4,6},{5,7},{6,4},{7,5},{8,10},{9,11},{10,... | collective-permute-start | bytes 786440 | tf_op jit(solution)/shard_map/ppermute | solution.py:629
  127.9 20.6 %collective-permute-start.25 = (bf16[2,128,1024]{2,1,0:T(8,128)(2,1)}, bf16[2,128,1024]{2,1,0:T(8,128)(2,1)S(1)}, u32[]{:S(2)}, u32[]{:S(2)}) collective-permute-start(bf16[2,128,1024]{2,1,0:T(8,128)(2,1)} %add_convert_fusion), channel_id=1, source_target_pairs={{0,4},{1,5},{2,6},{3,7},{4,0},{5,1},{6,2},{7,3},{8,12},{9,13},{10,... | collective-permute-start | bytes 1572872 | tf_op jit(solution)/shard_map/ppermute | solution.py:629
  132.7 15.7 %collective-permute-start.26 = (bf16[176,1024]{1,0:T(8,128)(2,1)S(1)}, bf16[176,1024]{1,0:T(8,128)(2,1)}, u32[]{:S(2)}, u32[]{:S(2)}) collective-permute-start(bf16[176,1024]{1,0:T(8,128)(2,1)S(1)} %copy-done.12), channel_id=1, source_target_pairs={{0,2},{1,3},{2,0},{3,1},{4,6},{5,7},{6,4},{7,5},{8,10},{9,11},{10,... | collective-permute-start | bytes 1081352 | tf_op jit(solution)/shard_map/ppermute | solution.py:629
  133.7 14.7 %collective-permute-start.27 = (bf16[128,1024]{1,0:T(8,128)(2,1)}, bf16[128,1024]{1,0:T(8,128)(2,1)}, u32[]{:S(2)}, u32[]{:S(2)}) collective-permute-start(bf16[128,1024]{1,0:T(8,128)(2,1)} %get-tuple-element.119.refs_10_), channel_id=1, source_target_pairs={{0,2},{1,3},{2,0},{3,1},{4,6},{5,7},{6,4},{7,5},{8,10},{9,11},{10,... | collective-permute-start | bytes 786440 | tf_op jit(solution)/shard_map/ppermute | solution.py:629
  134.8 15.2 %collective-permute-start.28 = (bf16[128,1024]{1,0:T(8,128)(2,1)}, bf16[128,1024]{1,0:T(8,128)(2,1)}, u32[]{:S(2)}, u32[]{:S(2)}) collective-permute-start(bf16[128,1024]{1,0:T(8,128)(2,1)} %get-tuple-element.115.refs_2_), channel_id=1, source_target_pairs={{0,1},{1,0},{2,3},{3,2},{4,5},{5,4},{6,7},{7,6},{8,9},{9,8},{10,11... | collective-permute-start | bytes 786440 | tf_op jit(solution)/shard_map/ppermute | solution.py:629
  134.8 15.2 %collective-permute-start.29 = (bf16[128,1024]{1,0:T(8,128)(2,1)}, bf16[128,1024]{1,0:T(8,128)(2,1)}, u32[]{:S(2)}, u32[]{:S(2)}) collective-permute-start(bf16[128,1024]{1,0:T(8,128)(2,1)} %collective-permute-done.17.refs_4_), channel_id=1, source_target_pairs={{0,1},{1,0},{2,3},{3,2},{4,5},{5,4},{6,7},{7,6},{8,9},{9,8},{10,11... | collective-permute-start | bytes 786440 | tf_op jit(solution)/shard_map/ppermute | solution.py:629
  148.5 3.7 %collective-permute-start.30 = (bf16[176,1024]{1,0:T(8,128)(2,1)S(1)}, bf16[176,1024]{1,0:T(8,128)(2,1)S(1)}, u32[]{:S(2)}, u32[]{:S(2)}) collective-permute-start(bf16[176,1024]{1,0:T(8,128)(2,1)S(1)} %copy-done.12), channel_id=1, source_target_pairs={{0,1},{1,0},{2,3},{3,2},{4,5},{5,4},{6,7},{7,6},{8,9},{9,8},{10,11... | collective-permute-start | bytes 1081352 | tf_op jit(solution)/shard_map/ppermute | solution.py:629
  148.5 4.4 %collective-permute-start.31 = (bf16[176,1024]{1,0:T(8,128)(2,1)}, bf16[176,1024]{1,0:T(8,128)(2,1)S(1)}, u32[]{:S(2)}, u32[]{:S(2)}) collective-permute-start(bf16[176,1024]{1,0:T(8,128)(2,1)} %collective-permute-done.26.refs_8_), channel_id=1, source_target_pairs={{0,1},{1,0},{2,3},{3,2},{4,5},{5,4},{6,7},{7,6},{8,9},{9,8},{10,11... | collective-permute-start | bytes 1081352 | tf_op jit(solution)/shard_map/ppermute | solution.py:629
  149.0 10.2 %collective-permute-start.34 = (bf16[144,1024]{1,0:T(8,128)(2,1)}, bf16[144,1024]{1,0:T(8,128)(2,1)}, u32[]{:S(2)}, u32[]{:S(2)}) collective-permute-start(bf16[144,1024]{1,0:T(8,128)(2,1)} %get-tuple-element.124.rest_0_), channel_id=1, source_target_pairs={{0,2},{1,3},{2,0},{3,1},{4,6},{5,7},{6,4},{7,5},{8,10},{9,11},{10,... | collective-permute-start | bytes 884744 | tf_op jit(solution)/shard_map/ppermute | solution.py:629
  159.8 15.7 %collective-permute-start.39 = (bf16[4,32,2176]{2,1,0:T(8,128)(2,1)}, bf16[4,32,2176]{2,1,0:T(8,128)(2,1)S(1)}, u32[]{:S(2)}, u32[]{:S(2)}) collective-permute-start(bf16[4,32,2176]{2,1,0:T(8,128)(2,1)} %get-tuple-element.122), channel_id=1, source_target_pairs={{0,4},{1,5},{2,6},{3,7},{4,0},{5,1},{6,2},{7,3},{8,12},{9,13},{10,... | collective-permute-start | bytes 1671176 | tf_op jit(solution)/shard_map/ppermute | solution.py:629
  167.9 20.8 %collective-permute-start.37 = (bf16[128,1024]{1,0:T(8,128)(2,1)}, bf16[128,1024]{1,0:T(8,128)(2,1)}, u32[]{:S(2)}, u32[]{:S(2)}) collective-permute-start(bf16[128,1024]{1,0:T(8,128)(2,1)} %fusion.4), channel_id=1, source_target_pairs={{0,2},{1,3},{2,0},{3,1},{4,6},{5,7},{6,4},{7,5},{8,10},{9,11},{10,... | collective-permute-start | bytes 786440 | tf_op jit(solution)/shard_map/ppermute | solution.py:629
  168.9 12.2 %collective-permute-start.40 = (bf16[4,32,1152]{2,1,0:T(8,128)(2,1)S(1)}, bf16[4,32,1152]{2,1,0:T(8,128)(2,1)S(1)}, u32[]{:S(2)}, u32[]{:S(2)}) collective-permute-start(bf16[4,32,1152]{2,1,0:T(8,128)(2,1)S(1)} %copy-done.28), channel_id=1, source_target_pairs={{0,4},{1,5},{2,6},{3,7},{4,0},{5,1},{6,2},{7,3},{8,12},{9,13},{10,... | collective-permute-start | bytes 884744 | tf_op jit(solution)/shard_map/ppermute | solution.py:629
  182.7 23.3 %collective-permute-start.38 = (bf16[128,3072]{1,0:T(8,128)(2,1)S(1)}, bf16[128,3072]{1,0:T(8,128)(2,1)S(1)}, u32[]{:S(2)}, u32[]{:S(2)}) collective-permute-start(bf16[128,3072]{1,0:T(8,128)(2,1)S(1)} %constant_dynamic-slice_fusion), channel_id=1, source_target_pairs={{0,4},{1,5},{2,6},{3,7},{4,0},{5,1},{6,2},{7,3},{8,12},{9,13},{10,... | collective-permute-start | bytes 2359304 | tf_op jit(solution)/shard_map/ppermute | solution.py:629
  184.3 10.1 %collective-permute-start.43 = (bf16[32,3328]{1,0:T(8,128)(2,1)S(1)}, bf16[32,3328]{1,0:T(8,128)(2,1)S(1)}, u32[]{:S(2)}, u32[]{:S(2)}) collective-permute-start(bf16[32,3328]{1,0:T(8,128)(2,1)S(1)} %get-tuple-element.149), channel_id=1, source_target_pairs={{0,24},{1,25},{2,26},{3,27},{4,28},{5,29},{6,30},{7,31},{8,16},{9,... | collective-permute-start | bytes 638984 | tf_op jit(solution)/shard_map/ppermute | solution.py:629
  187.1 18.8 %collective-permute-start.42 = (bf16[32,3328]{1,0:T(8,128)(2,1)S(1)}, bf16[32,3328]{1,0:T(8,128)(2,1)S(1)}, u32[]{:S(2)}, u32[]{:S(2)}) collective-permute-start(bf16[32,3328]{1,0:T(8,128)(2,1)S(1)} %get-tuple-element.150), channel_id=1, source_target_pairs={{0,16},{1,17},{2,18},{3,19},{4,20},{5,21},{6,22},{7,23},{8,24},{9,... | collective-permute-start | bytes 638984 | tf_op jit(solution)/shard_map/ppermute | solution.py:629
  187.3 18.6 %collective-permute-start.41 = (bf16[32,3328]{1,0:T(8,128)(2,1)S(1)}, bf16[32,3328]{1,0:T(8,128)(2,1)S(1)}, u32[]{:S(2)}, u32[]{:S(2)}) collective-permute-start(bf16[32,3328]{1,0:T(8,128)(2,1)S(1)} %get-tuple-element.151), channel_id=1, source_target_pairs={{0,8},{1,9},{2,10},{3,11},{4,12},{5,13},{6,14},{7,15},{8,0},{9,1},... | collective-permute-start | bytes 638984 | tf_op jit(solution)/shard_map/ppermute | solution.py:629
  (42 other events, 292.6 us)
Sparse Core Ops, SparseCore 0:
  71.1 110.2 reduce-scatter.1

commit v3 on v2

--- a/solution.py
+++ b/solution.py
@@ -367,19 +367,21 @@
         down_ref[e, :fh, :] = first[:, at : at + fh].T
         down_ref[e, fh:, :] = second[:, at : at + fh].T
     early, late = early_ref[0], late_ref[0]
+    late_kv = late[:, : 2 * wk_ref.shape[1]]
     for d in dense:
         early = early + d[:, :n_early].astype(jnp.float32)
-        late = late + d[:, n_early:].astype(jnp.float32)
+        late_kv = late_kv + d[:, n_early:].astype(jnp.float32)
     width, k_cols = wo_ref.shape[1], wk_ref.shape[1]
     wo_ref[...] = early[:, :width]
     wq_ref[...] = early[:, width + LANES :]
-    wk_ref[...] = late[:, :k_cols]
-    wv_ref[...] = late[:, k_cols : 2 * k_cols]
-    small = early[:, width : width + LANES]
+    wk_ref[...] = late_kv[:, :k_cols]
+    wv_ref[...] = late_kv[:, k_cols:]
+    small = early[:, width : width + LANES] + late[:, 2 * k_cols :]
     small = small.T
     router_ref[...] = small[1 : 1 + router_ref.shape[0], :]
     two_ref[...] = small[:1, :]
-    one_ref[...] = late[:, 2 * k_cols :].T[:1, :]
+    one = 1 + router_ref.shape[0]
+    one_ref[...] = small[one : one + 1, :]
 
 
 def selection(info_ref, select_ref, own_rows):
@@ -433,14 +435,15 @@
     put_shares(dot(normed_t, seq(query)), odd_ref, even_ref, width + LANES)
 
 
-def late_dense_kernel(info_ref, normed_t_ref, *rest):
+def late_dense_kernel(info_ref, normed_t_ref, *rest, lane):
     blocks = rest[:-3]
     odd_ref, even_ref, select_ref = rest[-3:]
     rows = normed_t_ref.shape[1] // len(blocks)
     selection(info_ref, select_ref, odd_ref.shape[1])
     kv = jnp.concatenate([b[:rows] for b in blocks], axis=0)
     put_shares(dot(normed_t_ref[...], kv), odd_ref, even_ref, 0)
-    put_shares(pick_small(blocks, rows, 1, select_ref[...]), odd_ref, even_ref, kv.shape[1])
+    small = pltpu.roll(pick_small(blocks, rows, 1, select_ref[...]), lane, 1)
+    put_shares(small, odd_ref, even_ref, kv.shape[1])
 
 
 def small_rows(count):
@@ -862,7 +865,7 @@
     _, *kv_even_blocks = lax.optimization_barrier((early_odd, *kv_even_blocks))
     kv_blocks = gather_odd(kv_even_blocks)
     late_odd, late_even = call(
-        late_dense_kernel,
+        lambda *refs: late_dense_kernel(*refs, lane=experts + 1),
         (shape(outer, own_rows, n_late), shape(outer, own_rows, n_late, dtype=f32)),
         "dense_late",
         scratch=(select,),
@@ -874,7 +877,16 @@
         mixture = mixture + a.astype(f32)
     block_out = (hidden_state + mixture).astype(low)
     late = late_even + send(late_odd, 1, 0).astype(f32)
-    dense_send = jnp.concatenate([early[1:].astype(low), late[1:].astype(low)], axis=2)
+    o_end, k_end = model_width + LANES, 2 * KV * HD
+    dense_send = jnp.concatenate(
+        [
+            early[1:, :, :model_width],
+            early[1:, :, model_width:o_end] + late[1:, :, k_end:],
+            early[1:, :, o_end:],
+            late[1:, :, :k_end],
+        ],
+        axis=2,
+    ).astype(low)
 
     swapped = send(
         lax.dynamic_slice_in_dim(reduced, (1 - half) * shard_rows, shard_rows, 0), 1, 0

time: 216 us -> 215 us (level)
    unnamed x59 -> x61, local copies, waits for them, and re-layouts: 5.73 us -> 5.62 us
  transfers between devices with their start and end apart: 45 -> 45, of which waited for: 26 -> 25; matrix products, arithmetic and copies ran while one was open for 8% -> 8% of each run, Pallas kernels for 22% -> 22%
where the time goes in v3:
time: 215 us
  waiting for transfers between devices  75.2 us (35%)
  Pallas kernels  68.8 us (32%)
  starting transfers between devices  32.6 us (15%)
  between operations  15.1 us (7%)
  other arithmetic  13.4 us (6%)
  local copies, waits for them, and re-layouts  9.62 us (4%)
    ppermute x44, waiting for transfers between devices, send(): lax.ppermute(block, ('dp', 'expert'), [(i * groups + j, (i ^ pair_flip) *...  75.2 us
    pallas_call x8, Pallas kernels, run(): pl.pallas_call(kernel, out_shape=out_shape, in_specs=specs, out_specs=[pl...  68.8 us
    ppermute x44, starting transfers between devices, send(): lax.ppermute(block, ('dp', 'expert'), [(i * groups + j, (i ^ pair_flip) *...  32.5 us
    unnamed x61, local copies, waits for them, and re-layouts  5.62 us
  transfers between devices with their start and end apart: 45, of which 25 were waited for; matrix products, arithmetic and copies ran while one was open for 8% of the time, Pallas kernels for 22%

profile of v3, /device:TPU:0, one launch (start us, length us, event | category | flops | bytes accessed | tf_op | source)
XLA Modules:
  0.0 214.7 jit_solution(368338181269762669)
XLA Ops:
  7.2 3.0 %collective-permute-start = (bf16[128,1024]{1,0:T(8,128)(2,1)}, bf16[128,1024]{1,0:T(8,128)(2,1)S(1)}, u32[]{:S(2)}, u32[]{:S(2)}) collective-permute-start(bf16[128,1024]{1,0:T(8,128)(2,1)} %tokens_ref.1), channel_id=1, source_target_pairs={{0,2},{1,3},{2,0},{3,1},{4,6},{5,7},{6,4},{7,5},{8,10},{9,11},{10,... | collective-permute-start | bytes 786440 | tf_op jit(solution)/shard_map/ppermute | solution.py:632
  12.1 1.6 collective-permute-start.4
  13.7 2.6 %negate_select_fusion = (f32[512,128]{1,0:T(8,128)}, f32[512,128]{1,0:T(8,128)}) fusion(s32[128]{0:T(128)S(1)} %get-tuple-element.166, s32[128]{0:T(128)S(1)} %get-tuple-element.168, s32[128]{0:T(128)S(1)} %get-tuple-element.167, s32[128]{0:T(128)S(1)} %get-tuple-element.169, s32[512]{0:T(512)S(1)} %get-tuple-element.159, s32[512]{0:T(512)S(1)} %get-tuple-element.160, ...), kind=kLoop, calls=%fused_computation.16 | loop fusion | flops 917504 | bytes 535812 | tf_op jit(solution)/shard_map/jit(_where)/select_n | solution.py:26
  16.8 2.7 %collective-permute-start.5 = (bf16[128,1152]{1,0:T(8,128)(2,1)S(1)}, bf16[128,1152]{1,0:T(8,128)(2,1)}, u32[]{:S(2)}, u32[]{:S(2)}) collective-permute-start(bf16[128,1152]{1,0:T(8,128)(2,1)S(1)} %pad_maximum_fusion.1.refs_5_.refs_2_), channel_id=1, source_target_pairs={{0,6},{1,7},{2,4},{3,5},{4,2},{5,3},{6,0},{7,1},{8,14},{9,15},{10,... | collective-permute-start | bytes 884744 | tf_op jit(solution)/shard_map/ppermute | solution.py:632
  22.6 8.2 %attention_forward.1 = (bf16[128,1024]{1,0:T(8,128)(2,1)}, bf16[8,512,128]{2,1,0:T(8,128)(2,1)}, bf16[8,512,128]{2,1,0:T(8,128)(2,1)}, f32[8,256]{1,0:T(8,128)},...) custom-call(s32[4]{0:T(128)} %pad_add_fusion.info_ref.refs_0_, ...), custom_call_target="tpu_custom_call" | custom-call | tf_op jit(solution)/shard_map/attention_forward/pallas_call | solution.py:583
  30.8 2.1 collective-permute-done.3.refs_7_
  36.9 6.3 %collective-permute-done.15.refs_19_ = bf16[128,1024]{1,0:T(8,128)(2,1)S(1)} collective-permute-done((bf16[128,1024]{1,0:T(8,128)(2,1)}, bf16[128,1024]{1,0:T(8,128)(2,1)S(1)}, u32[]{:S(2)}, u32[]{:S(2)}) %collective-permute-start.15) | collective-permute-done | bytes 262176 | tf_op jit(solution)/shard_map/ppermute | solution.py:632
  43.3 3.1 %collective-permute-done.13.refs_17_ = bf16[128,1024]{1,0:T(8,128)(2,1)S(1)} collective-permute-done((bf16[128,1024]{1,0:T(8,128)(2,1)}, bf16[128,1024]{1,0:T(8,128)(2,1)S(1)}, u32[]{:S(2)}, u32[]{:S(2)}) %collective-permute-start.13) | collective-permute-done | bytes 262176 | tf_op jit(solution)/shard_map/ppermute | solution.py:632
  51.5 19.5 %experts.1 = (bf16[1024,3072]{1,0:T(8,128)(2,1)}, bf16[4,1024,896]{2,1,0:T(8,128)(2,1)}) custom-call(s32[4]{0:T(128)S(1)} %copy-done.4, bf16[1024,16]{1,0:T(8,128)(2,1)S(1)} %copy.30.refs_1_.refs_5_, bf16[4,1024,512]{2,1,0:T(8,128)(2,1)} %wg_ref.1, bf16[4,1024,512]{2,1,0:T(8,128)(2,1)} %wu_ref.1, bf16[4,512,1024]{2,1,0:T(8,128)(2,1)} %refs_16_.1, ...), custom_call_target="tpu_custom_call" | custom-call | tf_op jit(solution)/shard_map/experts/pallas_call | solution.py:583
  72.1 10.3 %experts_rows.1 = (bf16[4,128,1152]{2,1,0:T(8,128)(2,1)}, f32[4,128,1152]{2,1,0:T(8,128)}) custom-call(s32[4]{0:T(128)} %pad_add_fusion.info_ref.refs_0_, bf16[4,1024,512]{2,1,0:T(8,128)(2,1)} %wg_ref.1, bf16[4,1024,512]{2,1,0:T(8,128)(2,1)} %wu_ref.1, bf16[4,1024,896]{2,1,0:T(8,128)(2,1)} %get-tuple-element.90.acts_in.refs_15_), custom_call_target="tpu_custom_call" | custom-call | tf_op jit(solution)/shard_map/experts_rows/pallas_call | solution.py:583
  82.5 3.0 %collective-permute-done.18 = bf16[4,128,1152]{2,1,0:T(8,128)(2,1)S(1)} collective-permute-done((bf16[4,128,1152]{2,1,0:T(8,128)(2,1)}, bf16[4,128,1152]{2,1,0:T(8,128)(2,1)S(1)}, u32[]{:S(2)}, u32[]{:S(2)}) %collective-permute-start.18) | collective-permute-done | bytes 1179680 | tf_op jit(solution)/shard_map/ppermute | solution.py:632
  85.6 2.0 fusion.15
  88.2 2.0 collective-permute-start.20
  92.1 6.4 %collective-permute-done.21.refs_19_ = bf16[128,1152]{1,0:T(8,128)(2,1)S(1)} collective-permute-done((bf16[128,1152]{1,0:T(8,128)(2,1)S(1)}, bf16[128,1152]{1,0:T(8,128)(2,1)S(1)}, u32[]{:S(2)}, u32[]{:S(2)}) %collective-permute-start.21) | collective-permute-done | bytes 294944 | tf_op jit(solution)/shard_map/ppermute | solution.py:632
  98.5 5.0 %collective-permute-done.20.refs_18_ = bf16[128,1152]{1,0:T(8,128)(2,1)S(1)} collective-permute-done((bf16[128,1152]{1,0:T(8,128)(2,1)S(1)}, bf16[128,1152]{1,0:T(8,128)(2,1)S(1)}, u32[]{:S(2)}, u32[]{:S(2)}) %collective-permute-start.20) | collective-permute-done | bytes 294944 | tf_op jit(solution)/shard_map/ppermute | solution.py:632
  104.7 15.6 %attention_backward.1 = (f32[128,1024]{1,0:T(8,128)}, bf16[176,1024]{1,0:T(8,128)(2,1)}, bf16[128,1024]{1,0:T(8,128)(2,1)}, bf16[2,128,1024]{2,1,0:T(8,128)(2,1)...) custom-call(s32[4]{0:T(128)} %pad_add_fusion.info_ref.refs_0_, ...), custom_call_target="tpu_custom_call" | custom-call | tf_op jit(solution)/shard_map/attention_backward/pallas_call | solution.py:583
  120.4 2.1 collective-permute-done.22
  122.5 1.5 convert_add_fusion.3
  125.3 1.6 collective-permute-done.23
  128.1 4.8 %collective-permute-done.24.rest_0_ = bf16[128,1024]{1,0:T(8,128)(2,1)S(1)} collective-permute-done((bf16[128,1024]{1,0:T(8,128)(2,1)S(1)}, bf16[128,1024]{1,0:T(8,128)(2,1)S(1)}, u32[]{:S(2)}, u32[]{:S(2)}) %collective-permute-start.24) | collective-permute-done | bytes 262176 | tf_op jit(solution)/shard_map/ppermute | solution.py:632
  136.3 4.1 %tokens_backward.1 = (bf16[144,1024]{1,0:T(8,128)(2,1)}, bf16[128,1024]{1,0:T(8,128)(2,1)}) custom-call(f32[128,1024]{1,0:T(8,128)} %slice_bitcast_fusion.2.own_ref, f32[128,1024]{1,0:T(8,128)} %get-tuple-element.105.gn_ref, bf16[1024,512]{1,0:T(8,128)(2,1)} %wk_ref.3, bf16[1024,512]{1,0:T(8,128)(2,1)} %wv_ref.3, bf16[128,1024]{1,0:T(8,128)(2,1)} %tokens_ref.1, ...), custom_call_target="tpu_custom_call" | custom-call | tf_op jit(solution)/shard_map/tokens_backward/pallas_call | solution.py:583
  140.4 8.2 %collective-permute-done.27.refs_12_ = bf16[128,1024]{1,0:T(8,128)(2,1)} collective-permute-done((bf16[128,1024]{1,0:T(8,128)(2,1)}, bf16[128,1024]{1,0:T(8,128)(2,1)}, u32[]{:S(2)}, u32[]{:S(2)}) %collective-permute-start.27) | collective-permute-done | bytes 262176 | tf_op jit(solution)/shard_map/ppermute | solution.py:632
  153.9 5.5 %dense_early.1 = (bf16[4,32,2176]{2,1,0:T(8,128)(2,1)}, f32[4,32,2176]{2,1,0:T(8,128)}, bf16[256,512]{1,0:T(8,128)(2,1)}) custom-call(s32[4]{0:T(128)} %pad_add_fusion.info_ref.refs_0_, bf16[512,1024]{1,0:T(8,128)(2,1)} %get-tuple-element.114.refs_1_, bf16[128,1024]{1,0:T(8,128)(2,1)} %get-tuple-element.115.refs_2_, ...), custom_call_target="tpu_custom_call" | custom-call | tf_op jit(solution)/shard_map/dense_early/pallas_call | solution.py:583
  162.5 3.0 %dense_late.1 = (bf16[4,32,1152]{2,1,0:T(8,128)(2,1)}, f32[4,32,1152]{2,1,0:T(8,128)}) custom-call(s32[4]{0:T(128)} %pad_add_fusion.info_ref.refs_0_, bf16[256,512]{1,0:T(8,128)(2,1)} %get-tuple-element.121.refs_1_, bf16[144,1024]{1,0:T(8,128)(2,1)} %get-tuple-element.124.refs_2_, bf16[144,1024]{1,0:T(8,128)(2,1)} %copy-done.17, ...), custom_call_target="tpu_custom_call" | custom-call | tf_op jit(solution)/shard_map/dense_late/pallas_call | solution.py:583
  165.5 1.8 convert_add_fusion.2
  170.0 5.6 %collective-permute-done.39 = bf16[4,32,2176]{2,1,0:T(8,128)(2,1)S(1)} collective-permute-done((bf16[4,32,2176]{2,1,0:T(8,128)(2,1)}, bf16[4,32,2176]{2,1,0:T(8,128)(2,1)S(1)}, u32[]{:S(2)}, u32[]{:S(2)}) %collective-permute-start.39) | collective-permute-done | bytes 557088 | tf_op jit(solution)/shard_map/ppermute | solution.py:632
  175.8 5.4 %collective-permute-done.40 = bf16[4,32,1152]{2,1,0:T(8,128)(2,1)S(1)} collective-permute-done((bf16[4,32,1152]{2,1,0:T(8,128)(2,1)S(1)}, bf16[4,32,1152]{2,1,0:T(8,128)(2,1)S(1)}, u32[]{:S(2)}, u32[]{:S(2)}) %collective-permute-start.40) | collective-permute-done | bytes 294944 | tf_op jit(solution)/shard_map/ppermute | solution.py:632
  184.2 2.9 %collective-permute-start.43 = (bf16[32,3200]{1,0:T(8,128)(2,1)S(1)}, bf16[32,3200]{1,0:T(8,128)(2,1)S(1)}, u32[]{:S(2)}, u32[]{:S(2)}) collective-permute-start(bf16[32,3200]{1,0:T(8,128)(2,1)S(1)} %get-tuple-element.151), channel_id=1, source_target_pairs={{0,24},{1,25},{2,26},{3,27},{4,28},{5,29},{6,30},{7,31},{8,16},{9,... | collective-permute-start | bytes 614408 | tf_op jit(solution)/shard_map/ppermute | solution.py:632
  188.7 1.8 fusion.2
  190.4 3.7 %collective-permute-done.43.refs_7_ = bf16[32,3200]{1,0:T(8,128)(2,1)S(1)} collective-permute-done((bf16[32,3200]{1,0:T(8,128)(2,1)S(1)}, bf16[32,3200]{1,0:T(8,128)(2,1)S(1)}, u32[]{:S(2)}, u32[]{:S(2)}) %collective-permute-start.43) | collective-permute-done | bytes 204832 | tf_op jit(solution)/shard_map/ppermute | solution.py:632
  194.2 11.0 %collective-permute-done.42.refs_6_ = bf16[32,3200]{1,0:T(8,128)(2,1)S(1)} collective-permute-done((bf16[32,3200]{1,0:T(8,128)(2,1)S(1)}, bf16[32,3200]{1,0:T(8,128)(2,1)S(1)}, u32[]{:S(2)}, u32[]{:S(2)}) %collective-permute-start.42) | collective-permute-done | bytes 204832 | tf_op jit(solution)/shard_map/ppermute | solution.py:632
  205.2 2.6 %place.1 = (f32[4,128,512]{2,1,0:T(8,128)}, f32[4,128,512]{2,1,0:T(8,128)}, f32[4,512,128]{2,1,0:T(8,128)}, f32[32,1024]{1,0:T(8,128)}, f32[32,512]{1,0:T(8,128)...) custom-call(s32[4]{0:T(128)S(1)} %copy-done.5, ...), custom_call_target="tpu_custom_call" | custom-call | tf_op jit(solution)/shard_map/place/pallas_call | solution.py:583
  (158 shorter events, 40.3 us)
Async XLA Ops:
  7.2 174.2 %reduce-scatter.2.cloned.1.call-start = ((), (), s32[]{:S(2)}) async-start(), calls=%async_computation.1 | async-start | bytes 7864320 | tf_op jit(solution)/shard_map/reduce_scatter | solution.py:756
  7.2 9.6 %collective-permute-start = (bf16[128,1024]{1,0:T(8,128)(2,1)}, bf16[128,1024]{1,0:T(8,128)(2,1)S(1)}, u32[]{:S(2)}, u32[]{:S(2)}) collective-permute-start(bf16[128,1024]{1,0:T(8,128)(2,1)} %tokens_ref.1), channel_id=1, source_target_pairs={{0,2},{1,3},{2,0},{3,1},{4,6},{5,7},{6,4},{7,5},{8,10},{9,11},{10,... | collective-permute-start | bytes 786440 | tf_op jit(solution)/shard_map/ppermute | solution.py:632
  12.1 18.7 %collective-permute-start.4 = (bf16[128,1152]{1,0:T(8,128)(2,1)S(1)}, bf16[128,1152]{1,0:T(8,128)(2,1)S(1)}, u32[]{:S(2)}, u32[]{:S(2)}) collective-permute-start(bf16[128,1152]{1,0:T(8,128)(2,1)S(1)} %pad_maximum_fusion.1.refs_5_.refs_2_), channel_id=1, source_target_pairs={{0,4},{1,5},{2,6},{3,7},{4,0},{5,1},{6,2},{7,3},{8,12},{9,13},{10,... | collective-permute-start | bytes 884744 | tf_op jit(solution)/shard_map/ppermute | solution.py:632
  16.8 14.0 %collective-permute-start.5 = (bf16[128,1152]{1,0:T(8,128)(2,1)S(1)}, bf16[128,1152]{1,0:T(8,128)(2,1)}, u32[]{:S(2)}, u32[]{:S(2)}) collective-permute-start(bf16[128,1152]{1,0:T(8,128)(2,1)S(1)} %pad_maximum_fusion.1.refs_5_.refs_2_), channel_id=1, source_target_pairs={{0,6},{1,7},{2,4},{3,5},{4,2},{5,3},{6,0},{7,1},{8,14},{9,15},{10,... | collective-permute-start | bytes 884744 | tf_op jit(solution)/shard_map/ppermute | solution.py:632
  19.5 13.5 %collective-permute-start.3 = (bf16[128,1152]{1,0:T(8,128)(2,1)S(1)}, bf16[128,1152]{1,0:T(8,128)(2,1)}, u32[]{:S(2)}, u32[]{:S(2)}) collective-permute-start(bf16[128,1152]{1,0:T(8,128)(2,1)S(1)} %pad_maximum_fusion.1.refs_5_.refs_2_), channel_id=1, source_target_pairs={{0,2},{1,3},{2,0},{3,1},{4,6},{5,7},{6,4},{7,5},{8,10},{9,11},{10,... | collective-permute-start | bytes 884744 | tf_op jit(solution)/shard_map/ppermute | solution.py:632
  32.9 10.3 %collective-permute-start.15 = (bf16[128,1024]{1,0:T(8,128)(2,1)}, bf16[128,1024]{1,0:T(8,128)(2,1)S(1)}, u32[]{:S(2)}, u32[]{:S(2)}) collective-permute-start(bf16[128,1024]{1,0:T(8,128)(2,1)} %get-tuple-element.89.refs_13_.refs_3_), channel_id=1, source_target_pairs={{0,6},{1,7},{2,4},{3,5},{4,2},{5,3},{6,0},{7,1},{8,14},{9,15},{10,... | collective-permute-start | bytes 786440 | tf_op jit(solution)/shard_map/ppermute | solution.py:632
  34.1 12.3 %collective-permute-start.13 = (bf16[128,1024]{1,0:T(8,128)(2,1)}, bf16[128,1024]{1,0:T(8,128)(2,1)S(1)}, u32[]{:S(2)}, u32[]{:S(2)}) collective-permute-start(bf16[128,1024]{1,0:T(8,128)(2,1)} %get-tuple-element.89.refs_13_.refs_3_), channel_id=1, source_target_pairs={{0,4},{1,5},{2,6},{3,7},{4,0},{5,1},{6,2},{7,3},{8,12},{9,13},{10,... | collective-permute-start | bytes 786440 | tf_op jit(solution)/shard_map/ppermute | solution.py:632
  35.4 12.3 %collective-permute-start.11 = (bf16[128,1024]{1,0:T(8,128)(2,1)}, bf16[128,1024]{1,0:T(8,128)(2,1)S(1)}, u32[]{:S(2)}, u32[]{:S(2)}) collective-permute-start(bf16[128,1024]{1,0:T(8,128)(2,1)} %get-tuple-element.89.refs_13_.refs_3_), channel_id=1, source_target_pairs={{0,2},{1,3},{2,0},{3,1},{4,6},{5,7},{6,4},{7,5},{8,10},{9,11},{10,... | collective-permute-start | bytes 786440 | tf_op jit(solution)/shard_map/ppermute | solution.py:632
  36.4 11.8 %collective-permute-start.6 = (bf16[128,1152]{1,0:T(8,128)(2,1)S(1)}, bf16[128,1152]{1,0:T(8,128)(2,1)S(1)}, u32[]{:S(2)}, u32[]{:S(2)}) collective-permute-start(bf16[128,1152]{1,0:T(8,128)(2,1)S(1)} %pad_maximum_fusion.1.refs_5_.refs_2_), channel_id=1, source_target_pairs={{0,1},{1,0},{2,3},{3,2},{4,5},{5,4},{6,7},{7,6},{8,9},{9,8},{10,11... | collective-permute-start | bytes 884744 | tf_op jit(solution)/shard_map/ppermute | solution.py:632
  36.4 11.9 %collective-permute-start.7 = (bf16[128,1152]{1,0:T(8,128)(2,1)}, bf16[128,1152]{1,0:T(8,128)(2,1)S(1)}, u32[]{:S(2)}, u32[]{:S(2)}) collective-permute-start(bf16[128,1152]{1,0:T(8,128)(2,1)} %collective-permute-done.3.refs_7_), channel_id=1, source_target_pairs={{0,1},{1,0},{2,3},{3,2},{4,5},{5,4},{6,7},{7,6},{8,9},{9,8},{10,11... | collective-permute-start | bytes 884744 | tf_op jit(solution)/shard_map/ppermute | solution.py:632
  43.3 4.4 %collective-permute-start.10 = (bf16[128,1024]{1,0:T(8,128)(2,1)}, bf16[128,1024]{1,0:T(8,128)(2,1)S(1)}, u32[]{:S(2)}, u32[]{:S(2)}) collective-permute-start(bf16[128,1024]{1,0:T(8,128)(2,1)} %get-tuple-element.89.refs_13_.refs_3_), channel_id=1, source_target_pairs={{0,1},{1,0},{2,3},{3,2},{4,5},{5,4},{6,7},{7,6},{8,9},{9,8},{10,11... | collective-permute-start | bytes 786440 | tf_op jit(solution)/shard_map/ppermute | solution.py:632
  71.0 11.4 %collective-permute-start.17 = (bf16[128,1024]{1,0:T(8,128)(2,1)}, bf16[128,1024]{1,0:T(8,128)(2,1)}, u32[]{:S(2)}, u32[]{:S(2)}) collective-permute-start(bf16[128,1024]{1,0:T(8,128)(2,1)} %get-tuple-element.115.refs_2_), channel_id=1, source_target_pairs={{0,2},{1,3},{2,0},{3,1},{4,6},{5,7},{6,4},{7,5},{8,10},{9,11},{10,... | collective-permute-start | bytes 786440 | tf_op jit(solution)/shard_map/ppermute | solution.py:632
  82.4 3.1 %collective-permute-start.18 = (bf16[4,128,1152]{2,1,0:T(8,128)(2,1)}, bf16[4,128,1152]{2,1,0:T(8,128)(2,1)S(1)}, u32[]{:S(2)}, u32[]{:S(2)}) collective-permute-start(bf16[4,128,1152]{2,1,0:T(8,128)(2,1)} %get-tuple-element.94), channel_id=1, source_target_pairs={{0,1},{1,0},{2,3},{3,2},{4,5},{5,4},{6,7},{7,6},{8,9},{9,8},{10,11... | collective-permute-start | bytes 3538952 | tf_op jit(solution)/shard_map/ppermute | solution.py:632
  87.7 10.9 %collective-permute-start.21 = (bf16[128,1152]{1,0:T(8,128)(2,1)S(1)}, bf16[128,1152]{1,0:T(8,128)(2,1)S(1)}, u32[]{:S(2)}, u32[]{:S(2)}) collective-permute-start(bf16[128,1152]{1,0:T(8,128)(2,1)S(1)} %get-tuple-element.148), channel_id=1, source_target_pairs={{0,6},{1,7},{2,4},{3,5},{4,2},{5,3},{6,0},{7,1},{8,14},{9,15},{10,... | collective-permute-start | bytes 884744 | tf_op jit(solution)/shard_map/ppermute | solution.py:632
  88.2 15.4 %collective-permute-start.20 = (bf16[128,1152]{1,0:T(8,128)(2,1)S(1)}, bf16[128,1152]{1,0:T(8,128)(2,1)S(1)}, u32[]{:S(2)}, u32[]{:S(2)}) collective-permute-start(bf16[128,1152]{1,0:T(8,128)(2,1)S(1)} %get-tuple-element.149), channel_id=1, source_target_pairs={{0,4},{1,5},{2,6},{3,7},{4,0},{5,1},{6,2},{7,3},{8,12},{9,13},{10,... | collective-permute-start | bytes 884744 | tf_op jit(solution)/shard_map/ppermute | solution.py:632
  90.2 13.8 %collective-permute-start.19 = (bf16[128,1152]{1,0:T(8,128)(2,1)S(1)}, bf16[128,1152]{1,0:T(8,128)(2,1)S(1)}, u32[]{:S(2)}, u32[]{:S(2)}) collective-permute-start(bf16[128,1152]{1,0:T(8,128)(2,1)S(1)} %get-tuple-element.150), channel_id=1, source_target_pairs={{0,2},{1,3},{2,0},{3,1},{4,6},{5,7},{6,4},{7,5},{8,10},{9,11},{10,... | collective-permute-start | bytes 884744 | tf_op jit(solution)/shard_map/ppermute | solution.py:632
  124.2 8.7 %collective-permute-start.24 = (bf16[128,1024]{1,0:T(8,128)(2,1)S(1)}, bf16[128,1024]{1,0:T(8,128)(2,1)S(1)}, u32[]{:S(2)}, u32[]{:S(2)}) collective-permute-start(bf16[128,1024]{1,0:T(8,128)(2,1)S(1)} %fusion.3), channel_id=1, source_target_pairs={{0,2},{1,3},{2,0},{3,1},{4,6},{5,7},{6,4},{7,5},{8,10},{9,11},{10,... | collective-permute-start | bytes 786440 | tf_op jit(solution)/shard_map/ppermute | solution.py:632
  128.0 20.6 %collective-permute-start.25 = (bf16[2,128,1024]{2,1,0:T(8,128)(2,1)}, bf16[2,128,1024]{2,1,0:T(8,128)(2,1)S(1)}, u32[]{:S(2)}, u32[]{:S(2)}) collective-permute-start(bf16[2,128,1024]{2,1,0:T(8,128)(2,1)} %add_convert_fusion), channel_id=1, source_target_pairs={{0,4},{1,5},{2,6},{3,7},{4,0},{5,1},{6,2},{7,3},{8,12},{9,13},{10,... | collective-permute-start | bytes 1572872 | tf_op jit(solution)/shard_map/ppermute | solution.py:632
  132.9 15.7 %collective-permute-start.26 = (bf16[176,1024]{1,0:T(8,128)(2,1)S(1)}, bf16[176,1024]{1,0:T(8,128)(2,1)}, u32[]{:S(2)}, u32[]{:S(2)}) collective-permute-start(bf16[176,1024]{1,0:T(8,128)(2,1)S(1)} %copy-done.13), channel_id=1, source_target_pairs={{0,2},{1,3},{2,0},{3,1},{4,6},{5,7},{6,4},{7,5},{8,10},{9,11},{10,... | collective-permute-start | bytes 1081352 | tf_op jit(solution)/shard_map/ppermute | solution.py:632
  133.9 14.7 %collective-permute-start.27 = (bf16[128,1024]{1,0:T(8,128)(2,1)}, bf16[128,1024]{1,0:T(8,128)(2,1)}, u32[]{:S(2)}, u32[]{:S(2)}) collective-permute-start(bf16[128,1024]{1,0:T(8,128)(2,1)} %get-tuple-element.119.refs_10_), channel_id=1, source_target_pairs={{0,2},{1,3},{2,0},{3,1},{4,6},{5,7},{6,4},{7,5},{8,10},{9,11},{10,... | collective-permute-start | bytes 786440 | tf_op jit(solution)/shard_map/ppermute | solution.py:632
  134.9 15.2 %collective-permute-start.28 = (bf16[128,1024]{1,0:T(8,128)(2,1)}, bf16[128,1024]{1,0:T(8,128)(2,1)}, u32[]{:S(2)}, u32[]{:S(2)}) collective-permute-start(bf16[128,1024]{1,0:T(8,128)(2,1)} %get-tuple-element.115.refs_2_), channel_id=1, source_target_pairs={{0,1},{1,0},{2,3},{3,2},{4,5},{5,4},{6,7},{7,6},{8,9},{9,8},{10,11... | collective-permute-start | bytes 786440 | tf_op jit(solution)/shard_map/ppermute | solution.py:632
  134.9 15.2 %collective-permute-start.29 = (bf16[128,1024]{1,0:T(8,128)(2,1)}, bf16[128,1024]{1,0:T(8,128)(2,1)}, u32[]{:S(2)}, u32[]{:S(2)}) collective-permute-start(bf16[128,1024]{1,0:T(8,128)(2,1)} %collective-permute-done.17.refs_4_), channel_id=1, source_target_pairs={{0,1},{1,0},{2,3},{3,2},{4,5},{5,4},{6,7},{7,6},{8,9},{9,8},{10,11... | collective-permute-start | bytes 786440 | tf_op jit(solution)/shard_map/ppermute | solution.py:632
  148.6 3.7 %collective-permute-start.30 = (bf16[176,1024]{1,0:T(8,128)(2,1)S(1)}, bf16[176,1024]{1,0:T(8,128)(2,1)S(1)}, u32[]{:S(2)}, u32[]{:S(2)}) collective-permute-start(bf16[176,1024]{1,0:T(8,128)(2,1)S(1)} %copy-done.13), channel_id=1, source_target_pairs={{0,1},{1,0},{2,3},{3,2},{4,5},{5,4},{6,7},{7,6},{8,9},{9,8},{10,11... | collective-permute-start | bytes 1081352 | tf_op jit(solution)/shard_map/ppermute | solution.py:632
  148.7 4.4 %collective-permute-start.31 = (bf16[176,1024]{1,0:T(8,128)(2,1)}, bf16[176,1024]{1,0:T(8,128)(2,1)S(1)}, u32[]{:S(2)}, u32[]{:S(2)}) collective-permute-start(bf16[176,1024]{1,0:T(8,128)(2,1)} %collective-permute-done.26.refs_8_), channel_id=1, source_target_pairs={{0,1},{1,0},{2,3},{3,2},{4,5},{5,4},{6,7},{7,6},{8,9},{9,8},{10,11... | collective-permute-start | bytes 1081352 | tf_op jit(solution)/shard_map/ppermute | solution.py:632
  149.2 10.2 %collective-permute-start.34 = (bf16[144,1024]{1,0:T(8,128)(2,1)}, bf16[144,1024]{1,0:T(8,128)(2,1)}, u32[]{:S(2)}, u32[]{:S(2)}) collective-permute-start(bf16[144,1024]{1,0:T(8,128)(2,1)} %get-tuple-element.124.refs_2_), channel_id=1, source_target_pairs={{0,2},{1,3},{2,0},{3,1},{4,6},{5,7},{6,4},{7,5},{8,10},{9,11},{10,... | collective-permute-start | bytes 884744 | tf_op jit(solution)/shard_map/ppermute | solution.py:632
  159.9 15.7 %collective-permute-start.39 = (bf16[4,32,2176]{2,1,0:T(8,128)(2,1)}, bf16[4,32,2176]{2,1,0:T(8,128)(2,1)S(1)}, u32[]{:S(2)}, u32[]{:S(2)}) collective-permute-start(bf16[4,32,2176]{2,1,0:T(8,128)(2,1)} %get-tuple-element.122), channel_id=1, source_target_pairs={{0,4},{1,5},{2,6},{3,7},{4,0},{5,1},{6,2},{7,3},{8,12},{9,13},{10,... | collective-permute-start | bytes 1671176 | tf_op jit(solution)/shard_map/ppermute | solution.py:632
  168.1 20.6 %collective-permute-start.37 = (bf16[128,1024]{1,0:T(8,128)(2,1)}, bf16[128,1024]{1,0:T(8,128)(2,1)}, u32[]{:S(2)}, u32[]{:S(2)}) collective-permute-start(bf16[128,1024]{1,0:T(8,128)(2,1)} %fusion.4), channel_id=1, source_target_pairs={{0,2},{1,3},{2,0},{3,1},{4,6},{5,7},{6,4},{7,5},{8,10},{9,11},{10,... | collective-permute-start | bytes 786440 | tf_op jit(solution)/shard_map/ppermute | solution.py:632
  169.1 12.1 %collective-permute-start.40 = (bf16[4,32,1152]{2,1,0:T(8,128)(2,1)S(1)}, bf16[4,32,1152]{2,1,0:T(8,128)(2,1)S(1)}, u32[]{:S(2)}, u32[]{:S(2)}) collective-permute-start(bf16[4,32,1152]{2,1,0:T(8,128)(2,1)S(1)} %copy-done.29), channel_id=1, source_target_pairs={{0,4},{1,5},{2,6},{3,7},{4,0},{5,1},{6,2},{7,3},{8,12},{9,13},{10,... | collective-permute-start | bytes 884744 | tf_op jit(solution)/shard_map/ppermute | solution.py:632
  182.7 22.5 %collective-permute-start.38 = (bf16[128,3072]{1,0:T(8,128)(2,1)S(1)}, bf16[128,3072]{1,0:T(8,128)(2,1)S(1)}, u32[]{:S(2)}, u32[]{:S(2)}) collective-permute-start(bf16[128,3072]{1,0:T(8,128)(2,1)S(1)} %constant_dynamic-slice_fusion), channel_id=1, source_target_pairs={{0,4},{1,5},{2,6},{3,7},{4,0},{5,1},{6,2},{7,3},{8,12},{9,13},{10,... | collective-permute-start | bytes 2359304 | tf_op jit(solution)/shard_map/ppermute | solution.py:632
  184.2 10.0 %collective-permute-start.43 = (bf16[32,3200]{1,0:T(8,128)(2,1)S(1)}, bf16[32,3200]{1,0:T(8,128)(2,1)S(1)}, u32[]{:S(2)}, u32[]{:S(2)}) collective-permute-start(bf16[32,3200]{1,0:T(8,128)(2,1)S(1)} %get-tuple-element.151), channel_id=1, source_target_pairs={{0,24},{1,25},{2,26},{3,27},{4,28},{5,29},{6,30},{7,31},{8,16},{9,... | collective-permute-start | bytes 614408 | tf_op jit(solution)/shard_map/ppermute | solution.py:632
  187.1 18.1 %collective-permute-start.42 = (bf16[32,3200]{1,0:T(8,128)(2,1)S(1)}, bf16[32,3200]{1,0:T(8,128)(2,1)S(1)}, u32[]{:S(2)}, u32[]{:S(2)}) collective-permute-start(bf16[32,3200]{1,0:T(8,128)(2,1)S(1)} %get-tuple-element.152), channel_id=1, source_target_pairs={{0,16},{1,17},{2,18},{3,19},{4,20},{5,21},{6,22},{7,23},{8,24},{9,... | collective-permute-start | bytes 614408 | tf_op jit(solution)/shard_map/ppermute | solution.py:632
  187.3 17.9 %collective-permute-start.41 = (bf16[32,3200]{1,0:T(8,128)(2,1)S(1)}, bf16[32,3200]{1,0:T(8,128)(2,1)S(1)}, u32[]{:S(2)}, u32[]{:S(2)}) collective-permute-start(bf16[32,3200]{1,0:T(8,128)(2,1)S(1)} %get-tuple-element.153), channel_id=1, source_target_pairs={{0,8},{1,9},{2,10},{3,11},{4,12},{5,13},{6,14},{7,15},{8,0},{9,1},... | collective-permute-start | bytes 614408 | tf_op jit(solution)/shard_map/ppermute | solution.py:632
  (43 other events, 287.8 us)
Sparse Core Ops, SparseCore 0:
  71.1 110.2 reduce-scatter.1

commit v4 on v3

--- a/solution.py
+++ b/solution.py
@@ -17,13 +17,16 @@
 
 
 def rope_tables(me, tok_rows, groups):
-    row = lax.broadcasted_iota(jnp.int32, (groups * tok_rows, LANES), 0)
-    lane = lax.broadcasted_iota(jnp.int32, (groups * tok_rows, LANES), 1)
-    position = ((row // tok_rows) ^ me) * tok_rows + row % tok_rows
+    lane = lax.broadcasted_iota(jnp.int32, (1, LANES), 1)
     frequency = jnp.exp((lane % (HD // 2)).astype(jnp.float32) * (-2.0 * math.log(10000.0) / HD))
-    angles = position.astype(jnp.float32) * frequency
-    sine = jnp.sin(angles)
-    return jnp.cos(angles), jnp.where(lane % HD < HD // 2, -sine, sine)
+    place = lax.broadcasted_iota(jnp.int32, (tok_rows, LANES), 0).astype(jnp.float32)
+    start = (lax.broadcasted_iota(jnp.int32, (groups, LANES), 0) ^ me) * tok_rows
+    inner, outer = place * frequency, start.astype(jnp.float32) * frequency
+    cos_in, sin_in = jnp.cos(inner)[None], jnp.sin(inner)[None]
+    cos_out, sin_out = jnp.cos(outer)[:, None], jnp.sin(outer)[:, None]
+    cosine = (cos_out * cos_in - sin_out * sin_in).reshape(groups * tok_rows, LANES)
+    sine = (sin_out * cos_in + cos_out * sin_in).reshape(groups * tok_rows, LANES)
+    return cosine, jnp.where(lane % HD < HD // 2, -sine, sine)
 
 
 LANES = 128

time: 215 us -> 215 us (level)
  transfers between devices with their start and end apart: 45 -> 45, of which waited for: 25 -> 26; matrix products, arithmetic and copies ran while one was open for 8% -> 8% of each run, Pallas kernels for 22% -> 22%
where the time goes in v4:
time: 215 us
  waiting for transfers between devices  76 us (35%)
  Pallas kernels  68.9 us (32%)
  starting transfers between devices  32.6 us (15%)
  between operations  15.1 us (7%)
  other arithmetic  12.6 us (6%)
  local copies, waits for them, and re-layouts  9.61 us (4%)
    ppermute x44, waiting for transfers between devices, send(): lax.ppermute(block, ('dp', 'expert'), [(i * groups + j, (i ^ pair_flip) *...  75.9 us
    pallas_call x8, Pallas kernels, run(): pl.pallas_call(kernel, out_shape=out_shape, in_specs=specs, out_specs=[pl...  68.9 us
    ppermute x44, starting transfers between devices, send(): lax.ppermute(block, ('dp', 'expert'), [(i * groups + j, (i ^ pair_flip) *...  32.6 us
    unnamed x61, local copies, waits for them, and re-layouts  5.62 us
  transfers between devices with their start and end apart: 45, of which 26 were waited for; matrix products, arithmetic and copies ran while one was open for 8% of the time, Pallas kernels for 22%

profile of v4, /device:TPU:0, one launch (start us, length us, event | category | flops | bytes accessed | tf_op | source)
XLA Modules:
  0.0 214.9 jit_solution(16995212378256079915)
XLA Ops:
  7.2 3.0 %collective-permute-start = (bf16[128,1024]{1,0:T(8,128)(2,1)}, bf16[128,1024]{1,0:T(8,128)(2,1)S(1)}, u32[]{:S(2)}, u32[]{:S(2)}) collective-permute-start(bf16[128,1024]{1,0:T(8,128)(2,1)} %tokens_ref.1), channel_id=1, source_target_pairs={{0,2},{1,3},{2,0},{3,1},{4,6},{5,7},{6,4},{7,5},{8,10},{9,11},{10,... | collective-permute-start | bytes 786440 | tf_op jit(solution)/shard_map/ppermute | solution.py:635
  12.1 1.6 collective-permute-start.4
  16.8 2.7 %collective-permute-start.5 = (bf16[128,1152]{1,0:T(8,128)(2,1)S(1)}, bf16[128,1152]{1,0:T(8,128)(2,1)}, u32[]{:S(2)}, u32[]{:S(2)}) collective-permute-start(bf16[128,1152]{1,0:T(8,128)(2,1)S(1)} %pad_maximum_fusion.1.refs_5_.refs_2_), channel_id=1, source_target_pairs={{0,6},{1,7},{2,4},{3,5},{4,2},{5,3},{6,0},{7,1},{8,14},{9,15},{10,... | collective-permute-start | bytes 884744 | tf_op jit(solution)/shard_map/ppermute | solution.py:635
  22.6 8.2 %attention_forward.1 = (bf16[128,1024]{1,0:T(8,128)(2,1)}, bf16[8,512,128]{2,1,0:T(8,128)(2,1)}, bf16[8,512,128]{2,1,0:T(8,128)(2,1)}, f32[8,256]{1,0:T(8,128)},...) custom-call(s32[4]{0:T(128)} %pad_add_fusion.info_ref.refs_0_, ...), custom_call_target="tpu_custom_call" | custom-call | tf_op jit(solution)/shard_map/attention_forward/pallas_call | solution.py:586
  30.8 2.1 collective-permute-done.3.refs_7_
  36.9 6.3 %collective-permute-done.15.refs_19_ = bf16[128,1024]{1,0:T(8,128)(2,1)S(1)} collective-permute-done((bf16[128,1024]{1,0:T(8,128)(2,1)}, bf16[128,1024]{1,0:T(8,128)(2,1)S(1)}, u32[]{:S(2)}, u32[]{:S(2)}) %collective-permute-start.15) | collective-permute-done | bytes 262176 | tf_op jit(solution)/shard_map/ppermute | solution.py:635
  43.3 3.1 %collective-permute-done.13.refs_17_ = bf16[128,1024]{1,0:T(8,128)(2,1)S(1)} collective-permute-done((bf16[128,1024]{1,0:T(8,128)(2,1)}, bf16[128,1024]{1,0:T(8,128)(2,1)S(1)}, u32[]{:S(2)}, u32[]{:S(2)}) %collective-permute-start.13) | collective-permute-done | bytes 262176 | tf_op jit(solution)/shard_map/ppermute | solution.py:635
  51.5 19.7 %experts.1 = (bf16[1024,3072]{1,0:T(8,128)(2,1)}, bf16[4,1024,896]{2,1,0:T(8,128)(2,1)}) custom-call(s32[4]{0:T(128)S(1)} %copy-done.4, bf16[1024,16]{1,0:T(8,128)(2,1)S(1)} %copy.30.refs_1_.refs_5_, bf16[4,1024,512]{2,1,0:T(8,128)(2,1)} %wg_ref.1, bf16[4,1024,512]{2,1,0:T(8,128)(2,1)} %wu_ref.1, bf16[4,512,1024]{2,1,0:T(8,128)(2,1)} %refs_16_.1, ...), custom_call_target="tpu_custom_call" | custom-call | tf_op jit(solution)/shard_map/experts/pallas_call | solution.py:586
  72.3 10.2 %experts_rows.1 = (bf16[4,128,1152]{2,1,0:T(8,128)(2,1)}, f32[4,128,1152]{2,1,0:T(8,128)}) custom-call(s32[4]{0:T(128)} %pad_add_fusion.info_ref.refs_0_, bf16[4,1024,512]{2,1,0:T(8,128)(2,1)} %wg_ref.1, bf16[4,1024,512]{2,1,0:T(8,128)(2,1)} %wu_ref.1, bf16[4,1024,896]{2,1,0:T(8,128)(2,1)} %get-tuple-element.90.acts_in.refs_15_), custom_call_target="tpu_custom_call" | custom-call | tf_op jit(solution)/shard_map/experts_rows/pallas_call | solution.py:586
  82.6 3.0 %collective-permute-done.18 = bf16[4,128,1152]{2,1,0:T(8,128)(2,1)S(1)} collective-permute-done((bf16[4,128,1152]{2,1,0:T(8,128)(2,1)}, bf16[4,128,1152]{2,1,0:T(8,128)(2,1)S(1)}, u32[]{:S(2)}, u32[]{:S(2)}) %collective-permute-start.18) | collective-permute-done | bytes 1179680 | tf_op jit(solution)/shard_map/ppermute | solution.py:635
  85.7 2.0 fusion.12
  88.2 2.1 collective-permute-start.20
  92.2 6.4 %collective-permute-done.21.refs_19_ = bf16[128,1152]{1,0:T(8,128)(2,1)S(1)} collective-permute-done((bf16[128,1152]{1,0:T(8,128)(2,1)S(1)}, bf16[128,1152]{1,0:T(8,128)(2,1)S(1)}, u32[]{:S(2)}, u32[]{:S(2)}) %collective-permute-start.21) | collective-permute-done | bytes 294944 | tf_op jit(solution)/shard_map/ppermute | solution.py:635
  98.6 5.0 %collective-permute-done.20.refs_18_ = bf16[128,1152]{1,0:T(8,128)(2,1)S(1)} collective-permute-done((bf16[128,1152]{1,0:T(8,128)(2,1)S(1)}, bf16[128,1152]{1,0:T(8,128)(2,1)S(1)}, u32[]{:S(2)}, u32[]{:S(2)}) %collective-permute-start.20) | collective-permute-done | bytes 294944 | tf_op jit(solution)/shard_map/ppermute | solution.py:635
  104.8 15.5 %attention_backward.1 = (f32[128,1024]{1,0:T(8,128)}, bf16[176,1024]{1,0:T(8,128)(2,1)}, bf16[128,1024]{1,0:T(8,128)(2,1)}, bf16[2,128,1024]{2,1,0:T(8,128)(2,1)...) custom-call(s32[4]{0:T(128)} %pad_add_fusion.info_ref.refs_0_, ...), custom_call_target="tpu_custom_call" | custom-call | tf_op jit(solution)/shard_map/attention_backward/pallas_call | solution.py:586
  120.5 2.0 collective-permute-done.22
  122.6 1.5 convert_add_fusion.3
  125.4 1.6 collective-permute-done.23
  128.1 4.9 %collective-permute-done.24.rest_0_ = bf16[128,1024]{1,0:T(8,128)(2,1)S(1)} collective-permute-done((bf16[128,1024]{1,0:T(8,128)(2,1)S(1)}, bf16[128,1024]{1,0:T(8,128)(2,1)S(1)}, u32[]{:S(2)}, u32[]{:S(2)}) %collective-permute-start.24) | collective-permute-done | bytes 262176 | tf_op jit(solution)/shard_map/ppermute | solution.py:635
  136.3 4.1 %tokens_backward.1 = (bf16[144,1024]{1,0:T(8,128)(2,1)}, bf16[128,1024]{1,0:T(8,128)(2,1)}) custom-call(f32[128,1024]{1,0:T(8,128)} %slice_bitcast_fusion.2.own_ref, f32[128,1024]{1,0:T(8,128)} %get-tuple-element.105.gn_ref, bf16[1024,512]{1,0:T(8,128)(2,1)} %wk_ref.3, bf16[1024,512]{1,0:T(8,128)(2,1)} %wv_ref.3, bf16[128,1024]{1,0:T(8,128)(2,1)} %tokens_ref.1, ...), custom_call_target="tpu_custom_call" | custom-call | tf_op jit(solution)/shard_map/tokens_backward/pallas_call | solution.py:586
  140.5 8.2 %collective-permute-done.27.refs_12_ = bf16[128,1024]{1,0:T(8,128)(2,1)} collective-permute-done((bf16[128,1024]{1,0:T(8,128)(2,1)}, bf16[128,1024]{1,0:T(8,128)(2,1)}, u32[]{:S(2)}, u32[]{:S(2)}) %collective-permute-start.27) | collective-permute-done | bytes 262176 | tf_op jit(solution)/shard_map/ppermute | solution.py:635
  153.9 5.5 %dense_early.1 = (bf16[4,32,2176]{2,1,0:T(8,128)(2,1)}, f32[4,32,2176]{2,1,0:T(8,128)}, bf16[256,512]{1,0:T(8,128)(2,1)}) custom-call(s32[4]{0:T(128)} %pad_add_fusion.info_ref.refs_0_, bf16[512,1024]{1,0:T(8,128)(2,1)} %get-tuple-element.114.refs_1_, bf16[128,1024]{1,0:T(8,128)(2,1)} %get-tuple-element.115.refs_2_, ...), custom_call_target="tpu_custom_call" | custom-call | tf_op jit(solution)/shard_map/dense_early/pallas_call | solution.py:586
  162.6 3.0 %dense_late.1 = (bf16[4,32,1152]{2,1,0:T(8,128)(2,1)}, f32[4,32,1152]{2,1,0:T(8,128)}) custom-call(s32[4]{0:T(128)} %pad_add_fusion.info_ref.refs_0_, bf16[256,512]{1,0:T(8,128)(2,1)} %get-tuple-element.121.refs_1_, bf16[144,1024]{1,0:T(8,128)(2,1)} %get-tuple-element.124.refs_2_, bf16[144,1024]{1,0:T(8,128)(2,1)} %copy-done.17, ...), custom_call_target="tpu_custom_call" | custom-call | tf_op jit(solution)/shard_map/dense_late/pallas_call | solution.py:586
  165.6 1.8 convert_add_fusion.2
  170.2 5.5 %collective-permute-done.39 = bf16[4,32,2176]{2,1,0:T(8,128)(2,1)S(1)} collective-permute-done((bf16[4,32,2176]{2,1,0:T(8,128)(2,1)}, bf16[4,32,2176]{2,1,0:T(8,128)(2,1)S(1)}, u32[]{:S(2)}, u32[]{:S(2)}) %collective-permute-start.39) | collective-permute-done | bytes 557088 | tf_op jit(solution)/shard_map/ppermute | solution.py:635
  175.9 5.4 %collective-permute-done.40 = bf16[4,32,1152]{2,1,0:T(8,128)(2,1)S(1)} collective-permute-done((bf16[4,32,1152]{2,1,0:T(8,128)(2,1)S(1)}, bf16[4,32,1152]{2,1,0:T(8,128)(2,1)S(1)}, u32[]{:S(2)}, u32[]{:S(2)}) %collective-permute-start.40) | collective-permute-done | bytes 294944 | tf_op jit(solution)/shard_map/ppermute | solution.py:635
  182.9 1.5 collective-permute-start.38
  184.4 2.9 %collective-permute-start.43 = (bf16[32,3200]{1,0:T(8,128)(2,1)S(1)}, bf16[32,3200]{1,0:T(8,128)(2,1)S(1)}, u32[]{:S(2)}, u32[]{:S(2)}) collective-permute-start(bf16[32,3200]{1,0:T(8,128)(2,1)S(1)} %get-tuple-element.151), channel_id=1, source_target_pairs={{0,24},{1,25},{2,26},{3,27},{4,28},{5,29},{6,30},{7,31},{8,16},{9,... | collective-permute-start | bytes 614408 | tf_op jit(solution)/shard_map/ppermute | solution.py:635
  188.9 1.8 fusion.2
  190.7 3.7 %collective-permute-done.43.refs_7_ = bf16[32,3200]{1,0:T(8,128)(2,1)S(1)} collective-permute-done((bf16[32,3200]{1,0:T(8,128)(2,1)S(1)}, bf16[32,3200]{1,0:T(8,128)(2,1)S(1)}, u32[]{:S(2)}, u32[]{:S(2)}) %collective-permute-start.43) | collective-permute-done | bytes 204832 | tf_op jit(solution)/shard_map/ppermute | solution.py:635
  194.4 11.0 %collective-permute-done.42.refs_6_ = bf16[32,3200]{1,0:T(8,128)(2,1)S(1)} collective-permute-done((bf16[32,3200]{1,0:T(8,128)(2,1)S(1)}, bf16[32,3200]{1,0:T(8,128)(2,1)S(1)}, u32[]{:S(2)}, u32[]{:S(2)}) %collective-permute-start.42) | collective-permute-done | bytes 204832 | tf_op jit(solution)/shard_map/ppermute | solution.py:635
  205.5 2.6 %place.1 = (f32[4,128,512]{2,1,0:T(8,128)}, f32[4,128,512]{2,1,0:T(8,128)}, f32[4,512,128]{2,1,0:T(8,128)}, f32[32,1024]{1,0:T(8,128)}, f32[32,512]{1,0:T(8,128)...) custom-call(s32[4]{0:T(128)S(1)} %copy-done.5, ...), custom_call_target="tpu_custom_call" | custom-call | tf_op jit(solution)/shard_map/place/pallas_call | solution.py:586
  (159 shorter events, 41.5 us)
Async XLA Ops:
  7.2 174.4 %reduce-scatter.2.cloned.1.call-start = ((), (), s32[]{:S(2)}) async-start(), calls=%async_computation.1 | async-start | bytes 7864320 | tf_op jit(solution)/shard_map/reduce_scatter | solution.py:759
  7.2 9.6 %collective-permute-start = (bf16[128,1024]{1,0:T(8,128)(2,1)}, bf16[128,1024]{1,0:T(8,128)(2,1)S(1)}, u32[]{:S(2)}, u32[]{:S(2)}) collective-permute-start(bf16[128,1024]{1,0:T(8,128)(2,1)} %tokens_ref.1), channel_id=1, source_target_pairs={{0,2},{1,3},{2,0},{3,1},{4,6},{5,7},{6,4},{7,5},{8,10},{9,11},{10,... | collective-permute-start | bytes 786440 | tf_op jit(solution)/shard_map/ppermute | solution.py:635
  12.1 18.7 %collective-permute-start.4 = (bf16[128,1152]{1,0:T(8,128)(2,1)S(1)}, bf16[128,1152]{1,0:T(8,128)(2,1)S(1)}, u32[]{:S(2)}, u32[]{:S(2)}) collective-permute-start(bf16[128,1152]{1,0:T(8,128)(2,1)S(1)} %pad_maximum_fusion.1.refs_5_.refs_2_), channel_id=1, source_target_pairs={{0,4},{1,5},{2,6},{3,7},{4,0},{5,1},{6,2},{7,3},{8,12},{9,13},{10,... | collective-permute-start | bytes 884744 | tf_op jit(solution)/shard_map/ppermute | solution.py:635
  16.8 14.0 %collective-permute-start.5 = (bf16[128,1152]{1,0:T(8,128)(2,1)S(1)}, bf16[128,1152]{1,0:T(8,128)(2,1)}, u32[]{:S(2)}, u32[]{:S(2)}) collective-permute-start(bf16[128,1152]{1,0:T(8,128)(2,1)S(1)} %pad_maximum_fusion.1.refs_5_.refs_2_), channel_id=1, source_target_pairs={{0,6},{1,7},{2,4},{3,5},{4,2},{5,3},{6,0},{7,1},{8,14},{9,15},{10,... | collective-permute-start | bytes 884744 | tf_op jit(solution)/shard_map/ppermute | solution.py:635
  19.5 13.5 %collective-permute-start.3 = (bf16[128,1152]{1,0:T(8,128)(2,1)S(1)}, bf16[128,1152]{1,0:T(8,128)(2,1)}, u32[]{:S(2)}, u32[]{:S(2)}) collective-permute-start(bf16[128,1152]{1,0:T(8,128)(2,1)S(1)} %pad_maximum_fusion.1.refs_5_.refs_2_), channel_id=1, source_target_pairs={{0,2},{1,3},{2,0},{3,1},{4,6},{5,7},{6,4},{7,5},{8,10},{9,11},{10,... | collective-permute-start | bytes 884744 | tf_op jit(solution)/shard_map/ppermute | solution.py:635
  32.9 10.3 %collective-permute-start.15 = (bf16[128,1024]{1,0:T(8,128)(2,1)}, bf16[128,1024]{1,0:T(8,128)(2,1)S(1)}, u32[]{:S(2)}, u32[]{:S(2)}) collective-permute-start(bf16[128,1024]{1,0:T(8,128)(2,1)} %get-tuple-element.89.refs_13_.refs_3_), channel_id=1, source_target_pairs={{0,6},{1,7},{2,4},{3,5},{4,2},{5,3},{6,0},{7,1},{8,14},{9,15},{10,... | collective-permute-start | bytes 786440 | tf_op jit(solution)/shard_map/ppermute | solution.py:635
  34.1 12.3 %collective-permute-start.13 = (bf16[128,1024]{1,0:T(8,128)(2,1)}, bf16[128,1024]{1,0:T(8,128)(2,1)S(1)}, u32[]{:S(2)}, u32[]{:S(2)}) collective-permute-start(bf16[128,1024]{1,0:T(8,128)(2,1)} %get-tuple-element.89.refs_13_.refs_3_), channel_id=1, source_target_pairs={{0,4},{1,5},{2,6},{3,7},{4,0},{5,1},{6,2},{7,3},{8,12},{9,13},{10,... | collective-permute-start | bytes 786440 | tf_op jit(solution)/shard_map/ppermute | solution.py:635
  35.4 12.3 %collective-permute-start.11 = (bf16[128,1024]{1,0:T(8,128)(2,1)}, bf16[128,1024]{1,0:T(8,128)(2,1)S(1)}, u32[]{:S(2)}, u32[]{:S(2)}) collective-permute-start(bf16[128,1024]{1,0:T(8,128)(2,1)} %get-tuple-element.89.refs_13_.refs_3_), channel_id=1, source_target_pairs={{0,2},{1,3},{2,0},{3,1},{4,6},{5,7},{6,4},{7,5},{8,10},{9,11},{10,... | collective-permute-start | bytes 786440 | tf_op jit(solution)/shard_map/ppermute | solution.py:635
  36.4 11.8 %collective-permute-start.6 = (bf16[128,1152]{1,0:T(8,128)(2,1)S(1)}, bf16[128,1152]{1,0:T(8,128)(2,1)S(1)}, u32[]{:S(2)}, u32[]{:S(2)}) collective-permute-start(bf16[128,1152]{1,0:T(8,128)(2,1)S(1)} %pad_maximum_fusion.1.refs_5_.refs_2_), channel_id=1, source_target_pairs={{0,1},{1,0},{2,3},{3,2},{4,5},{5,4},{6,7},{7,6},{8,9},{9,8},{10,11... | collective-permute-start | bytes 884744 | tf_op jit(solution)/shard_map/ppermute | solution.py:635
  36.4 11.9 %collective-permute-start.7 = (bf16[128,1152]{1,0:T(8,128)(2,1)}, bf16[128,1152]{1,0:T(8,128)(2,1)S(1)}, u32[]{:S(2)}, u32[]{:S(2)}) collective-permute-start(bf16[128,1152]{1,0:T(8,128)(2,1)} %collective-permute-done.3.refs_7_), channel_id=1, source_target_pairs={{0,1},{1,0},{2,3},{3,2},{4,5},{5,4},{6,7},{7,6},{8,9},{9,8},{10,11... | collective-permute-start | bytes 884744 | tf_op jit(solution)/shard_map/ppermute | solution.py:635
  43.3 4.4 %collective-permute-start.10 = (bf16[128,1024]{1,0:T(8,128)(2,1)}, bf16[128,1024]{1,0:T(8,128)(2,1)S(1)}, u32[]{:S(2)}, u32[]{:S(2)}) collective-permute-start(bf16[128,1024]{1,0:T(8,128)(2,1)} %get-tuple-element.89.refs_13_.refs_3_), channel_id=1, source_target_pairs={{0,1},{1,0},{2,3},{3,2},{4,5},{5,4},{6,7},{7,6},{8,9},{9,8},{10,11... | collective-permute-start | bytes 786440 | tf_op jit(solution)/shard_map/ppermute | solution.py:635
  71.2 11.3 %collective-permute-start.17 = (bf16[128,1024]{1,0:T(8,128)(2,1)}, bf16[128,1024]{1,0:T(8,128)(2,1)}, u32[]{:S(2)}, u32[]{:S(2)}) collective-permute-start(bf16[128,1024]{1,0:T(8,128)(2,1)} %get-tuple-element.115.refs_2_), channel_id=1, source_target_pairs={{0,2},{1,3},{2,0},{3,1},{4,6},{5,7},{6,4},{7,5},{8,10},{9,11},{10,... | collective-permute-start | bytes 786440 | tf_op jit(solution)/shard_map/ppermute | solution.py:635
  82.6 3.1 %collective-permute-start.18 = (bf16[4,128,1152]{2,1,0:T(8,128)(2,1)}, bf16[4,128,1152]{2,1,0:T(8,128)(2,1)S(1)}, u32[]{:S(2)}, u32[]{:S(2)}) collective-permute-start(bf16[4,128,1152]{2,1,0:T(8,128)(2,1)} %get-tuple-element.94), channel_id=1, source_target_pairs={{0,1},{1,0},{2,3},{3,2},{4,5},{5,4},{6,7},{7,6},{8,9},{9,8},{10,11... | collective-permute-start | bytes 3538952 | tf_op jit(solution)/shard_map/ppermute | solution.py:635
  87.8 10.9 %collective-permute-start.21 = (bf16[128,1152]{1,0:T(8,128)(2,1)S(1)}, bf16[128,1152]{1,0:T(8,128)(2,1)S(1)}, u32[]{:S(2)}, u32[]{:S(2)}) collective-permute-start(bf16[128,1152]{1,0:T(8,128)(2,1)S(1)} %get-tuple-element.148), channel_id=1, source_target_pairs={{0,6},{1,7},{2,4},{3,5},{4,2},{5,3},{6,0},{7,1},{8,14},{9,15},{10,... | collective-permute-start | bytes 884744 | tf_op jit(solution)/shard_map/ppermute | solution.py:635
  88.2 15.5 %collective-permute-start.20 = (bf16[128,1152]{1,0:T(8,128)(2,1)S(1)}, bf16[128,1152]{1,0:T(8,128)(2,1)S(1)}, u32[]{:S(2)}, u32[]{:S(2)}) collective-permute-start(bf16[128,1152]{1,0:T(8,128)(2,1)S(1)} %get-tuple-element.149), channel_id=1, source_target_pairs={{0,4},{1,5},{2,6},{3,7},{4,0},{5,1},{6,2},{7,3},{8,12},{9,13},{10,... | collective-permute-start | bytes 884744 | tf_op jit(solution)/shard_map/ppermute | solution.py:635
  90.3 13.8 %collective-permute-start.19 = (bf16[128,1152]{1,0:T(8,128)(2,1)S(1)}, bf16[128,1152]{1,0:T(8,128)(2,1)S(1)}, u32[]{:S(2)}, u32[]{:S(2)}) collective-permute-start(bf16[128,1152]{1,0:T(8,128)(2,1)S(1)} %get-tuple-element.150), channel_id=1, source_target_pairs={{0,2},{1,3},{2,0},{3,1},{4,6},{5,7},{6,4},{7,5},{8,10},{9,11},{10,... | collective-permute-start | bytes 884744 | tf_op jit(solution)/shard_map/ppermute | solution.py:635
  124.3 8.7 %collective-permute-start.24 = (bf16[128,1024]{1,0:T(8,128)(2,1)S(1)}, bf16[128,1024]{1,0:T(8,128)(2,1)S(1)}, u32[]{:S(2)}, u32[]{:S(2)}) collective-permute-start(bf16[128,1024]{1,0:T(8,128)(2,1)S(1)} %fusion.3), channel_id=1, source_target_pairs={{0,2},{1,3},{2,0},{3,1},{4,6},{5,7},{6,4},{7,5},{8,10},{9,11},{10,... | collective-permute-start | bytes 786440 | tf_op jit(solution)/shard_map/ppermute | solution.py:635
  128.1 20.6 %collective-permute-start.25 = (bf16[2,128,1024]{2,1,0:T(8,128)(2,1)}, bf16[2,128,1024]{2,1,0:T(8,128)(2,1)S(1)}, u32[]{:S(2)}, u32[]{:S(2)}) collective-permute-start(bf16[2,128,1024]{2,1,0:T(8,128)(2,1)} %add_convert_fusion), channel_id=1, source_target_pairs={{0,4},{1,5},{2,6},{3,7},{4,0},{5,1},{6,2},{7,3},{8,12},{9,13},{10,... | collective-permute-start | bytes 1572872 | tf_op jit(solution)/shard_map/ppermute | solution.py:635
  133.0 15.7 %collective-permute-start.26 = (bf16[176,1024]{1,0:T(8,128)(2,1)S(1)}, bf16[176,1024]{1,0:T(8,128)(2,1)}, u32[]{:S(2)}, u32[]{:S(2)}) collective-permute-start(bf16[176,1024]{1,0:T(8,128)(2,1)S(1)} %copy-done.13), channel_id=1, source_target_pairs={{0,2},{1,3},{2,0},{3,1},{4,6},{5,7},{6,4},{7,5},{8,10},{9,11},{10,... | collective-permute-start | bytes 1081352 | tf_op jit(solution)/shard_map/ppermute | solution.py:635
  133.9 14.7 %collective-permute-start.27 = (bf16[128,1024]{1,0:T(8,128)(2,1)}, bf16[128,1024]{1,0:T(8,128)(2,1)}, u32[]{:S(2)}, u32[]{:S(2)}) collective-permute-start(bf16[128,1024]{1,0:T(8,128)(2,1)} %get-tuple-element.119.refs_10_), channel_id=1, source_target_pairs={{0,2},{1,3},{2,0},{3,1},{4,6},{5,7},{6,4},{7,5},{8,10},{9,11},{10,... | collective-permute-start | bytes 786440 | tf_op jit(solution)/shard_map/ppermute | solution.py:635
  135.0 15.2 %collective-permute-start.28 = (bf16[128,1024]{1,0:T(8,128)(2,1)}, bf16[128,1024]{1,0:T(8,128)(2,1)}, u32[]{:S(2)}, u32[]{:S(2)}) collective-permute-start(bf16[128,1024]{1,0:T(8,128)(2,1)} %get-tuple-element.115.refs_2_), channel_id=1, source_target_pairs={{0,1},{1,0},{2,3},{3,2},{4,5},{5,4},{6,7},{7,6},{8,9},{9,8},{10,11... | collective-permute-start | bytes 786440 | tf_op jit(solution)/shard_map/ppermute | solution.py:635
  135.0 15.2 %collective-permute-start.29 = (bf16[128,1024]{1,0:T(8,128)(2,1)}, bf16[128,1024]{1,0:T(8,128)(2,1)}, u32[]{:S(2)}, u32[]{:S(2)}) collective-permute-start(bf16[128,1024]{1,0:T(8,128)(2,1)} %collective-permute-done.17.refs_4_), channel_id=1, source_target_pairs={{0,1},{1,0},{2,3},{3,2},{4,5},{5,4},{6,7},{7,6},{8,9},{9,8},{10,11... | collective-permute-start | bytes 786440 | tf_op jit(solution)/shard_map/ppermute | solution.py:635
  148.7 3.7 %collective-permute-start.30 = (bf16[176,1024]{1,0:T(8,128)(2,1)S(1)}, bf16[176,1024]{1,0:T(8,128)(2,1)S(1)}, u32[]{:S(2)}, u32[]{:S(2)}) collective-permute-start(bf16[176,1024]{1,0:T(8,128)(2,1)S(1)} %copy-done.13), channel_id=1, source_target_pairs={{0,1},{1,0},{2,3},{3,2},{4,5},{5,4},{6,7},{7,6},{8,9},{9,8},{10,11... | collective-permute-start | bytes 1081352 | tf_op jit(solution)/shard_map/ppermute | solution.py:635
  148.8 4.4 %collective-permute-start.31 = (bf16[176,1024]{1,0:T(8,128)(2,1)}, bf16[176,1024]{1,0:T(8,128)(2,1)S(1)}, u32[]{:S(2)}, u32[]{:S(2)}) collective-permute-start(bf16[176,1024]{1,0:T(8,128)(2,1)} %collective-permute-done.26.refs_8_), channel_id=1, source_target_pairs={{0,1},{1,0},{2,3},{3,2},{4,5},{5,4},{6,7},{7,6},{8,9},{9,8},{10,11... | collective-permute-start | bytes 1081352 | tf_op jit(solution)/shard_map/ppermute | solution.py:635
  149.3 10.2 %collective-permute-start.34 = (bf16[144,1024]{1,0:T(8,128)(2,1)}, bf16[144,1024]{1,0:T(8,128)(2,1)}, u32[]{:S(2)}, u32[]{:S(2)}) collective-permute-start(bf16[144,1024]{1,0:T(8,128)(2,1)} %get-tuple-element.124.refs_2_), channel_id=1, source_target_pairs={{0,2},{1,3},{2,0},{3,1},{4,6},{5,7},{6,4},{7,5},{8,10},{9,11},{10,... | collective-permute-start | bytes 884744 | tf_op jit(solution)/shard_map/ppermute | solution.py:635
  160.0 15.7 %collective-permute-start.39 = (bf16[4,32,2176]{2,1,0:T(8,128)(2,1)}, bf16[4,32,2176]{2,1,0:T(8,128)(2,1)S(1)}, u32[]{:S(2)}, u32[]{:S(2)}) collective-permute-start(bf16[4,32,2176]{2,1,0:T(8,128)(2,1)} %get-tuple-element.122), channel_id=1, source_target_pairs={{0,4},{1,5},{2,6},{3,7},{4,0},{5,1},{6,2},{7,3},{8,12},{9,13},{10,... | collective-permute-start | bytes 1671176 | tf_op jit(solution)/shard_map/ppermute | solution.py:635
  168.2 20.7 %collective-permute-start.37 = (bf16[128,1024]{1,0:T(8,128)(2,1)}, bf16[128,1024]{1,0:T(8,128)(2,1)}, u32[]{:S(2)}, u32[]{:S(2)}) collective-permute-start(bf16[128,1024]{1,0:T(8,128)(2,1)} %fusion.4), channel_id=1, source_target_pairs={{0,2},{1,3},{2,0},{3,1},{4,6},{5,7},{6,4},{7,5},{8,10},{9,11},{10,... | collective-permute-start | bytes 786440 | tf_op jit(solution)/shard_map/ppermute | solution.py:635
  169.2 12.1 %collective-permute-start.40 = (bf16[4,32,1152]{2,1,0:T(8,128)(2,1)S(1)}, bf16[4,32,1152]{2,1,0:T(8,128)(2,1)S(1)}, u32[]{:S(2)}, u32[]{:S(2)}) collective-permute-start(bf16[4,32,1152]{2,1,0:T(8,128)(2,1)S(1)} %copy-done.29), channel_id=1, source_target_pairs={{0,4},{1,5},{2,6},{3,7},{4,0},{5,1},{6,2},{7,3},{8,12},{9,13},{10,... | collective-permute-start | bytes 884744 | tf_op jit(solution)/shard_map/ppermute | solution.py:635
  182.9 22.6 %collective-permute-start.38 = (bf16[128,3072]{1,0:T(8,128)(2,1)S(1)}, bf16[128,3072]{1,0:T(8,128)(2,1)S(1)}, u32[]{:S(2)}, u32[]{:S(2)}) collective-permute-start(bf16[128,3072]{1,0:T(8,128)(2,1)S(1)} %constant_dynamic-slice_fusion), channel_id=1, source_target_pairs={{0,4},{1,5},{2,6},{3,7},{4,0},{5,1},{6,2},{7,3},{8,12},{9,13},{10,... | collective-permute-start | bytes 2359304 | tf_op jit(solution)/shard_map/ppermute | solution.py:635
  184.4 10.0 %collective-permute-start.43 = (bf16[32,3200]{1,0:T(8,128)(2,1)S(1)}, bf16[32,3200]{1,0:T(8,128)(2,1)S(1)}, u32[]{:S(2)}, u32[]{:S(2)}) collective-permute-start(bf16[32,3200]{1,0:T(8,128)(2,1)S(1)} %get-tuple-element.151), channel_id=1, source_target_pairs={{0,24},{1,25},{2,26},{3,27},{4,28},{5,29},{6,30},{7,31},{8,16},{9,... | collective-permute-start | bytes 614408 | tf_op jit(solution)/shard_map/ppermute | solution.py:635
  187.3 18.1 %collective-permute-start.42 = (bf16[32,3200]{1,0:T(8,128)(2,1)S(1)}, bf16[32,3200]{1,0:T(8,128)(2,1)S(1)}, u32[]{:S(2)}, u32[]{:S(2)}) collective-permute-start(bf16[32,3200]{1,0:T(8,128)(2,1)S(1)} %get-tuple-element.152), channel_id=1, source_target_pairs={{0,16},{1,17},{2,18},{3,19},{4,20},{5,21},{6,22},{7,23},{8,24},{9,... | collective-permute-start | bytes 614408 | tf_op jit(solution)/shard_map/ppermute | solution.py:635
  187.5 17.9 %collective-permute-start.41 = (bf16[32,3200]{1,0:T(8,128)(2,1)S(1)}, bf16[32,3200]{1,0:T(8,128)(2,1)S(1)}, u32[]{:S(2)}, u32[]{:S(2)}) collective-permute-start(bf16[32,3200]{1,0:T(8,128)(2,1)S(1)} %get-tuple-element.153), channel_id=1, source_target_pairs={{0,8},{1,9},{2,10},{3,11},{4,12},{5,13},{6,14},{7,15},{8,0},{9,1},... | collective-permute-start | bytes 614408 | tf_op jit(solution)/shard_map/ppermute | solution.py:635
  (43 other events, 288.4 us)
Sparse Core Ops, SparseCore 0:
  71.3 110.2 reduce-scatter.1
